TPU v7x, 32 devices: a whole 2x2x4 slice. The times are simulated.
32 devices in a mesh: gx: 4 (over x, core), gy: 4 (over z), gz: 2 (over y).
Axes of the slice: x: 2, y: 2, z: 4, core: 2. Of those that a mesh axis runs over, the one named last changes fastest.
Arguments:
- grains: float32 [4, 4, 2, 7, 4096], P('gx', 'gy', 'gz'), as said below
- pairs: int32 [4, 4, 2, 32, 27], P('gx', 'gy', 'gz'), may hold values from -1 to 863, as said below
Outputs:
- fields: float32 [4, 4, 2, 10, 8, 256], P('gx', 'gy', 'gz')
- fits: float32 [4, 4, 2, 256], P('gx', 'gy', None, 'gz')
- inertial: float32 [4, 4, 16, 256], P('gx', 'gy', None, 'gz')
Inputs may be any that keep to these rules, and one draw needn't show every extreme that they name: Rows 0 to 2 of a brick's grains lie within the box of side 5 of the tile that its slot holds, inside the brick; row 3 (radius) lies between 0.4 and 0.6; tile slots hold the boxes of a brick in an order drawn per brick. `pairs`: for each tile slot, the slots of all 27 tile boxes touching its box, itself included, in drawn order; -1 where that box lies outside the window.
All inputs are finite; a program needn't handle non-finite values.
Results may differ from a plain program's by a relative error of at most 0.0092.
Values sent between devices are 32-bit elements; how exact they have to be, the bound alone decides.
No kernel may reach another device: no remote copies, remote signals or barrier semaphores. Data moves between devices by JAX's collectives and lax.ppermute only.
A program may use at most 64 MiB of HBM per device.

v0:
```python
import math

import jax
import jax.numpy as jnp
from jax import lax
from jax.sharding import PartitionSpec as P

TILE = 128
BOXES_DOWNSLOPE = 8
BOXES_SPANWISE = 2
BOXES_NORMAL = 2
CELLS_PER_EDGE = 4


TILE_BOX_EDGE = 5.0
SPRING = 2.0
SOFTEN = 0.05
FLOOR_LEVEL = 0.1
RIDGE_SHARE = 0.1
CUT_LEVEL = math.exp(-12.5)
NORM_ONE = 1.0 / math.sqrt(2.0 * math.pi)


def padded(value, sides, width):
    for axis, dim in sides:
        count, length = (lax.axis_size(axis), value.shape[dim])
        up = [(i, (i + 1) % count) for i in range(count - 1)]
        down = [(j, i) for i, j in up]
        last = lax.slice_in_dim(value, length - width, length, axis=dim)
        first = lax.slice_in_dim(value, 0, width, axis=dim)
        before = lax.ppermute(last, axis, up)
        after = lax.ppermute(first, axis, down)
        value = jnp.concatenate([before, value, after], axis=dim)
    return value


def offset_table():
    steps_all = jnp.arange(27, dtype=jnp.int32)
    shift_a = (steps_all // 9 - 1).astype(jnp.float32) * (BOXES_DOWNSLOPE * TILE_BOX_EDGE)
    shift_b = (steps_all // 3 % 3 - 1).astype(jnp.float32) * (BOXES_SPANWISE * TILE_BOX_EDGE)
    shift_c = (steps_all % 3 - 1).astype(jnp.float32) * (BOXES_NORMAL * TILE_BOX_EDGE)
    return jnp.stack([shift_a, shift_b, shift_c], axis=1)


def contact_tiles(table, partner_idx, own_idx):
    tiles = partner_idx.shape[0]
    hood_count = partner_idx.shape[1]
    row_ids = jnp.arange(TILE, dtype=jnp.int32)
    col_ids = jnp.arange(hood_count * TILE, dtype=jnp.int32) % TILE

    def one_tile(slot):
        own_place = own_idx[slot]
        own_tile = table[own_place]
        partner_ids = partner_idx[slot]
        is_valid = partner_ids >= 0
        safe_ids = jnp.where(is_valid, partner_ids, 0)
        others = table[safe_ids].transpose(1, 0, 2).reshape(4, hood_count * TILE)
        live_cols = jnp.repeat(is_valid, TILE)
        same_tile = jnp.repeat(safe_ids == own_place, TILE)
        itself = same_tile[None, :] & (col_ids[None, :] == row_ids[:, None])
        keep = live_cols[None, :] & jnp.logical_not(itself)
        delta_x = own_tile[0][:, None] - others[0][None, :]
        delta_y = own_tile[1][:, None] - others[1][None, :]
        delta_z = own_tile[2][:, None] - others[2][None, :]
        distance = jnp.sqrt(delta_x * delta_x + delta_y * delta_y + delta_z * delta_z)
        intersection = jnp.where(
            keep, jnp.maximum(own_tile[3][:, None] + others[3][None, :] - distance, 0.0), 0.0
        )
        force = 0.5 * SPRING * intersection / (distance + SOFTEN)
        return jnp.stack(
            [
                jnp.sum(force * delta_x * delta_x, 1),
                jnp.sum(force * delta_y * delta_y, 1),
                jnp.sum(force * delta_z * delta_z, 1),
                jnp.sum(force * delta_x * delta_y, 1),
                jnp.sum(force * delta_x * delta_z, 1),
                jnp.sum(force * delta_y * delta_z, 1),
            ]
        )

    blocks = lax.map(one_tile, jnp.arange(tiles, dtype=jnp.int32))
    return blocks.transpose(1, 0, 2).reshape(6, tiles * TILE)


def whole_contact(hood, partner):
    tiles = BOXES_DOWNSLOPE * BOXES_SPANWISE * BOXES_NORMAL
    shifted = jnp.concatenate([hood[:, :3] + offset_table()[:, :, None], hood[:, 3:4]], axis=1)
    table = shifted.reshape(27, 4, tiles, TILE).transpose(0, 2, 1, 3).reshape(27 * tiles, 4, TILE)
    own_idx = 13 * tiles + jnp.arange(tiles, dtype=jnp.int32)
    return contact_tiles(table, partner, own_idx)


def grain_loads(state, contact):
    radius = state[3]
    masses = 4.0 * math.pi / 3.0 * radius * radius * radius
    vel_u, vel_v, vel_w = (state[4], state[5], state[6])
    kinetic = jnp.stack(
        [vel_u * vel_u, vel_v * vel_v, vel_w * vel_w, vel_u * vel_v, vel_u * vel_w, vel_v * vel_w]
    )
    moments = jnp.stack([masses, masses * vel_u, masses * vel_v, masses * vel_w])
    return jnp.concatenate([moments, contact + masses[None, :] * kinetic], axis=0)


def kernel_rows(coords, centres):
    diff = coords[:, None] - centres[None, :]
    return jnp.maximum(jnp.exp(-0.5 * diff * diff) - CUT_LEVEL, 0.0) * NORM_ONE


def deposit(positions, loads, centres_x, centres_y, centres_z):
    weight_x = kernel_rows(positions[0], centres_x)
    weight_y = kernel_rows(positions[1], centres_y)
    weight_z = kernel_rows(positions[2], centres_z)
    count = positions.shape[1]
    plane = (weight_x[:, :, None] * weight_y[:, None, :]).astype(jnp.bfloat16).reshape(count, -1)
    height = (loads[:, None, :] * weight_z.T[None, :, :]).astype(jnp.bfloat16).reshape(-1, count)
    return jnp.dot(height, plane, preferred_element_type=jnp.float32)


def add_rims(wide, received, axis, border_extent):
    length = wide.shape[axis]
    inner = lax.slice_in_dim(wide, border_extent, length - border_extent, axis=axis)
    count = inner.shape[axis]
    lower = lax.slice_in_dim(received, 0, border_extent, axis=axis)
    upper = lax.slice_in_dim(received, 3 * border_extent, 4 * border_extent, axis=axis)
    low_pad = [(0, 0)] * wide.ndim
    high_pad = [(0, 0)] * wide.ndim
    low_pad[axis] = (0, count - border_extent)
    high_pad[axis] = (count - border_extent, 0)
    return inner + jnp.pad(lower, low_pad) + jnp.pad(upper, high_pad)


def both_rims(wide, axis, border_extent):
    length = wide.shape[axis]
    return jnp.concatenate(
        [
            lax.slice_in_dim(wide, 0, border_extent, axis=axis),
            lax.slice_in_dim(wide, length - border_extent, length, axis=axis),
        ],
        axis=axis,
    )


def column_fit(profile):
    cell_pitch = TILE_BOX_EDGE / CELLS_PER_EDGE
    density, velocity, shear, press = (profile[0], profile[1], profile[2], profile[3])
    upper = jnp.concatenate([velocity[..., 1:, :], velocity[..., -1:, :]], axis=-2)
    lower = jnp.concatenate([velocity[..., :1, :], velocity[..., :-1, :]], axis=-2)
    rate = (upper - lower) / (2.0 * cell_pitch)
    inertial = rate * 1.0 / jnp.sqrt((press + FLOOR_LEVEL) / (density + FLOOR_LEVEL))
    friction = shear / (press + FLOOR_LEVEL)
    weight = density + FLOOR_LEVEL
    sum_zero = jnp.sum(weight, axis=-2)
    sum_one = jnp.sum(weight * inertial, axis=-2)
    sum_two = jnp.sum(weight * inertial * inertial, axis=-2) + RIDGE_SHARE * sum_zero
    mix_zero = jnp.sum(weight * friction, axis=-2)
    mix_one = jnp.sum(weight * friction * inertial, axis=-2)
    determ = sum_zero * sum_two - sum_one * sum_one
    fitted = jnp.stack(
        [
            (mix_zero * sum_two - sum_one * mix_one) / determ,
            (sum_zero * mix_one - sum_one * mix_zero) / determ,
        ]
    )
    return (fitted, inertial)


def local(grains, pairs):
    tiles = BOXES_DOWNSLOPE * BOXES_SPANWISE * BOXES_NORMAL
    grains_all = tiles * TILE
    extent_downslope, extent_spanwise, extent_normal = (
        CELLS_PER_EDGE * BOXES_DOWNSLOPE,
        CELLS_PER_EDGE * BOXES_SPANWISE,
        CELLS_PER_EDGE * BOXES_NORMAL,
    )
    border_extent = CELLS_PER_EDGE
    cell_pitch = TILE_BOX_EDGE / CELLS_PER_EDGE
    own_state = grains[0, 0, 0]
    partner = pairs[0, 0, 0]
    shapes = padded(grains[:, :, :, :4], (("gx", 0), ("gy", 1), ("gz", 2)), 1)
    contact = whole_contact(shapes.reshape(27, 4, grains_all), partner)
    loads = grain_loads(own_state, contact)
    centres_x = (
        jnp.arange(extent_downslope + 2 * border_extent, dtype=jnp.float32) - border_extent + 0.5
    ) * cell_pitch
    centres_y = (
        jnp.arange(extent_spanwise + 2 * border_extent, dtype=jnp.float32) - border_extent + 0.5
    ) * cell_pitch
    centres_z = (
        jnp.arange(extent_normal + 2 * border_extent, dtype=jnp.float32) - border_extent + 0.5
    ) * cell_pitch
    wide = deposit(own_state[:3], loads, centres_x, centres_y, centres_z)
    wide = wide.reshape(
        10,
        extent_normal + 2 * border_extent,
        extent_downslope + 2 * border_extent,
        extent_spanwise + 2 * border_extent,
    )
    received = padded(both_rims(wide, 2, border_extent), (("gx", 2),), border_extent)
    wide = add_rims(wide, received, 2, border_extent)
    received = padded(both_rims(wide, 3, border_extent), (("gy", 3),), border_extent)
    wide = add_rims(wide, received, 3, border_extent)
    received = padded(both_rims(wide, 1, border_extent), (("gz", 1),), border_extent)
    wide = add_rims(wide, received, 1, border_extent)
    fields = wide.reshape(10, extent_normal, extent_downslope * extent_spanwise)
    density = fields[0]
    velocity = fields[1] / (density + FLOOR_LEVEL)
    shear = fields[8]
    press = (fields[4] + fields[5] + fields[6]) / 3.0
    profile = jnp.stack([density, velocity, shear, press])
    whole = lax.all_gather(profile, "gz", axis=1, tiled=True)
    fitted, inertial = column_fit(whole)
    share = extent_downslope * extent_spanwise // lax.axis_size("gz")
    start = lax.axis_index("gz") * share
    fitted = lax.dynamic_slice_in_dim(fitted, start, share, 1)
    inertial = lax.dynamic_slice_in_dim(inertial, start, share, 1)
    return (fields[None, None, None], fitted[None, None], inertial[None, None])


def solution(mesh):
    in_specs = (P("gx", "gy", "gz", None, None), P("gx", "gy", "gz", None, None))
    out_specs = (
        P("gx", "gy", "gz", None, None, None),
        P("gx", "gy", None, "gz"),
        P("gx", "gy", None, "gz"),
    )
    return jax.shard_map(local, mesh=mesh, in_specs=in_specs, out_specs=out_specs, check_vma=False)
```

profile of v0, /device:TPU:10, one launch (start us, length us, event | category | flops | bytes accessed | tf_op | source)
XLA Modules:
  0.0 505.8 jit_solution(16609334066317939805)
XLA Ops:
  3.4 3.6 collective-permute-start.1
  12.1 3.3 fusion.21
  16.9 3.5 collective-permute-start.2
  24.5 3.5 collective-permute-done.3
  28.6 3.5 collective-permute-start.4
  34.9 7.2 %collective-permute-done.4 = f32[3,3,1,4,4096]{4,2,3,1,0:T(1,128)S(1)} collective-permute-done((f32[3,3,1,4,4096]{4,2,3,1,0:T(1,128)S(1)}, f32[3,3,1,4,4096]{4,2,3,1,0:T(1,128)S(1)}, u32[]{:S(2)}, u32[]{:S(2)}) %collective-permute-start.4) | collective-permute-done | bytes 589856 | tf_op jit(solution)/shard_map/ppermute | solution.py:31
  42.1 4.1 collective-permute-done.5
  53.8 389.9 %while.11 = (s32[]{:T(128)}, f32[32,6,128]{2,1,0:T(8,128)}, s32[32]{0:T(128)S(1)}, s32[32,27]{1,0:T(8,128)}, s32[32]{0:T(128)}, /*index=5*/f32[864,4,128]{2,1,0:...) while((s32[]{:T(128)}, f32[32,6,128]{2,1,0:T(8,128)}, s32[32]{0:T(128)S(1)}, ...), condition=%wide.region_7.8_spmd.clone, body=%wide.region_0.7_spmd.clone.sunk | while | flops 14619360 | bytes 350041 | solution.py:81
  62.5 2.9 fusion.74
  74.7 2.9 fusion.74
  86.9 2.9 fusion.74
  99.1 2.9 fusion.74
  111.3 2.9 fusion.74
  123.5 2.9 fusion.74
  135.7 2.9 fusion.74
  147.9 2.9 fusion.74
  160.1 2.9 fusion.74
  184.4 2.9 fusion.74
  196.6 2.9 fusion.74
  208.7 2.9 fusion.74
  233.1 2.9 fusion.74
  245.2 2.9 fusion.74
  257.4 2.9 fusion.74
  281.8 2.9 fusion.74
  445.0 9.1 %fusion.22 = f32[10,16,40,16]{2,1,3,0:T(8,128)S(1)} fusion(bf16[40,16,4096]{2,1,0:T(8,128)(2,1)} %fusion.21, f32[16,4096]{1,0:T(8,128)S(1)} %copy-done.1, f32[10,4096]{1,0:T(8,128)S(1)} %concatenate.25), kind=kOutput, calls=%fused_computation.56 | convolution fusion | flops 840171520 | bytes 6078464 | tf_op jit(solution)/shard_map/dot_general | solution.py:116
  461.8 3.9 collective-permute-start.7
  470.6 3.0 copy.37
  475.7 3.5 collective-permute-start.8
  481.6 3.1 collective-permute-done.8
  484.7 3.5 collective-permute-done.9
  493.0 4.1 collective-permute-done.11
  498.1 4.6 all_gather.3
  (516 shorter events, 271.7 us)
Async XLA Ops:
  1.5 15.3 %collective-permute-start = (f32[1,1,1,4,4096]{4,2,3,1,0:T(1,128)S(1)}, f32[1,1,1,4,4096]{4,2,3,1,0:T(1,128)S(1)}, u32[]{:S(2)}, u32[]{:S(2)}) collective-permute-start(f32[1,1,1,4,4096]{4,2,3,1,0:T(1,128)S(1)} %slice.171), channel_id=1, source_target_pairs={{0,8},{8,16},{16,24},{1,9},{9,17},{17,25},{2,10},{10,18},{18,26},{... | collective-permute-start | bytes 196616 | tf_op jit(solution)/shard_map/ppermute | solution.py:31
  3.4 13.3 %collective-permute-start.1 = (f32[1,1,1,4,4096]{4,2,3,1,0:T(1,128)S(1)}, f32[1,1,1,4,4096]{4,2,3,1,0:T(1,128)S(1)}, u32[]{:S(2)}, u32[]{:S(2)}) collective-permute-start(f32[1,1,1,4,4096]{4,2,3,1,0:T(1,128)S(1)} %slice.171), channel_id=1, source_target_pairs={{8,0},{16,8},{24,16},{9,1},{17,9},{25,17},{10,2},{18,10},{26,18},{... | collective-permute-start | bytes 196616 | tf_op jit(solution)/shard_map/ppermute | solution.py:32
  16.9 7.6 %collective-permute-start.2 = (f32[3,1,1,4,4096]{4,2,3,1,0:T(1,128)S(1)}, f32[3,1,1,4,4096]{4,2,3,1,0:T(1,128)S(1)}, u32[]{:S(2)}, u32[]{:S(2)}) collective-permute-start(f32[3,1,1,4,4096]{4,2,3,1,0:T(1,128)S(1)} %pad_maximum_fusion.3), channel_id=1, source_target_pairs={{0,2},{2,4},{4,6},{1,3},{3,5},{5,7},{8,10},{10,12},{12,14},{9,11},... | collective-permute-start | bytes 589832 | tf_op jit(solution)/shard_map/ppermute | solution.py:31
  20.4 7.6 %collective-permute-start.3 = (f32[3,1,1,4,4096]{4,2,3,1,0:T(1,128)S(1)}, f32[3,1,1,4,4096]{4,2,3,1,0:T(1,128)S(1)}, u32[]{:S(2)}, u32[]{:S(2)}) collective-permute-start(f32[3,1,1,4,4096]{4,2,3,1,0:T(1,128)S(1)} %pad_maximum_fusion.3), channel_id=1, source_target_pairs={{2,0},{4,2},{6,4},{3,1},{5,3},{7,5},{10,8},{12,10},{14,12},{11,9},... | collective-permute-start | bytes 589832 | tf_op jit(solution)/shard_map/ppermute | solution.py:32
  28.6 13.5 %collective-permute-start.4 = (f32[3,3,1,4,4096]{4,2,3,1,0:T(1,128)S(1)}, f32[3,3,1,4,4096]{4,2,3,1,0:T(1,128)S(1)}, u32[]{:S(2)}, u32[]{:S(2)}) collective-permute-start(f32[3,3,1,4,4096]{4,2,3,1,0:T(1,128)S(1)} %pad_maximum_fusion.2), channel_id=1, source_target_pairs={{0,1},{2,3},{4,5},{6,7},{8,9},{10,11},{12,13},{14,15},{16,17},{18,... | collective-permute-start | bytes 1769480 | tf_op jit(solution)/shard_map/ppermute | solution.py:31
  32.1 14.2 %collective-permute-start.5 = (f32[3,3,1,4,4096]{4,2,3,1,0:T(1,128)S(1)}, f32[3,3,1,4,4096]{4,2,3,1,0:T(1,128)S(1)}, u32[]{:S(2)}, u32[]{:S(2)}) collective-permute-start(f32[3,3,1,4,4096]{4,2,3,1,0:T(1,128)S(1)} %pad_maximum_fusion.2), channel_id=1, source_target_pairs={{1,0},{3,2},{5,4},{7,6},{9,8},{11,10},{13,12},{15,14},{17,16},{19,... | collective-permute-start | bytes 1769480 | tf_op jit(solution)/shard_map/ppermute | solution.py:32
  53.8 389.9 %copy-start = (f32[6,4096]{1,0:T(8,128)S(1)}, f32[6,4096]{1,0:T(8,128)}, u32[]{:S(2)}) copy-start(f32[6,4096]{1,0:T(8,128)} %stack.30) | copy-start | bytes 294916
  53.8 389.9 %copy-start.5 = (f32[4096]{0:T(1024)S(1)}, f32[4096]{0:T(1024)}, u32[]{:S(2)}) copy-start(f32[4096]{0:T(1024)} %multiply_multiply_fusion.3) | copy-start | bytes 49156
  53.8 390.9 %copy-start.2 = (f32[1,4096]{1,0:T(1,128)S(1)}, f32[1,4096]{1,0:T(1,128)}, u32[]{:S(2)}) copy-start(f32[1,4096]{1,0:T(1,128)} %get-tuple-element.120) | copy-start | bytes 49156
  53.8 390.9 %copy-start.3 = (f32[1,4096]{1,0:T(1,128)S(1)}, f32[1,4096]{1,0:T(1,128)}, u32[]{:S(2)}) copy-start(f32[1,4096]{1,0:T(1,128)} %get-tuple-element.108) | copy-start | bytes 49156
  53.8 390.9 %copy-start.4 = (f32[1,4096]{1,0:T(1,128)S(1)}, f32[1,4096]{1,0:T(1,128)}, u32[]{:S(2)}) copy-start(f32[1,4096]{1,0:T(1,128)} %get-tuple-element.109) | copy-start | bytes 49156
  53.8 391.2 %copy-start.1 = (f32[16,4096]{1,0:T(8,128)S(1)}, f32[16,4096]{1,0:T(8,128)}, u32[]{:S(2)}) copy-start(f32[16,4096]{1,0:T(8,128)} %fusion.39) | copy-start | bytes 786436
  458.0 8.7 %collective-permute-start.6 = (f32[10,16,4,16]{3,1,2,0:T(8,128)S(1)}, f32[10,16,4,16]{3,1,2,0:T(8,128)S(1)}, u32[]{:S(2)}, u32[]{:S(2)}) collective-permute-start(f32[10,16,4,16]{3,1,2,0:T(8,128)S(1)} %copy.34), channel_id=1, source_target_pairs={{0,8},{8,16},{16,24},{1,9},{9,17},{17,25},{2,10},{10,18},{18,26},{... | collective-permute-start | bytes 122888 | tf_op jit(solution)/shard_map/ppermute | solution.py:31
  461.8 8.8 %collective-permute-start.7 = (f32[10,16,4,16]{3,1,2,0:T(8,128)}, f32[10,16,4,16]{3,1,2,0:T(8,128)}, u32[]{:S(2)}, u32[]{:S(2)}) collective-permute-start(f32[10,16,4,16]{3,1,2,0:T(8,128)} %copy.36), channel_id=1, source_target_pairs={{8,0},{16,8},{24,16},{9,1},{17,9},{25,17},{10,2},{18,10},{26,18},{... | collective-permute-start | bytes 122888 | tf_op jit(solution)/shard_map/ppermute | solution.py:32
  475.7 9.0 %collective-permute-start.8 = (f32[10,16,32,4]{2,1,3,0:T(8,128)S(1)}, f32[10,16,32,4]{2,1,3,0:T(8,128)S(1)}, u32[]{:S(2)}, u32[]{:S(2)}) collective-permute-start(f32[10,16,32,4]{2,1,3,0:T(8,128)S(1)} %get-tuple-element.98), channel_id=1, source_target_pairs={{0,2},{2,4},{4,6},{1,3},{3,5},{5,7},{8,10},{10,12},{12,14},{9,11},... | collective-permute-start | bytes 245768 | tf_op jit(solution)/shard_map/ppermute | solution.py:31
  479.2 9.0 %collective-permute-start.9 = (f32[10,16,32,4]{2,1,3,0:T(8,128)S(1)}, f32[10,16,32,4]{2,1,3,0:T(8,128)S(1)}, u32[]{:S(2)}, u32[]{:S(2)}) collective-permute-start(f32[10,16,32,4]{2,1,3,0:T(8,128)S(1)} %get-tuple-element.99), channel_id=1, source_target_pairs={{2,0},{4,2},{6,4},{3,1},{5,3},{7,5},{10,8},{12,10},{14,12},{11,9},... | collective-permute-start | bytes 245768 | tf_op jit(solution)/shard_map/ppermute | solution.py:32
  488.4 4.6 collective-permute-start.10
  489.9 7.2 %collective-permute-start.11 = (f32[10,4,32,8]{2,1,3,0:T(4,128)S(1)}, f32[10,4,32,8]{2,1,3,0:T(4,128)S(1)}, u32[]{:S(2)}, u32[]{:S(2)}) collective-permute-start(f32[10,4,32,8]{2,1,3,0:T(4,128)S(1)} %get-tuple-element.103), channel_id=1, source_target_pairs={{1,0},{3,2},{5,4},{7,6},{9,8},{11,10},{13,12},{15,14},{17,16},{19,... | collective-permute-start | bytes 122888 | tf_op jit(solution)/shard_map/ppermute | solution.py:32
where the time goes:
time: 511 us; the launch traced here: 506 us
  other arithmetic  174 us (34%)
  local copies, waits for them, and re-layouts  131 us (26%)
  loops' own time  123 us (24%)
  waiting for transfers between devices  32.3 us (6%)
  starting transfers between devices  30.8 us (6%)
  matrix products  9.09 us (2%)
    another operation x1, loops' own time, contact_tiles(): blocks = lax.map(one_tile, jnp.arange(tiles, dtype=jnp.int32))  123 us
    reduce_sum x32, other arithmetic, one_tile(): jnp.sum(force * delta_y * delta_z, 1)  92.3 us
    ge x32, other arithmetic, one_tile(): is_valid = partner_ids >= 0  42.3 us
    dynamic_slice x32, local copies, waits for them, and re-layouts, one_tile(): own_place = own_idx[slot]  41.9 us
    select_n x32, other arithmetic, one_tile(): others = table[safe_ids].transpose(1, 0, 2).reshape(4, hood_count * TILE)  22.1 us
    dynamic_slice x32, local copies, waits for them, and re-layouts, contact_tiles(): blocks = lax.map(one_tile, jnp.arange(tiles, dtype=jnp.int32))  20.7 us
    gather x32, local copies, waits for them, and re-layouts, one_tile(): others = table[safe_ids].transpose(1, 0, 2).reshape(4, hood_count * TILE)  19.3 us
    dynamic_update_slice x32, local copies, waits for them, and re-layouts, contact_tiles(): blocks = lax.map(one_tile, jnp.arange(tiles, dtype=jnp.int32))  19.2 us
  transfers between devices with their start and end apart: 12, of which 10 were waited for; matrix products, arithmetic and copies ran while one was open for 3% of the time, Pallas kernels for 0%

commit v1 on v0

v1 whole, which is shorter than its diff:
```python
import math

import jax
import jax.numpy as jnp
from jax import lax
from jax.experimental import pallas as pl
from jax.experimental.pallas import tpu as pltpu
from jax.sharding import PartitionSpec as P

TILE = 128
BOXES_DOWNSLOPE = 8
BOXES_SPANWISE = 2
BOXES_NORMAL = 2
CELLS_PER_EDGE = 4

TILE_BOX_EDGE = 5.0
SPRING = 2.0
SOFTEN = 0.05
FLOOR_LEVEL = 0.1
RIDGE_SHARE = 0.1
CUT_LEVEL = math.exp(-12.5)
NORM_ONE = 1.0 / math.sqrt(2.0 * math.pi)

PITCH = TILE_BOX_EDGE / CELLS_PER_EDGE
REACH = 1.21
ABSENT = -10.0

NB = BOXES_DOWNSLOPE * BOXES_SPANWISE * BOXES_NORMAL
COLS = CELLS_PER_EDGE * BOXES_DOWNSLOPE * CELLS_PER_EDGE * BOXES_SPANWISE
CAPS = (16, 12, 16, 12, 14)

F32 = jnp.float32
BF16 = jnp.bfloat16


def iota(shape, dim):
    return lax.broadcasted_iota(jnp.int32, shape, dim)


def split3(value):
    high = value.astype(BF16)
    rest = value - high.astype(F32)
    mid = rest.astype(BF16)
    low = (rest - mid.astype(F32)).astype(BF16)
    return high, mid, low


def pick(value, onehot):
    high, mid, low = split3(value)
    dot = lambda part: jnp.dot(part, onehot, preferred_element_type=F32)
    return (dot(low) + dot(mid)) + dot(high)


def sort_kernel(place_ref, grains_ref, pairs_ref, out_ref):
    pairs = pairs_ref[...]
    live = pairs >= 0
    hood = jnp.where(live, pairs, 0) >> 5
    third = (hood * 11) >> 5
    part_c = hood - 3 * third
    part_b = third - 3 * ((third * 11) >> 5)

    def has(part, value):
        hit = jnp.where(live & (part == value), 1.0, 0.0)
        return jnp.max(hit, axis=1, keepdims=True) > 0.5

    last_b = place_ref[0] == 1
    last_c = place_ref[1] == 1
    box_y = has(part_b, 2) | (last_b & jnp.logical_not(has(part_b, 0)))
    box_z = has(part_c, 2) | (last_c & jnp.logical_not(has(part_c, 0)))
    rows = [grains_ref[r] for r in range(7)]
    centre = 0.5 * (jnp.min(rows[0], axis=1, keepdims=True) + jnp.max(rows[0], axis=1, keepdims=True))
    key = centre + jnp.where(box_y, 64.0, 0.0) + jnp.where(box_z, 128.0, 0.0)
    sub = iota((NB, TILE), 0)
    lane = iota((NB, TILE), 1)
    wide = jnp.broadcast_to(key, (NB, TILE))
    key_row = jnp.sum(jnp.where(sub == lane, wide, 0.0), axis=0, keepdims=True)
    before = (wide < key_row) | ((wide == key_row) & (sub < lane))
    rank = jnp.sum(jnp.where(before, 1.0, 0.0), axis=0, keepdims=True)
    onehot = jnp.where((rank == sub.astype(F32)) & (lane < NB), 1.0, 0.0).astype(BF16)[:, :NB]
    for r in range(7):
        high, mid, low = split3(rows[r])
        dot = lambda part: jnp.dot(onehot, part, preferred_element_type=F32)
        out_ref[r] = (dot(low) + dot(mid)) + dot(high)


def box_sort(grains, pairs, place):
    return pl.pallas_call(
        sort_kernel,
        out_shape=jax.ShapeDtypeStruct((7, NB, TILE), F32),
        in_specs=[
            pl.BlockSpec(memory_space=pltpu.SMEM),
            pl.BlockSpec(memory_space=pltpu.VMEM),
            pl.BlockSpec(memory_space=pltpu.VMEM),
        ],
        out_specs=pl.BlockSpec(memory_space=pltpu.VMEM),
        name="box_sort",
    )(place, grains, pairs)


def pack(lists, tri):
    rows = lists[0][1][0].shape[0]
    lane = iota((rows, TILE), 1)
    lane_f = lane.astype(F32)
    offset = jnp.zeros((rows, TILE), F32)
    outs = [jnp.zeros((rows, TILE), F32)] * 3 + [jnp.full((rows, TILE), ABSENT, F32)]
    for mask, arrays in lists:
        both = jnp.dot(jnp.where(mask, 1.0, 0.0).astype(BF16), tri, preferred_element_type=F32)
        ranks, total = both[:, :TILE], both[:, TILE:]
        wanted = lane_f - offset
        place = jnp.zeros((rows, TILE), jnp.int32)
        for bit in (64, 32, 16, 8, 4, 2, 1):
            probe = jnp.take_along_axis(ranks, place + (bit - 1), axis=1)
            place = jnp.where(probe <= wanted, place + bit, place)
        ours = (wanted >= 0.0) & (wanted < total)
        outs = [jnp.where(ours, jnp.take_along_axis(a, place, axis=1), o) for a, o in zip(arrays, outs)]
        offset = offset + total
    return outs, offset


def pair_terms(own, cand, sums):
    own_x, own_y, own_z, own_r = own
    cand_x, cand_y, cand_z, cand_r = cand
    dx, dy, dz = own_x - cand_x, own_y - cand_y, own_z - cand_z
    square = dx * dx + dy * dy + dz * dz
    distance = square * lax.rsqrt(jnp.maximum(square, 1e-30))
    overlap = jnp.maximum(own_r + cand_r - distance, 0.0)
    below = distance + SOFTEN
    guess = pl.reciprocal(below, approx=True)
    force = (0.5 * SPRING) * overlap * (guess * (2.0 - below * guess))
    fx, fy, fz = force * dx, force * dy, force * dz
    terms = (fx * dx, fy * dy, fz * dz, fx * dy, fx * dz, fy * dz)
    return tuple(s + t for s, t in zip(sums, terms))


def stress_kernel(grid_ref, side_ref, grains_ref, out_ref, cand_ref, all_ref, contact_ref, plane_ref, height_ref):
    tri_row = iota((TILE, 2 * TILE), 0)
    tri_col = iota((TILE, 2 * TILE), 1)
    tri = jnp.where((tri_row <= tri_col) | (tri_col >= TILE), 1.0, 0.0).astype(BF16)

    row = iota((16 * 8, TILE), 0)
    row_x = row & 7
    row_y = (row >> 3) & 3
    row_z = row >> 5
    span_y = BOXES_SPANWISE * TILE_BOX_EDGE
    span_z = BOXES_NORMAL * TILE_BOX_EDGE
    span_x = BOXES_DOWNSLOPE * TILE_BOX_EDGE
    shift_y = jnp.where(row_y == 0, -span_y, jnp.where(row_y == 3, span_y, 0.0))
    shift_z = jnp.where(row_z == 0, -span_z, jnp.where(row_z == 3, span_z, 0.0))
    radius = grid_ref[3]
    radius = jnp.where(radius == 0.0, ABSENT, radius)
    here = [grid_ref[0], grid_ref[1] + shift_y, grid_ref[2] + shift_z, radius]

    side = iota((16, TILE), 0)
    side_y = side & 3
    side_z = side >> 2
    side_shift_y = jnp.where(side_y == 0, -span_y, jnp.where(side_y == 3, span_y, 0.0))
    side_shift_z = jnp.where(side_z == 0, -span_z, jnp.where(side_z == 3, span_z, 0.0))
    sides = []
    for k, shift_x in ((0, -span_x), (1, span_x)):
        r = side_ref[k, 3]
        sides.append(
            [
                side_ref[k, 0] + shift_x,
                side_ref[k, 1] + side_shift_y,
                side_ref[k, 2] + side_shift_z,
                jnp.where(r == 0.0, ABSENT, r),
            ]
        )

    in_box_x = iota((16, 8, TILE), 1)

    def neighbours(centre, edge, step):
        cube = centre.reshape(16, 8, TILE)
        moved = pltpu.roll(cube, 1 if step < 0 else 7, 1)
        at_edge = in_box_x == (0 if step < 0 else 7)
        return jnp.where(at_edge, edge[:, None, :], moved).reshape(16 * 8, TILE)

    before = [neighbours(c, e, -1) for c, e in zip(here, sides[0])]
    after = [neighbours(c, e, 1) for c, e in zip(here, sides[1])]
    low_x = TILE_BOX_EDGE * row_x.astype(F32)
    beside_x, count_x = pack(
        [
            ((before[0] >= low_x - REACH) & (before[3] > 0.0), before),
            ((after[0] <= low_x + (TILE_BOX_EDGE + REACH)) & (after[3] > 0.0), after),
        ],
        tri,
    )
    worst = [jnp.max(count_x) - 8.0 * CAPS[1]]

    def cut_y(arrays, start):
        return [a.reshape(4, 4, 8, TILE)[:, start : start + 2].reshape(4 * 2 * 8, TILE) for a in arrays]

    low_y = TILE_BOX_EDGE * ((iota((64, TILE), 0) >> 3) & 1).astype(F32)

    def near_y(arrays, start):
        cut = cut_y(arrays, start)
        near = (cut[1] >= low_y - REACH) if start == 0 else (cut[1] <= low_y + (TILE_BOX_EDGE + REACH))
        return near & (cut[3] > 0.0), cut

    beside_y, count_y = pack(
        [near_y(here, 0), near_y(beside_x, 0), near_y(here, 2), near_y(beside_x, 2)], tri
    )
    worst.append(jnp.max(count_y) - 8.0 * CAPS[2])

    def cut_z(arrays, start):
        return [a[16 * start : 16 * start + 32] for a in arrays]

    low_z = TILE_BOX_EDGE * (iota((32, TILE), 0) >> 4).astype(F32)

    def near_z(arrays, start):
        cut = cut_z(arrays, start)
        near = (cut[2] >= low_z - REACH) if start == 0 else (cut[2] <= low_z + (TILE_BOX_EDGE + REACH))
        return near & (cut[3] > 0.0), cut

    mid_here, mid_x = cut_y(here, 1), cut_y(beside_x, 1)
    above, count_z = pack([near_z(mid_here, 0), near_z(mid_here, 2)], tri)
    worst.append(jnp.max(count_z) - 8.0 * CAPS[3])
    above_rest, count_w = pack(
        [near_z(mid_x, 0), near_z(beside_y, 0), near_z(mid_x, 2), near_z(beside_y, 2)], tri
    )
    worst.append(jnp.max(count_w) - 8.0 * CAPS[4])
    chunks = [cut_z(mid_here, 1), cut_z(mid_x, 1), cut_z(beside_y, 1), above, above_rest]
    for k, chunk in enumerate(chunks):
        for c in range(4):
            cand_ref[(4 * k + c) * NB : (4 * k + c + 1) * NB, :] = chunk[c]
    overflow = worst[0]
    for w in worst[1:]:
        overflow = jnp.maximum(overflow, w)

    def own_rows(t):
        return tuple(
            jnp.broadcast_to(cand_ref[pl.ds(c * NB + t, 1), :], (8, TILE)) for c in range(4)
        )

    def group(columns, first, g):
        return tuple(
            jnp.broadcast_to(columns[8 * g : 8 * g + 8, first + c : first + c + 1], (8, TILE)) for c in range(4)
        )

    def put(t, sums):
        for k in range(6):
            contact_ref[pl.ds(k * NB + t, 1), :] = jnp.sum(sums[k], axis=0, keepdims=True)

    zeros = tuple(jnp.zeros((8, TILE), F32) for _ in range(6))

    @pl.when(overflow <= 0.0)
    def _():
        def one_tile(t, carry):
            own = own_rows(t)
            columns = cand_ref[pl.ds(t, 24, stride=NB), :].T
            sums = zeros
            for k in range(5):
                for g in range(CAPS[k]):
                    sums = pair_terms(own, group(columns, 4 * k, g), sums)
            put(t, sums)
            return carry

        lax.fori_loop(0, NB, one_tile, 0)

    @pl.when(overflow > 0.0)
    def _():
        stride = 16 * 8 + 32
        for c in range(4):
            all_ref[c * stride : c * stride + 128, :] = here[c]
            all_ref[c * stride + 128 : c * stride + 144, :] = sides[0][c]
            all_ref[c * stride + 144 : c * stride + 160, :] = sides[1][c]
            all_ref[(c + 4) * stride : (c + 5) * stride, :] = jnp.zeros((stride, TILE), F32)

        def one_tile(t, carry):
            own = own_rows(t)
            tile_x, tile_y, tile_z = t & 7, (t >> 3) & 1, t >> 4

            def one_near(n, sums):
                n_x = n // 9
                n_y = (n - 9 * n_x) // 3
                n_z = n - 9 * n_x - 3 * n_y
                at_x = tile_x + n_x - 1
                plane = 4 * (tile_z + n_z) + tile_y + n_y
                place = jnp.where(
                    at_x < 0, 128 + plane, jnp.where(at_x > 7, 144 + plane, 8 * plane + at_x)
                )
                columns = all_ref[pl.ds(place, 8, stride=stride), :].T
                for g in range(16):
                    sums = pair_terms(own, group(columns, 0, g), sums)
                return sums

            put(t, lax.fori_loop(0, 27, one_near, zeros))
            return carry

        lax.fori_loop(0, NB, one_tile, 0)

    nx = CELLS_PER_EDGE * (BOXES_DOWNSLOPE + 2)
    ny = CELLS_PER_EDGE * (BOXES_SPANWISE + 2)
    nz = CELLS_PER_EDGE * (BOXES_NORMAL + 2)

    def weights(coords, centres):
        diff = coords - centres
        return jnp.maximum(jnp.exp(-0.5 * diff * diff) - CUT_LEVEL, 0.0) * NORM_ONE

    def centres(count):
        return (iota((count, TILE), 0).astype(F32) - CELLS_PER_EDGE + 0.5) * PITCH

    at_z = iota((8, TILE), 0)
    rim_z = jnp.where(at_z < 4, at_z, at_z + 8)
    centres_rim = (rim_z.astype(F32) - CELLS_PER_EDGE + 0.5) * PITCH

    def one_deposit(t, carry):
        rows = [grains_ref[pl.ds(r * NB + t, 1), :] for r in range(7)]
        wx = weights(rows[0], centres(nx))
        wy = weights(rows[1], centres(ny))
        wz = weights(rows[2], centres(nz))
        wz_rim = jnp.concatenate([wz[0:4], wz[12:16]], axis=0)
        wz_inner = wz[4:12]
        masses = 4.0 * math.pi / 3.0 * rows[3] * rows[3] * rows[3]
        vel = rows[4:7]
        cont = [contact_ref[pl.ds(k * NB + t, 1), :] for k in range(6)]
        loads = [masses, masses * vel[0], masses * vel[1], masses * vel[2]]
        for k, (i, j) in enumerate(((0, 0), (1, 1), (2, 2), (0, 1), (0, 2), (1, 2))):
            loads.append(cont[k] + masses * (vel[i] * vel[j]))
        height = [load * wz_inner for load in loads] + [load * wz_rim for load in loads]
        lanes = pl.ds(pl.multiple_of(t * TILE, TILE), TILE)
        height_ref[:, lanes] = jnp.concatenate(height, axis=0).astype(BF16)
        parts = [wx[x : x + 1] * wy for x in list(range(4)) + list(range(nx - 4, nx))]
        inner_x = wx[4 : nx - 4]
        parts += [inner_x * wy[y : y + 1] for y in list(range(4)) + list(range(ny - 4, ny))]
        inner_y = wy[4 : ny - 4]
        parts += [wx[x : x + 1] * inner_y for x in range(4, nx - 4)]
        plane_ref[:, lanes] = jnp.concatenate(parts, axis=0).astype(BF16)
        return carry

    lax.fori_loop(0, NB, one_deposit, 0)
    out_ref[...] = lax.dot_general(
        height_ref[...], plane_ref[...], (((1,), (1,)), ((), ())), preferred_element_type=F32
    )


def stress_and_deposit(grid, side, grains):
    vmem = pl.BlockSpec(memory_space=pltpu.VMEM)
    return pl.pallas_call(
        stress_kernel,
        out_shape=jax.ShapeDtypeStruct((160, 128 + 2 * 128 + COLS), F32),
        in_specs=[vmem, vmem, vmem],
        out_specs=vmem,
        scratch_shapes=[
            pltpu.VMEM((24 * NB, TILE), F32),
            pltpu.VMEM((8 * 160, TILE), F32),
            pltpu.VMEM((6 * NB, TILE), F32),
            pltpu.VMEM((128 + 2 * 128 + COLS, NB * TILE), BF16),
            pltpu.VMEM((160, NB * TILE), BF16),
        ],
        name="stress_deposit",
    )(grid, side, grains)


def rim_x_kernel(wide_ref, left_ref, right_ref, low_ref, high_ref, inner_ref):
    lane = iota((160, TILE), 1)
    got = jnp.where(lane < 64, right_ref[...], left_ref[...])
    src = iota((TILE, 1), 0)
    x = (src >> 4) & 3
    x = jnp.where(src >= 64, x, x + (CELLS_PER_EDGE * BOXES_DOWNSLOPE - 4))
    y = src & 15
    target = jnp.where(y < 4, y * 32 + x, jnp.where(y >= 12, 128 + (y - 12) * 32 + x, 256 + x * 8 + y - 4))
    onehot = jnp.where(iota((TILE, 512), 1) == target, 1.0, 0.0).astype(BF16)
    total = wide_ref[:, 128:] + pick(got, onehot)
    low_ref[...] = total[:, :128]
    high_ref[...] = total[:, 128:256]
    inner_ref[...] = total[:, 256:]


def rim_y_kernel(inner_ref, left_ref, right_ref, out_ref):
    got = jnp.concatenate([left_ref[...], right_ref[...]], axis=1)
    src = iota((256, 1), 0)
    target = (src & 31) * 8 + 4 * (src >> 7) + ((src >> 5) & 3)
    onehot = jnp.where(iota((256, 256), 1) == target, 1.0, 0.0).astype(BF16)
    out_ref[...] = inner_ref[...] + pick(got, onehot)


def plain_call(kernel, shapes, name, *args):
    vmem = pl.BlockSpec(memory_space=pltpu.VMEM)
    return pl.pallas_call(
        kernel,
        out_shape=shapes,
        in_specs=[vmem] * len(args),
        out_specs=jax.tree.map(lambda _: vmem, shapes),
        name=name,
    )(*args)


def column_fit(density, velocity, shear, press):
    upper = jnp.concatenate([velocity[1:, :], velocity[-1:, :]], axis=0)
    lower = jnp.concatenate([velocity[:1, :], velocity[:-1, :]], axis=0)
    rate = (upper - lower) / (2.0 * PITCH)
    inertial = rate * 1.0 / jnp.sqrt((press + FLOOR_LEVEL) / (density + FLOOR_LEVEL))
    friction = shear / (press + FLOOR_LEVEL)
    weight = density + FLOOR_LEVEL
    add = lambda v: jnp.sum(v, axis=0, keepdims=True)
    sum_zero = add(weight)
    sum_one = add(weight * inertial)
    sum_two = add(weight * inertial * inertial) + RIDGE_SHARE * sum_zero
    mix_zero = add(weight * friction)
    mix_one = add(weight * friction * inertial)
    determ = sum_zero * sum_two - sum_one * sum_one
    fitted = jnp.concatenate(
        [
            (mix_zero * sum_two - sum_one * mix_one) / determ,
            (sum_zero * mix_one - sum_one * mix_zero) / determ,
        ],
        axis=0,
    )
    return fitted, inertial


def exchange(low, high, axis):
    count = lax.axis_size(axis)
    if count == 1:
        return jnp.zeros_like(high), jnp.zeros_like(low)
    even = lax.axis_index(axis) % 2 == 0

    def swap(value, first):
        links = []
        for i in range(first, count - 1, 2):
            links += [(i, i + 1), (i + 1, i)]
        return lax.ppermute(value, axis, links)

    one = swap(jnp.where(even, high, low), 0)
    two = swap(jnp.where(even, low, high), 1) if count > 2 else jnp.zeros_like(low)
    return jnp.where(even, two, one), jnp.where(even, one, two)


def local(grains, pairs):
    place = jnp.stack(
        [lax.axis_index(a) == lax.axis_size(a) - 1 for a in ("gy", "gz")]
    ).astype(jnp.int32)
    own = box_sort(grains.reshape(7, NB, TILE), pairs.reshape(NB, 27), place)
    cube = own[:4].reshape(4, 2, 2, 8, TILE)
    below, above = exchange(cube[:, 0], cube[:, 1], "gz")
    cube = jnp.concatenate([below[:, None], cube, above[:, None]], axis=1)
    below, above = exchange(cube[:, :, 0], cube[:, :, 1], "gy")
    cube = jnp.concatenate([below[:, :, None], cube, above[:, :, None]], axis=2)
    below, above = exchange(cube[:, :, :, 0], cube[:, :, :, 7], "gx")
    side = jnp.stack([below, above]).reshape(2, 4, 16, TILE)
    wide = stress_and_deposit(cube.reshape(4, 128, TILE), side, own.reshape(7 * NB, TILE))
    left, right = exchange(wide[:, :128], wide[:, :128], "gx")
    block = jax.ShapeDtypeStruct((160, 128), F32)
    low, high, inner = plain_call(
        rim_x_kernel, [block, block, jax.ShapeDtypeStruct((160, COLS), F32)], "rim_x", wide, left, right
    )
    left, right = exchange(low, high, "gy")
    total = plain_call(
        rim_y_kernel, jax.ShapeDtypeStruct((160, COLS), F32), "rim_y", inner, left, right
    )
    fields = total[:80].reshape(10, 8, COLS)
    rim = total[80:].reshape(10, 8, COLS)
    from_below, from_above = exchange(rim[:, :4], rim[:, 4:], "gz")
    fields = fields + jnp.concatenate([from_below, from_above], axis=1)
    share = COLS // lax.axis_size("gz")
    start = lax.axis_index("gz") * share
    density = fields[0]
    velocity = fields[1] / (density + FLOOR_LEVEL)
    shear = fields[8]
    press = (fields[4] + fields[5] + fields[6]) / 3.0
    profile = jnp.stack([density, velocity, shear, press])
    whole = lax.all_gather(profile, "gz", axis=1, tiled=True)
    whole = lax.dynamic_slice_in_dim(whole, start, share, 2)
    fitted, inertial = column_fit(*whole)
    return (fields[None, None, None], fitted[None, None], inertial[None, None])


def solution(mesh):
    in_specs = (P("gx", "gy", "gz", None, None), P("gx", "gy", "gz", None, None))
    out_specs = (
        P("gx", "gy", "gz", None, None, None),
        P("gx", "gy", None, "gz"),
        P("gx", "gy", None, "gz"),
    )
    return jax.shard_map(local, mesh=mesh, in_specs=in_specs, out_specs=out_specs, check_vma=False)
```

time: 511 us -> 88.6 us (0.17)
  other arithmetic: 174 us -> 5.92 us
  local copies, waits for them, and re-layouts: 131 us -> 5.16 us
  loops' own time: 123 us -> 0 us
  Pallas kernels: 0 us -> 38.4 us
  starting transfers between devices: 30.8 us -> 13.1 us
  waiting for transfers between devices: 32.3 us -> 19.5 us
  matrix products: 9.09 us -> 0 us
    another operation x1 -> x0, loops' own time: 123 us -> none  [contact_tiles(): blocks = lax.map(one_tile, jnp.arange(tiles, dtype=jnp.int32))]
    reduce_sum x34 -> x2, other arithmetic: 92.4 us -> 0.06 us  [column_fit(): add = lambda v: jnp.sum(v, axis=0, keepdims=True)]
    dynamic_slice x96 -> x0, local copies, waits for them, and re-layouts: 62.9 us -> none  [the longest x32 41.9 us: one_tile(): own_place = own_idx[slot]]
    ge x32 -> x0, other arithmetic: 42.3 us -> none  [one_tile(): is_valid = partner_ids >= 0]
    pallas_call x0 -> x4, Pallas kernels: none -> 38.4 us  [the longest x1 32.6 us: stress_and_deposit(): pl.pallas_call(stress_kernel, out_shape=jax.ShapeDtypeStruct((160, 128 +...]
    select_n x64 -> x11, other arithmetic: 22.3 us -> 2.4 us  [the longest x6 1.39 us: exchange(): return (jnp.where(even, two, one), jnp.where(even, one, two))]
    gather x32 -> x0, local copies, waits for them, and re-layouts: 19.3 us -> none  [one_tile(): others = table[safe_ids].transpose(1, 0, 2).reshape(4, hood_count * TILE)]
    dynamic_update_slice x32 -> x0, local copies, waits for them, and re-layouts: 19.2 us -> none  [contact_tiles(): blocks = lax.map(one_tile, jnp.arange(tiles, dtype=jnp.int32))]
  transfers between devices with their start and end apart: 12 -> 10, of which waited for: 10 -> 8; matrix products, arithmetic and copies ran while one was open for 3% -> 1% of each run, Pallas kernels for 0% -> 0%
where the time goes in v1:
time: 88.6 us; the launch traced here: 87.6 us
  Pallas kernels  38.4 us (43%)
  waiting for transfers between devices  19.5 us (22%)
  starting transfers between devices  13.1 us (15%)
  other arithmetic  5.92 us (7%)
  local copies, waits for them, and re-layouts  5.16 us (6%)
  blocking collectives  4.58 us (5%)
    pallas_call x1, Pallas kernels, stress_and_deposit(): pl.pallas_call(stress_kernel, out_shape=jax.ShapeDtypeStruct((160, 128 +...  32.6 us
    ppermute x10, waiting for transfers between devices, swap(): return lax.ppermute(value, axis, links)  19.5 us
    ppermute x10, starting transfers between devices, swap(): return lax.ppermute(value, axis, links)  13.1 us
    all_gather x1, blocking collectives, local(): whole = lax.all_gather(profile, 'gz', axis=1, tiled=True)  4.58 us
    pallas_call x2, Pallas kernels, plain_call(): pl.pallas_call(kernel, out_shape=shapes, in_specs=[vmem] * len(args), out...  3.99 us
    pallas_call x1, Pallas kernels, box_sort(): pl.pallas_call(sort_kernel, out_shape=jax.ShapeDtypeStruct((7, NB, TILE),...  1.88 us
  transfers between devices with their start and end apart: 10, of which 8 were waited for; matrix products, arithmetic and copies ran while one was open for 1% of the time, Pallas kernels for 0%

profile of v1, /device:TPU:10, one launch (start us, length us, event | category | flops | bytes accessed | tf_op | source)
XLA Modules:
  0.0 87.6 jit_solution(18100733236390716668)
XLA Ops:
  0.7 0.7 copy-done.1
  1.3 0.7 copy.5
  2.0 0.6 add_convert_fusion.place_ref
  2.7 1.9 %box_sort.1 = f32[7,32,128]{2,1,0:T(8,128)} custom-call(s32[2]{0:T(128)} %add_convert_fusion.place_ref, f32[7,32,128]{2,1,0:T(8,128)} %bitcast.144, s32[32,27]{1,0:T(8,128)} %bitcast.147), custom_call_target="tpu_custom_call" | custom-call | tf_op jit(solution)/shard_map/box_sort/pallas_call | solution.py:87
  4.5 0.8 slice.109
  5.4 1.6 %collective-permute-start = (f32[4,2,8,128]{3,0,2,1:T(4,128)S(1)}, f32[4,2,8,128]{3,0,2,1:T(4,128)S(1)}, u32[]{:S(2)}, u32[]{:S(2)}) collective-permute-start(f32[4,2,8,128]{3,0,2,1:T(4,128)S(1)} %fusion), channel_id=1, source_target_pairs={{0,1},{1,0},{2,3},{3,2},{4,5},{5,4},{6,7},{7,6},{8,9},{9,8},{10,11... | collective-permute-start | bytes 98312 | tf_op jit(solution)/shard_map/ppermute | solution.py:423
  7.1 2.3 %collective-permute-done = f32[4,2,8,128]{3,0,2,1:T(4,128)S(1)} collective-permute-done((f32[4,2,8,128]{3,0,2,1:T(4,128)S(1)}, f32[4,2,8,128]{3,0,2,1:T(4,128)S(1)}, u32[]{:S(2)}, u32[]{:S(2)}) %collective-permute-start) | collective-permute-done | bytes 32800 | tf_op jit(solution)/shard_map/ppermute | solution.py:423
  9.5 3.5 %collective-permute-start.1 = (f32[4,4,8,128]{3,1,0,2:T(4,128)S(1)}, f32[4,4,8,128]{3,1,0,2:T(4,128)S(1)}, u32[]{:S(2)}, u32[]{:S(2)}) collective-permute-start(f32[4,4,8,128]{3,1,0,2:T(4,128)S(1)} %get-tuple-element.23), channel_id=1, source_target_pairs={{2,4},{4,2},{3,5},{5,3},{10,12},{12,10},{11,13},{13,11},{18,20},{2... | collective-permute-start | bytes 196616 | tf_op jit(solution)/shard_map/ppermute | solution.py:423
  13.2 2.5 %collective-permute-done.1 = f32[4,4,8,128]{3,1,0,2:T(4,128)S(1)} collective-permute-done((f32[4,4,8,128]{3,1,0,2:T(4,128)S(1)}, f32[4,4,8,128]{3,1,0,2:T(4,128)S(1)}, u32[]{:S(2)}, u32[]{:S(2)}) %collective-permute-start.1) | collective-permute-done | bytes 65568 | tf_op jit(solution)/shard_map/ppermute | solution.py:423
  15.7 1.7 %collective-permute-done.2 = f32[4,4,8,128]{3,1,0,2:T(4,128)S(1)} collective-permute-done((f32[4,4,8,128]{3,1,0,2:T(4,128)S(1)}, f32[4,4,8,128]{3,1,0,2:T(4,128)S(1)}, u32[]{:S(2)}, u32[]{:S(2)}) %collective-permute-start.2) | collective-permute-done | bytes 65568 | tf_op jit(solution)/shard_map/ppermute | solution.py:423
  17.6 1.9 %collective-permute-start.3 = (f32[4,4,4,128]{3,2,1,0:T(4,128)S(1)}, f32[4,4,4,128]{3,2,1,0:T(4,128)S(1)}, u32[]{:S(2)}, u32[]{:S(2)}) collective-permute-start(f32[4,4,4,128]{3,2,1,0:T(4,128)S(1)} %get-tuple-element.13), channel_id=1, source_target_pairs={{8,16},{16,8},{9,17},{17,9},{10,18},{18,10},{11,19},{19,11},{12,20... | collective-permute-start | bytes 98312 | tf_op jit(solution)/shard_map/ppermute | solution.py:423
  19.6 0.9 copy.12
  20.5 2.4 %collective-permute-done.3 = f32[4,4,4,128]{3,2,1,0:T(4,128)S(1)} collective-permute-done((f32[4,4,4,128]{3,2,1,0:T(4,128)S(1)}, f32[4,4,4,128]{3,2,1,0:T(4,128)S(1)}, u32[]{:S(2)}, u32[]{:S(2)}) %collective-permute-start.3) | collective-permute-done | bytes 32800 | tf_op jit(solution)/shard_map/ppermute | solution.py:423
  22.8 0.6 pad_maximum_fusion.2.side_ref
  23.5 32.6 %stress_deposit.1.wide_ref = f32[160,640]{1,0:T(8,128)} custom-call(f32[4,128,128]{2,1,0:T(8,128)} %bitcast.132, f32[2,4,16,128]{3,2,1,0:T(8,128)} %pad_maximum_fusion.2.side_ref, f32[224,128]{1,0:T(8,128)} %bitcast.133), custom_call_target="tpu_custom_call" | custom-call | tf_op jit(solution)/shard_map/stress_deposit/pallas_call | solution.py:339
  56.0 0.9 %slice.116 = f32[160,128]{1,0:T(8,128)S(1)} slice(f32[160,640]{1,0:T(8,128)} %stress_deposit.1.wide_ref), slice={[0:160], [0:128]} | slice | bytes 163840 | tf_op jit(solution)/shard_map/slice | solution.py:443
  56.9 1.9 %collective-permute-start.5 = (f32[160,128]{1,0:T(8,128)S(1)}, f32[160,128]{1,0:T(8,128)S(1)}, u32[]{:S(2)}, u32[]{:S(2)}) collective-permute-start(f32[160,128]{1,0:T(8,128)S(1)} %slice.116), channel_id=1, source_target_pairs={{8,16},{16,8},{9,17},{17,9},{10,18},{18,10},{11,19},{19,11},{12,20... | collective-permute-start | bytes 245768 | tf_op jit(solution)/shard_map/ppermute | solution.py:423
  58.9 3.8 %collective-permute-done.5 = f32[160,128]{1,0:T(8,128)S(1)} collective-permute-done((f32[160,128]{1,0:T(8,128)S(1)}, f32[160,128]{1,0:T(8,128)S(1)}, u32[]{:S(2)}, u32[]{:S(2)}) %collective-permute-start.5) | collective-permute-done | bytes 81952 | tf_op jit(solution)/shard_map/ppermute | solution.py:423
  62.7 0.7 broadcast_select_fusion.4
  63.4 2.1 %rim_x.1 = (f32[160,128]{1,0:T(8,128)}, f32[160,128]{1,0:T(8,128)}, f32[160,256]{1,0:T(8,128)}) custom-call(f32[160,640]{1,0:T(8,128)} %stress_deposit.1.wide_ref, f32[160,128]{1,0:T(8,128)} %get-tuple-element.20.left_ref, f32[160,128]{1,0:T(8,128)} %get-tuple-element.19.right_ref), custom_call_target="tpu_custom_call" | custom-call | tf_op jit(solution)/shard_map/rim_x/pallas_call | solution.py:380
  65.4 0.9 %broadcast_select_fusion.2 = (f32[160,128]{1,0:T(8,128)S(1)}, f32[160,128]{1,0:T(8,128)S(1)}) fusion(f32[160,128]{1,0:T(8,128)} %get-tuple-element.8, f32[160,128]{1,0:T(8,128)} %get-tuple-element.7, pred[]{:T(512)S(6)} %eq.25), kind=kLoop, calls=%fused_computation.11 | loop fusion | flops 40960 | bytes 327681 | tf_op jit(solution)/shard_map/jit(_where)/select_n | solution.py:425
  66.4 2.4 %collective-permute-start.7 = (f32[160,128]{1,0:T(8,128)S(1)}, f32[160,128]{1,0:T(8,128)S(1)}, u32[]{:S(2)}, u32[]{:S(2)}) collective-permute-start(f32[160,128]{1,0:T(8,128)S(1)} %get-tuple-element.18), channel_id=1, source_target_pairs={{2,4},{4,2},{3,5},{5,3},{10,12},{12,10},{11,13},{13,11},{18,20},{2... | collective-permute-start | bytes 245768 | tf_op jit(solution)/shard_map/ppermute | solution.py:423
  68.8 3.9 %collective-permute-done.7 = f32[160,128]{1,0:T(8,128)S(1)} collective-permute-done((f32[160,128]{1,0:T(8,128)S(1)}, f32[160,128]{1,0:T(8,128)S(1)}, u32[]{:S(2)}, u32[]{:S(2)}) %collective-permute-start.7) | collective-permute-done | bytes 81952 | tf_op jit(solution)/shard_map/ppermute | solution.py:423
  73.2 0.7 broadcast_select_fusion
  73.9 1.9 %rim_y.1 = f32[160,256]{1,0:T(8,128)} custom-call(f32[160,256]{1,0:T(8,128)} %get-tuple-element.6.inner_ref, f32[160,128]{1,0:T(8,128)} %get-tuple-element.16.left_ref, f32[160,128]{1,0:T(8,128)} %get-tuple-element.15.right_ref), custom_call_target="tpu_custom_call" | custom-call | tf_op jit(solution)/shard_map/rim_y/pallas_call | solution.py:380
  75.8 0.9 %slice_bitcast_fusion = f32[10,8,256]{2,1,0:T(8,128)S(1)} fusion(f32[160,256]{1,0:T(8,128)} %rim_y.1), kind=kLoop, calls=%fused_computation.2 | loop fusion | bytes 163840 | tf_op jit(solution)/shard_map/reshape | solution.py:453
  76.7 1.6 %collective-permute-start.9 = (f32[10,4,256]{2,1,0:T(4,128)S(1)}, f32[10,4,256]{2,1,0:T(4,128)S(1)}, u32[]{:S(2)}, u32[]{:S(2)}) collective-permute-start(f32[10,4,256]{2,1,0:T(4,128)S(1)} %slice_select_fusion), channel_id=1, source_target_pairs={{0,1},{1,0},{2,3},{3,2},{4,5},{5,4},{6,7},{7,6},{8,9},{9,8},{10,11... | collective-permute-start | bytes 122888 | tf_op jit(solution)/shard_map/ppermute | solution.py:423
  78.3 2.5 %collective-permute-done.9 = f32[10,4,256]{2,1,0:T(4,128)S(1)} collective-permute-done((f32[10,4,256]{2,1,0:T(4,128)S(1)}, f32[10,4,256]{2,1,0:T(4,128)S(1)}, u32[]{:S(2)}, u32[]{:S(2)}) %collective-permute-start.9) | collective-permute-done | bytes 40992 | tf_op jit(solution)/shard_map/ppermute | solution.py:423
  80.9 4.6 %all_gather.3 = f32[4,16,256]{2,1,0:T(8,128)S(1)} all-gather(f32[4,8,256]{2,1,0:T(8,128)S(1)} %pad_maximum_fusion.3), channel_id=1, replica_groups=mesh['gx'=4,'gy'=4,'gz'=2] {'gz'}, dimensions={1}, use_global_device_ids=true | all-gather | bytes 98304 | tf_op jit(solution)/shard_map/all_gather | solution.py:463
  85.7 0.6 maximum_bitcast_fusion
  86.3 0.7 maximum_add_fusion
  87.0 0.6 fusion.7
  (32 shorter events, 1.7 us)
Async XLA Ops:
  0.6 0.7 copy-start.1
  5.4 4.0 %collective-permute-start = (f32[4,2,8,128]{3,0,2,1:T(4,128)S(1)}, f32[4,2,8,128]{3,0,2,1:T(4,128)S(1)}, u32[]{:S(2)}, u32[]{:S(2)}) collective-permute-start(f32[4,2,8,128]{3,0,2,1:T(4,128)S(1)} %fusion), channel_id=1, source_target_pairs={{0,1},{1,0},{2,3},{3,2},{4,5},{5,4},{6,7},{7,6},{8,9},{9,8},{10,11... | collective-permute-start | bytes 98312 | tf_op jit(solution)/shard_map/ppermute | solution.py:423
  9.5 6.2 %collective-permute-start.1 = (f32[4,4,8,128]{3,1,0,2:T(4,128)S(1)}, f32[4,4,8,128]{3,1,0,2:T(4,128)S(1)}, u32[]{:S(2)}, u32[]{:S(2)}) collective-permute-start(f32[4,4,8,128]{3,1,0,2:T(4,128)S(1)} %get-tuple-element.23), channel_id=1, source_target_pairs={{2,4},{4,2},{3,5},{5,3},{10,12},{12,10},{11,13},{13,11},{18,20},{2... | collective-permute-start | bytes 196616 | tf_op jit(solution)/shard_map/ppermute | solution.py:423
  13.0 4.3 %collective-permute-start.2 = (f32[4,4,8,128]{3,1,0,2:T(4,128)S(1)}, f32[4,4,8,128]{3,1,0,2:T(4,128)S(1)}, u32[]{:S(2)}, u32[]{:S(2)}) collective-permute-start(f32[4,4,8,128]{3,1,0,2:T(4,128)S(1)} %get-tuple-element.24), channel_id=1, source_target_pairs={{0,2},{2,0},{4,6},{6,4},{1,3},{3,1},{5,7},{7,5},{8,10},{10,8},{12,... | collective-permute-start | bytes 196616 | tf_op jit(solution)/shard_map/ppermute | solution.py:423
  17.6 5.2 %collective-permute-start.3 = (f32[4,4,4,128]{3,2,1,0:T(4,128)S(1)}, f32[4,4,4,128]{3,2,1,0:T(4,128)S(1)}, u32[]{:S(2)}, u32[]{:S(2)}) collective-permute-start(f32[4,4,4,128]{3,2,1,0:T(4,128)S(1)} %get-tuple-element.13), channel_id=1, source_target_pairs={{8,16},{16,8},{9,17},{17,9},{10,18},{18,10},{11,19},{19,11},{12,20... | collective-permute-start | bytes 98312 | tf_op jit(solution)/shard_map/ppermute | solution.py:423
  19.5 3.3 %collective-permute-start.4 = (f32[4,4,4,128]{3,2,1,0:T(4,128)S(1)}, f32[4,4,4,128]{3,2,1,0:T(4,128)S(1)}, u32[]{:S(2)}, u32[]{:S(2)}) collective-permute-start(f32[4,4,4,128]{3,2,1,0:T(4,128)S(1)} %get-tuple-element.14), channel_id=1, source_target_pairs={{0,8},{8,0},{16,24},{24,16},{1,9},{9,1},{17,25},{25,17},{2,10},{10... | collective-permute-start | bytes 98312 | tf_op jit(solution)/shard_map/ppermute | solution.py:423
  56.9 5.7 %collective-permute-start.5 = (f32[160,128]{1,0:T(8,128)S(1)}, f32[160,128]{1,0:T(8,128)S(1)}, u32[]{:S(2)}, u32[]{:S(2)}) collective-permute-start(f32[160,128]{1,0:T(8,128)S(1)} %slice.116), channel_id=1, source_target_pairs={{8,16},{16,8},{9,17},{17,9},{10,18},{18,10},{11,19},{19,11},{12,20... | collective-permute-start | bytes 245768 | tf_op jit(solution)/shard_map/ppermute | solution.py:423
  58.8 3.8 %collective-permute-start.6 = (f32[160,128]{1,0:T(8,128)S(1)}, f32[160,128]{1,0:T(8,128)S(1)}, u32[]{:S(2)}, u32[]{:S(2)}) collective-permute-start(f32[160,128]{1,0:T(8,128)S(1)} %slice.116), channel_id=1, source_target_pairs={{0,8},{8,0},{16,24},{24,16},{1,9},{9,1},{17,25},{25,17},{2,10},{10... | collective-permute-start | bytes 245768 | tf_op jit(solution)/shard_map/ppermute | solution.py:423
  66.4 6.3 %collective-permute-start.7 = (f32[160,128]{1,0:T(8,128)S(1)}, f32[160,128]{1,0:T(8,128)S(1)}, u32[]{:S(2)}, u32[]{:S(2)}) collective-permute-start(f32[160,128]{1,0:T(8,128)S(1)} %get-tuple-element.18), channel_id=1, source_target_pairs={{2,4},{4,2},{3,5},{5,3},{10,12},{12,10},{11,13},{13,11},{18,20},{2... | collective-permute-start | bytes 245768 | tf_op jit(solution)/shard_map/ppermute | solution.py:423
  68.7 4.5 %collective-permute-start.8 = (f32[160,128]{1,0:T(8,128)S(1)}, f32[160,128]{1,0:T(8,128)S(1)}, u32[]{:S(2)}, u32[]{:S(2)}) collective-permute-start(f32[160,128]{1,0:T(8,128)S(1)} %get-tuple-element.17), channel_id=1, source_target_pairs={{0,2},{2,0},{4,6},{6,4},{1,3},{3,1},{5,7},{7,5},{8,10},{10,8},{12,... | collective-permute-start | bytes 245768 | tf_op jit(solution)/shard_map/ppermute | solution.py:423
  76.7 4.1 %copy-start = (f32[160,256]{1,0:T(8,128)S(1)}, f32[160,256]{1,0:T(8,128)}, u32[]{:S(2)}) copy-start(f32[160,256]{1,0:T(8,128)} %rim_y.1) | copy-start | bytes 491524
  76.7 4.1 %collective-permute-start.9 = (f32[10,4,256]{2,1,0:T(4,128)S(1)}, f32[10,4,256]{2,1,0:T(4,128)S(1)}, u32[]{:S(2)}, u32[]{:S(2)}) collective-permute-start(f32[10,4,256]{2,1,0:T(4,128)S(1)} %slice_select_fusion), channel_id=1, source_target_pairs={{0,1},{1,0},{2,3},{3,2},{4,5},{5,4},{6,7},{7,6},{8,9},{9,8},{10,11... | collective-permute-start | bytes 122888 | tf_op jit(solution)/shard_map/ppermute | solution.py:423

commit v2 on v1

v2 whole, which is shorter than its diff:
```python
import math

import jax
import jax.numpy as jnp
from jax import lax
from jax.experimental import pallas as pl
from jax.experimental.pallas import tpu as pltpu
from jax.sharding import PartitionSpec as P

TILE = 128
BOXES_DOWNSLOPE = 8
BOXES_SPANWISE = 2
BOXES_NORMAL = 2
CELLS_PER_EDGE = 4

TILE_BOX_EDGE = 5.0
SPRING = 2.0
SOFTEN = 0.05
FLOOR_LEVEL = 0.1
RIDGE_SHARE = 0.1
CUT_LEVEL = math.exp(-12.5)
NORM_ONE = 1.0 / math.sqrt(2.0 * math.pi)

PITCH = TILE_BOX_EDGE / CELLS_PER_EDGE
REACH = 1.21
ABSENT = -10.0

NB = BOXES_DOWNSLOPE * BOXES_SPANWISE * BOXES_NORMAL
PITCH_ROWS = NB + 8
UNROLL = 4
COLS = CELLS_PER_EDGE * BOXES_DOWNSLOPE * CELLS_PER_EDGE * BOXES_SPANWISE
CAPS = (16, 12, 16, 12, 14)

F32 = jnp.float32
BF16 = jnp.bfloat16


def iota(shape, dim):
    return lax.broadcasted_iota(jnp.int32, shape, dim)


def split3(value):
    high = value.astype(BF16)
    rest = value - high.astype(F32)
    mid = rest.astype(BF16)
    low = (rest - mid.astype(F32)).astype(BF16)
    return high, mid, low


def pick(value, onehot):
    high, mid, low = split3(value)
    dot = lambda part: jnp.dot(part, onehot, preferred_element_type=F32)
    return (dot(low) + dot(mid)) + dot(high)


def is_last(axis):
    return lax.axis_index(axis) == lax.axis_size(axis) - 1


def is_even(axis):
    return lax.axis_index(axis) % 2 == 0


def sort_kernel(grains_ref, pairs_ref, own_ref, near_ref):
    pairs = pairs_ref[0, 0, 0]
    live = pairs >= 0
    hood = jnp.where(live, pairs, 0) >> 5
    third = (hood * 11) >> 5
    part_c = hood - 3 * third
    part_b = third - 3 * ((third * 11) >> 5)

    def has(part, value):
        hit = jnp.where(live & (part == value), 1.0, 0.0)
        return jnp.max(hit, axis=1, keepdims=True) > 0.5

    box_y = has(part_b, 2) | (is_last("gy") & jnp.logical_not(has(part_b, 0)))
    box_z = has(part_c, 2) | (is_last("gz") & jnp.logical_not(has(part_c, 0)))
    grains = grains_ref[0, 0, 0].reshape(7, NB, TILE)
    rows = [grains[r] for r in range(7)]
    centre = 0.5 * (jnp.min(rows[0], axis=1, keepdims=True) + jnp.max(rows[0], axis=1, keepdims=True))
    key = centre + jnp.where(box_y, 64.0, 0.0) + jnp.where(box_z, 128.0, 0.0)
    sub = iota((NB, TILE), 0)
    lane = iota((NB, TILE), 1)
    wide = jnp.broadcast_to(key, (NB, TILE))
    key_row = jnp.sum(jnp.where(sub == lane, wide, 0.0), axis=0, keepdims=True)
    before = (wide < key_row) | ((wide == key_row) & (sub < lane))
    rank = jnp.sum(jnp.where(before, 1.0, 0.0), axis=0, keepdims=True)
    onehot = jnp.where((rank == sub.astype(F32)) & (lane < NB), 1.0, 0.0).astype(BF16)[:, :NB]
    for r in range(7):
        high, mid, low = split3(rows[r])
        dot = lambda part: jnp.dot(onehot, part, preferred_element_type=F32)
        value = (dot(low) + dot(mid)) + dot(high)
        own_ref[r] = value
        if r < 4:
            near_ref[r] = value


def box_sort(grains, pairs):
    shape = lambda rows: jax.ShapeDtypeStruct((rows, NB, TILE), F32)
    return plain_call(sort_kernel, [shape(7), shape(4)], "box_sort", grains, pairs)


def lane_take(value, index):
    dims = lax.GatherDimensionNumbers(
        offset_dims=(),
        collapsed_slice_dims=(1,),
        start_index_map=(1,),
        operand_batching_dims=(0,),
        start_indices_batching_dims=(0,),
    )
    return lax.gather(
        value, index[..., None], dims, (1, 1), mode=lax.GatherScatterMode.PROMISE_IN_BOUNDS
    )


def pack(groups, tri):
    masks = [jnp.where(mask, 1.0, 0.0).astype(BF16) for lists in groups for mask, _ in lists]
    both = jnp.dot(jnp.concatenate(masks, axis=0), tri, preferred_element_type=F32)
    rows = masks[0].shape[0]
    lane_f = iota((rows, TILE), 1).astype(F32)
    packed, at = [], 0
    for lists in groups:
        offset = jnp.zeros((rows, TILE), F32)
        outs = [jnp.zeros((rows, TILE), F32)] * 3 + [jnp.full((rows, TILE), ABSENT, F32)]
        for _, arrays in lists:
            ranks, total = both[at : at + rows, :TILE], both[at : at + rows, TILE:]
            at += rows
            wanted = lane_f - offset
            place = jnp.zeros((rows, TILE), jnp.int32)
            for bit in (64, 32, 16, 8, 4, 2, 1):
                probe = lane_take(ranks, place + (bit - 1))
                place = jnp.where(probe <= wanted, place + bit, place)
            ours = (wanted >= 0.0) & (wanted < total)
            outs = [jnp.where(ours, lane_take(a, place), o) for a, o in zip(arrays, outs)]
            offset = offset + total
        packed.append((outs, offset))
    return packed


def pair_terms(own, cand, sums):
    own_x, own_y, own_z, own_r = own
    cand_x, cand_y, cand_z, cand_r = cand
    dx, dy, dz = own_x - cand_x, own_y - cand_y, own_z - cand_z
    square = dx * dx + dy * dy + dz * dz
    distance = square * lax.rsqrt(jnp.maximum(square, 1e-30))
    overlap = jnp.maximum(own_r + cand_r - distance, 0.0)
    below = distance + SOFTEN
    guess = pl.reciprocal(below, approx=True)
    force = (0.5 * SPRING) * overlap * (guess * (2.0 - below * guess))
    fx, fy, fz = force * dx, force * dy, force * dz
    terms = (fx * dx, fy * dy, fz * dz, fx * dy, fx * dz, fy * dz)
    return tuple(s + t for s, t in zip(sums, terms))


def stress_kernel(grid_ref, side_ref, grains_ref, rim0_ref, rim1_ref, out_ref, cand_ref, all_ref, contact_ref, plane_ref, height_ref,
    feature_ref, moment_ref, own_ref, sum_ref,
):
    tri_row = iota((TILE, 2 * TILE), 0)
    tri_col = iota((TILE, 2 * TILE), 1)
    tri = jnp.where((tri_row <= tri_col) | (tri_col >= TILE), 1.0, 0.0).astype(BF16)

    span_x = BOXES_DOWNSLOPE * TILE_BOX_EDGE
    span_y = BOXES_SPANWISE * TILE_BOX_EDGE
    span_z = BOXES_NORMAL * TILE_BOX_EDGE

    def shifts(place, span):
        return jnp.where(place == 0, -span, jnp.where(place == 3, span, 0.0))

    def alive(radius):
        return jnp.where(radius == 0.0, ABSENT, radius)

    row = iota((128, TILE), 0)
    low_x = TILE_BOX_EDGE * (row & 7).astype(F32)
    low_y = TILE_BOX_EDGE * ((iota((64, TILE), 0) >> 3) & 1).astype(F32)
    low_z = TILE_BOX_EDGE * (iota((32, TILE), 0) >> 4).astype(F32)
    here = [
        grid_ref[0],
        grid_ref[1] + shifts((row >> 3) & 3, span_y),
        grid_ref[2] + shifts(row >> 5, span_z),
        alive(grid_ref[3]),
    ]
    side_row = iota((16, TILE), 0)
    sides = []
    for k, shift_x in ((0, -span_x), (1, span_x)):
        sides.append(
            [
                side_ref[k, 0] + shift_x,
                side_ref[k, 1] + shifts(side_row & 3, span_y),
                side_ref[k, 2] + shifts(side_row >> 2, span_z),
                alive(side_ref[k, 3]),
            ]
        )
    in_box_x = iota((16, 8, TILE), 1)

    def neighbours(centre, edge, step):
        cube = centre.reshape(16, 8, TILE)
        moved = pltpu.roll(cube, 1 if step < 0 else 7, 1)
        at_edge = in_box_x == (0 if step < 0 else 7)
        return jnp.where(at_edge, edge[:, None, :], moved).reshape(128, TILE)

    def near(arrays, axis, low, step):
        limit = arrays[axis] >= low - REACH if step < 0 else arrays[axis] <= low + (TILE_BOX_EDGE + REACH)
        return limit & (arrays[3] > 0.0), arrays

    def cut_y(arrays, start):
        return [a.reshape(4, 4, 8, TILE)[:, start : start + 2].reshape(64, TILE) for a in arrays]

    def cut_z(arrays, start):
        return [a[16 * start : 16 * start + 32] for a in arrays]

    before = [neighbours(c, e, -1) for c, e in zip(here, sides[0])]
    after = [neighbours(c, e, 1) for c, e in zip(here, sides[1])]
    ((beside_x, count_x),) = pack([[near(before, 0, low_x, -1), near(after, 0, low_x, 1)]], tri)
    ((beside_y, count_y),) = pack(
        [
            [
                near(cut_y(here, 0), 1, low_y, -1),
                near(cut_y(beside_x, 0), 1, low_y, -1),
                near(cut_y(here, 2), 1, low_y, 1),
                near(cut_y(beside_x, 2), 1, low_y, 1),
            ]
        ],
        tri,
    )
    mid, mid_x = cut_y(here, 1), cut_y(beside_x, 1)
    (above, count_z), (above_rest, count_w) = pack(
        [
            [near(cut_z(mid, 0), 2, low_z, -1), near(cut_z(mid, 2), 2, low_z, 1)],
            [
                near(cut_z(mid_x, 0), 2, low_z, -1),
                near(cut_z(beside_y, 0), 2, low_z, -1),
                near(cut_z(mid_x, 2), 2, low_z, 1),
                near(cut_z(beside_y, 2), 2, low_z, 1),
            ],
        ],
        tri,
    )
    worst = [
        jnp.max(count, axis=0, keepdims=True) - 8.0 * cap
        for count, cap in zip((count_x, count_y, count_z, count_w), CAPS[1:])
    ]

    def keep(ref, first, values):
        for f, value in enumerate(values):
            at = (first + f) * PITCH_ROWS
            ref[at : at + NB, :] = value

    half_box = 0.5 * TILE_BOX_EDGE
    ones = jnp.ones((NB, TILE), F32)
    none = jnp.zeros((NB, TILE), F32)

    def parts(value):
        return [p.astype(F32) for p in split3(value)]

    middle = [
        TILE_BOX_EDGE * (iota((NB, TILE), 0) & 7).astype(F32) + half_box,
        TILE_BOX_EDGE * ((iota((NB, TILE), 0) >> 3) & 1).astype(F32) + half_box,
        low_z + half_box,
    ]
    for k, chunk in enumerate((cut_z(mid, 1), cut_z(mid_x, 1), cut_z(beside_y, 1), above, above_rest)):
        x, y, z = (chunk[c] - middle[c] for c in range(3))
        squares = [x * x, y * y, z * z]
        norm = squares[0] + squares[1] + squares[2]
        xs, ys, zs, ns, rs = (parts(v) for v in (x, y, z, norm, chunk[3]))
        keep(
            feature_ref, 16 * k,
            [xs[0], ys[0], zs[0], xs[1], ys[1], zs[1], ones, ns[0]]
            + [xs[2], ys[2], zs[2], ns[1], ns[2]] + rs,
        )
        products = squares + [x * y, x * z, y * z]
        highs = [v.astype(BF16).astype(F32) for v in products]
        lows = [v - h for v, h in zip(products, highs)]
        keep(moment_ref, 16 * k, highs + [none] * 2 + lows + [none] * 2)
        if k == 0:
            for c in range(4):
                cand_ref[c * NB : c * NB + NB, :] = chunk[c]
            xi, yi, zi = ([-2.0 * p for p in v] for v in (xs, ys, zs))
            keep(
                own_ref, 0,
                [xi[0], yi[0], zi[0], xi[0], yi[0], zi[0], ns[0], ones]
                + [xi[0], yi[0], zi[0], ones, ones] + [none] * 3
                + [xi[1], yi[1], zi[1], xi[1], yi[1], zi[1], ns[1], none]
                + [xi[2], yi[2], zi[2], none, none, none, ns[2], none]
                + rs + [x, y, z],
            )
    overflow = worst[0]
    for w in worst[1:]:
        overflow = jnp.maximum(overflow, w)
    overflow = jnp.max(overflow)

    nx = CELLS_PER_EDGE * (BOXES_DOWNSLOPE + 2)
    ny = CELLS_PER_EDGE * (BOXES_SPANWISE + 2)

    def weights(coords, centres):
        diff = coords - centres
        return jnp.maximum(jnp.exp(-0.5 * diff * diff) - CUT_LEVEL, 0.0) * NORM_ONE

    def centres(places):
        return (places.astype(F32) - CELLS_PER_EDGE + 0.5) * PITCH

    at_z = iota((8, TILE), 0)
    centres_inner = centres(at_z + 4)
    centres_rim = centres(jnp.where(at_z < 4, at_z, at_z + 8))

    def put_plane(t):
        wx = weights(grains_ref[pl.ds(t, 1), :], centres(iota((nx, TILE), 0)))
        wy = weights(grains_ref[pl.ds(NB + t, 1), :], centres(iota((ny, TILE), 0)))
        parts = [wx[x : x + 1] * wy for x in list(range(4)) + list(range(nx - 4, nx))]
        inner_x = wx[4 : nx - 4]
        parts += [inner_x * wy[y : y + 1] for y in list(range(4)) + list(range(ny - 4, ny))]
        inner_y = wy[4 : ny - 4]
        parts += [wx[x : x + 1] * inner_y for x in range(4, nx - 4)]
        lanes = pl.ds(pl.multiple_of(t * TILE, TILE), TILE)
        plane_ref[:, lanes] = jnp.concatenate(parts, axis=0).astype(BF16)

    def put_height(t):
        rows = [grains_ref[pl.ds(r * NB + t, 1), :] for r in range(2, 7)]
        wz_inner = weights(rows[0], centres_inner)
        wz_rim = weights(rows[0], centres_rim)
        masses = 4.0 * math.pi / 3.0 * rows[1] * rows[1] * rows[1]
        vel = rows[2:]
        cont = [contact_ref[pl.ds(k * NB + t, 1), :] for k in range(6)]
        loads = [masses, masses * vel[0], masses * vel[1], masses * vel[2]]
        for k, (i, j) in enumerate(((0, 0), (1, 1), (2, 2), (0, 1), (0, 2), (1, 2))):
            loads.append(cont[k] + masses * (vel[i] * vel[j]))
        height = [load * wz_inner for load in loads] + [load * wz_rim for load in loads]
        lanes = pl.ds(pl.multiple_of(t * TILE, TILE), TILE)
        height_ref[:, lanes] = jnp.concatenate(height, axis=0).astype(BF16)

    def own_rows(t):
        return tuple(
            jnp.broadcast_to(cand_ref[pl.ds(c * NB + t, 1), :], (8, TILE)) for c in range(4)
        )

    def group(columns, first, g):
        return tuple(
            jnp.broadcast_to(columns[8 * g : 8 * g + 8, first + c : first + c + 1], (8, TILE)) for c in range(4)
        )

    def put(t, sums):
        for k in range(6):
            contact_ref[pl.ds(k * NB + t, 1), :] = jnp.sum(sums[k], axis=0, keepdims=True)

    zeros = tuple(jnp.zeros((8, TILE), F32) for _ in range(6))

    @pl.when(overflow <= 0.0)
    def _():
        sub = iota((8, TILE), 0)

        def one_tile(t, carry):
            put_plane(t)
            radii = [own_ref[pl.ds((32 + p) * PITCH_ROWS + t, 1), :] for p in range(3)]
            radii = [jnp.where(sub == 6, jnp.broadcast_to(r, (8, TILE)), 0.0) for r in radii]
            reach = [radii[0], jnp.where(sub >= 5, 1.0, 0.0), radii[1], radii[2]]
            rhs = jnp.concatenate(
                [own_ref[pl.ds(t, 32, stride=PITCH_ROWS), :], jnp.concatenate(reach, axis=0)], axis=1
            ).astype(BF16)
            highs, lows, moments = [], [], []
            for k in range(5):
                rows = feature_ref[pl.ds(16 * k * PITCH_ROWS + t, 16, stride=PITCH_ROWS), :]
                first = rows[:8]
                lhs = jnp.concatenate([rows, first, first], axis=0).T.astype(BF16)
                both = jnp.dot(lhs[: 8 * CAPS[k]], rhs, preferred_element_type=F32)
                square = jnp.maximum(both[:, :TILE], 1e-12)
                distance = square * lax.rsqrt(square)
                overlap = jnp.maximum(both[:, TILE:] - distance, 0.0)
                below = distance + SOFTEN
                guess = pl.reciprocal(below, approx=True)
                force = overlap * (guess * (2.0 - below * guess))
                if k == 0:
                    at = iota((TILE, TILE), 0) == iota((TILE, TILE), 1)
                    force = jnp.where(at, 0.0, force)
                high = force.astype(BF16)
                low = (force - high.astype(F32)).astype(BF16)
                rest = TILE - 8 * CAPS[k]
                highs.append(high)
                lows.append(low)
                if rest:
                    highs.append(jnp.zeros((rest, TILE), BF16))
                    lows.append(jnp.zeros((rest, TILE), BF16))
                more = moment_ref[pl.ds(16 * k * PITCH_ROWS + t, 16, stride=PITCH_ROWS), :]
                moments.append(jnp.concatenate([first, more, first], axis=0))
            lhs = jnp.concatenate(moments, axis=1).astype(BF16)
            one = jnp.dot(lhs, jnp.concatenate(highs, axis=0), preferred_element_type=F32)
            two = jnp.dot(lhs[:16], jnp.concatenate(lows, axis=0), preferred_element_type=F32)
            sum_ref[pl.ds(t, 8, stride=PITCH_ROWS), :] = one[:8] + two[:8]
            sum_ref[pl.ds(8 * PITCH_ROWS + t, 8, stride=PITCH_ROWS), :] = one[8:16] + (one[16:24] + two[8:])
            return carry

        def some_tiles(q, carry):
            for i in range(UNROLL):
                one_tile(UNROLL * q + i, carry)
            return carry

        lax.fori_loop(0, NB // UNROLL, some_tiles, 0)
        total = [sum_ref[m * PITCH_ROWS : m * PITCH_ROWS + NB, :] for m in range(14)]
        first = [total[c] + total[3 + c] for c in range(3)]
        own_mid = [own_ref[(35 + c) * PITCH_ROWS : (35 + c) * PITCH_ROWS + NB, :] for c in range(3)]
        for k, (i, j) in enumerate(((0, 0), (1, 1), (2, 2), (0, 1), (0, 2), (1, 2))):
            a, b = own_mid[i], own_mid[j]
            contact_ref[k * NB : (k + 1) * NB, :] = (0.5 * SPRING) * (
                total[8 + k] - (a * first[j] + b * first[i]) + a * b * total[6]
            )

    @pl.when(overflow > 0.0)
    def _():
        stride = 16 * 8 + 32
        for c in range(4):
            all_ref[c * stride : c * stride + 128, :] = here[c]
            all_ref[c * stride + 128 : c * stride + 144, :] = sides[0][c]
            all_ref[c * stride + 144 : c * stride + 160, :] = sides[1][c]
        all_ref[4 * stride : 8 * stride, :] = jnp.zeros((4 * stride, TILE), F32)

        def one_tile(t, carry):
            own = own_rows(t)
            tile_x, tile_y, tile_z = t & 7, (t >> 3) & 1, t >> 4

            def one_near(n, sums):
                n_x = n // 9
                n_y = (n - 9 * n_x) // 3
                n_z = n - 9 * n_x - 3 * n_y
                at_x = tile_x + n_x - 1
                plane = 4 * (tile_z + n_z) + tile_y + n_y
                place = jnp.where(
                    at_x < 0, 128 + plane, jnp.where(at_x > 7, 144 + plane, 8 * plane + at_x)
                )
                columns = all_ref[pl.ds(place, 8, stride=stride), :].T
                for g in range(16):
                    sums = pair_terms(own, group(columns, 0, g), sums)
                return sums

            put(t, lax.fori_loop(0, 27, one_near, zeros))
            put_plane(t)
            return carry

        lax.fori_loop(0, NB, one_tile, 0)

    def four_heights(q, carry):
        for i in range(4):
            put_height(4 * q + i)
        return carry

    lax.fori_loop(0, NB // 4, four_heights, 0)
    wide = lax.dot_general(
        height_ref[...], plane_ref[...], (((1,), (1,)), ((), ())), preferred_element_type=F32
    )
    out_ref[...] = wide[:, TILE:]
    rim = wide[:, :TILE]
    rim = jnp.where(is_even("gx"), pltpu.roll(rim, 64, 1), rim)
    upper, lower = rim[:80], rim[80:]
    left_half = iota((80, TILE), 1) < 64
    rim0_ref[...] = jnp.where(left_half, upper, pltpu.roll(lower, 64, 1))
    rim1_ref[...] = jnp.where(left_half, pltpu.roll(upper, 64, 1), lower)


def stress_and_deposit(grid, side, grains):
    vmem = pl.BlockSpec(memory_space=pltpu.VMEM)
    return pl.pallas_call(
        stress_kernel,
        out_shape=[
            jax.ShapeDtypeStruct((80, TILE), F32),
            jax.ShapeDtypeStruct((80, TILE), F32),
            jax.ShapeDtypeStruct((160, 2 * TILE + COLS), F32),
        ],
        in_specs=[vmem, vmem, vmem],
        out_specs=[vmem, vmem, vmem],
        scratch_shapes=[
            pltpu.VMEM((4 * NB, TILE), F32),
            pltpu.VMEM((8 * 160, TILE), F32),
            pltpu.VMEM((6 * NB, TILE), F32),
            pltpu.VMEM((128 + 2 * 128 + COLS, NB * TILE), BF16),
            pltpu.VMEM((160, NB * TILE), BF16),
            pltpu.VMEM((5 * 16 * PITCH_ROWS, TILE), F32),
            pltpu.VMEM((5 * 16 * PITCH_ROWS, TILE), F32),
            pltpu.VMEM((38 * PITCH_ROWS, TILE), F32),
            pltpu.VMEM((16 * PITCH_ROWS, TILE), F32),
        ],
        name="stress_deposit",
    )(grid, side, grains)


def rim_x_kernel(wide_ref, first_ref, second_ref, rim0_ref, rim1_ref, inner_ref):
    even = is_even("gx")
    right = jnp.where(even, first_ref[...], second_ref[...])
    left = jnp.where(even, second_ref[...], first_ref[...])
    left_half = iota((80, TILE), 1) < 64
    got = jnp.concatenate(
        [
            jnp.where(left_half, right, pltpu.roll(left, 64, 1)),
            jnp.where(left_half, pltpu.roll(right, 64, 1), left),
        ],
        axis=0,
    )
    src = iota((TILE, 1), 0)
    x = (src >> 4) & 3
    x = jnp.where(src >= 64, x, x + (CELLS_PER_EDGE * BOXES_DOWNSLOPE - 4))
    y = src & 15
    target = jnp.where(y < 4, y * 32 + x, jnp.where(y >= 12, 128 + (y - 12) * 32 + x, 256 + x * 8 + y - 4))
    onehot = jnp.where(iota((TILE, 512), 1) == target, 1.0, 0.0).astype(BF16)
    total = wide_ref[...] + pick(got, onehot)
    low, high = total[:, :TILE], total[:, TILE : 2 * TILE]
    even = is_even("gy")
    rim0_ref[...] = jnp.where(even, high, low)
    rim1_ref[...] = jnp.where(even, low, high)
    inner_ref[...] = total[:, 2 * TILE :]


def add_rim_y(inner_ref, first_ref, second_ref):
    even = is_even("gy")
    right = jnp.where(even, first_ref[...], second_ref[...])
    left = jnp.where(even, second_ref[...], first_ref[...])
    got = jnp.concatenate([left, right], axis=1)
    src = iota((256, 1), 0)
    target = (src & 31) * 8 + 4 * (src >> 7) + ((src >> 5) & 3)
    onehot = jnp.where(iota((256, 256), 1) == target, 1.0, 0.0).astype(BF16)
    return inner_ref[...] + pick(got, onehot)


def rim_y_kernel(inner_ref, first_ref, second_ref, out_ref):
    out_ref[...] = add_rim_y(inner_ref, first_ref, second_ref)


PROFILED = (0, 1, 4, 5, 6, 8)


def rim_y_two_kernel(inner_ref, first_ref, second_ref, out_ref, send_ref):
    total = add_rim_y(inner_ref, first_ref, second_ref)
    out_ref[...] = total
    lower = lax.axis_index("gz") == 0
    top = iota((8, COLS), 0) < 4
    for p in range(5):
        one = total[80 + 16 * p : 88 + 16 * p]
        two = total[88 + 16 * p : 96 + 16 * p]
        to_upper = jnp.where(top, pltpu.roll(one, 4, 0), two)
        to_lower = jnp.where(top, one, pltpu.roll(two, 4, 0))
        both = jnp.where(lower, to_upper, to_lower)
        send_ref[8 * p : 8 * p + 8, :] = both[:, :TILE]
        send_ref[40 + 8 * p : 48 + 8 * p, :] = both[:, TILE:]
    for i, c in enumerate(PROFILED):
        rows = total[8 * c : 8 * c + 8]
        send_ref[80 + 8 * i : 88 + 8 * i, :] = jnp.where(lower, rows[:, TILE:], rows[:, :TILE])


def finish_two_kernel(total_ref, got_ref, fields_ref, fits_ref, inertial_ref):
    lower = lax.axis_index("gz") == 0
    row = iota((8, COLS), 0)
    from_rim = jnp.where(lower, 7 - row, row)
    ours = from_rim < 4
    theirs = from_rim[:, :TILE] >= 4
    fields = []
    for p in range(5):
        got = jnp.concatenate(
            [got_ref[8 * p : 8 * p + 8, :], got_ref[40 + 8 * p : 48 + 8 * p, :]], axis=1
        )
        turned = pltpu.roll(got, 4, 0)
        for i, add in enumerate(
            (jnp.where(lower, turned, got), jnp.where(lower, got, turned))
        ):
            c = 2 * p + i
            fields.append(total_ref[8 * c : 8 * c + 8, :] + jnp.where(ours, add, 0.0))
            fields_ref[0, 0, 0, c] = fields[c]
    column = {}
    for i, c in enumerate(PROFILED):
        mine = jnp.where(lower, fields[c][:, :TILE], fields[c][:, TILE:])
        rim = total_ref[80 + 8 * c : 88 + 8 * c, :]
        rim = pltpu.roll(jnp.where(lower, rim[:, :TILE], rim[:, TILE:]), 4, 0)
        other = got_ref[80 + 8 * i : 88 + 8 * i, :] + jnp.where(theirs, rim, 0.0)
        column[c] = jnp.concatenate(
            [jnp.where(lower, mine, other), jnp.where(lower, other, mine)], axis=0
        )
    density = column[0]
    velocity = column[1] / (density + FLOOR_LEVEL)
    press = (column[4] + column[5] + column[6]) / 3.0
    fitted, inertial = column_fit(density, velocity, column[8], press)
    fits_ref[0, 0] = fitted
    inertial_ref[0, 0] = inertial


def plain_call(kernel, shapes, name, *args):
    vmem = pl.BlockSpec(memory_space=pltpu.VMEM)
    return pl.pallas_call(
        kernel,
        out_shape=shapes,
        in_specs=[vmem] * len(args),
        out_specs=jax.tree.map(lambda _: vmem, shapes),
        name=name,
    )(*args)


def column_fit(density, velocity, shear, press):
    upper = jnp.concatenate([velocity[1:, :], velocity[-1:, :]], axis=0)
    lower = jnp.concatenate([velocity[:1, :], velocity[:-1, :]], axis=0)
    rate = (upper - lower) / (2.0 * PITCH)
    inertial = rate * 1.0 / jnp.sqrt((press + FLOOR_LEVEL) / (density + FLOOR_LEVEL))
    friction = shear / (press + FLOOR_LEVEL)
    weight = density + FLOOR_LEVEL
    add = lambda v: jnp.sum(v, axis=0, keepdims=True)
    sum_zero = add(weight)
    sum_one = add(weight * inertial)
    sum_two = add(weight * inertial * inertial) + RIDGE_SHARE * sum_zero
    mix_zero = add(weight * friction)
    mix_one = add(weight * friction * inertial)
    determ = sum_zero * sum_two - sum_one * sum_one
    fitted = jnp.concatenate(
        [
            (mix_zero * sum_two - sum_one * mix_one) / determ,
            (sum_zero * mix_one - sum_one * mix_zero) / determ,
        ],
        axis=0,
    )
    return fitted, inertial


def swaps(first, second, axis):
    count = lax.axis_size(axis)
    got = []
    for start, value in ((0, first), (1, second)):
        links = []
        for i in range(start, count - 1, 2):
            links += [(i, i + 1), (i + 1, i)]
        got.append(lax.ppermute(value, axis, links) if links else jnp.zeros_like(value))
    return got


def exchange(low, high, axis):
    even = is_even(axis)
    one, two = swaps(jnp.where(even, high, low), jnp.where(even, low, high), axis)
    return jnp.where(even, two, one), jnp.where(even, one, two)


def local(grains, pairs):
    own, near = box_sort(grains, pairs)
    cube = near.reshape(4, 2, 2, 8, TILE)
    below, above = exchange(cube[:, 0], cube[:, 1], "gz")
    cube = jnp.concatenate([below[:, None], cube, above[:, None]], axis=1)
    below, above = exchange(cube[:, :, 0], cube[:, :, 1], "gy")
    cube = jnp.concatenate([below[:, :, None], cube, above[:, :, None]], axis=2)
    below, above = exchange(cube[:, :, :, 0], cube[:, :, :, 7], "gx")
    side = jnp.stack([below, above]).reshape(2, 4, 16, TILE)
    rim0, rim1, wide = stress_and_deposit(cube.reshape(4, 128, TILE), side, own.reshape(7 * NB, TILE))
    first, second = swaps(rim0, rim1, "gx")
    block = jax.ShapeDtypeStruct((160, TILE), F32)
    square = jax.ShapeDtypeStruct((160, COLS), F32)
    rim0, rim1, inner = plain_call(rim_x_kernel, [block, block, square], "rim_x", wide, first, second)
    first, second = swaps(rim0, rim1, "gy")
    if lax.axis_size("gz") == 2:
        sends = jax.ShapeDtypeStruct((128, TILE), F32)
        total, send = plain_call(rim_y_two_kernel, [square, sends], "rim_y", inner, first, second)
        got, _ = swaps(send, send, "gz")
        outs = [(1, 1, 1, 10, 8, COLS), (1, 1, 2, TILE), (1, 1, 16, TILE)]
        outs = [jax.ShapeDtypeStruct(shape, F32) for shape in outs]
        return tuple(plain_call(finish_two_kernel, outs, "finish", total, got))
    total = plain_call(rim_y_kernel, square, "rim_y", inner, first, second)
    fields = total[:80].reshape(10, 8, COLS)
    rim = total[80:].reshape(10, 8, COLS)
    from_below, from_above = exchange(rim[:, :4], rim[:, 4:], "gz")
    fields = fields + jnp.concatenate([from_below, from_above], axis=1)
    share = COLS // lax.axis_size("gz")
    start = lax.axis_index("gz") * share
    density = fields[0]
    velocity = fields[1] / (density + FLOOR_LEVEL)
    shear = fields[8]
    press = (fields[4] + fields[5] + fields[6]) / 3.0
    profile = jnp.stack([density, velocity, shear, press])
    whole = lax.all_gather(profile, "gz", axis=1, tiled=True)
    whole = lax.dynamic_slice_in_dim(whole, start, share, 2)
    fitted, inertial = column_fit(*whole)
    return (fields[None, None, None], fitted[None, None], inertial[None, None])


def solution(mesh):
    in_specs = (P("gx", "gy", "gz", None, None), P("gx", "gy", "gz", None, None))
    out_specs = (
        P("gx", "gy", "gz", None, None, None),
        P("gx", "gy", None, "gz"),
        P("gx", "gy", None, "gz"),
    )
    return jax.shard_map(local, mesh=mesh, in_specs=in_specs, out_specs=out_specs, check_vma=False)
```

time: 88.6 us -> 72.1 us (0.81)
  Pallas kernels: 38.4 us -> 30.7 us
  other arithmetic: 5.92 us -> 1.01 us
  blocking collectives: 4.58 us -> 0 us
  local copies, waits for them, and re-layouts: 5.16 us -> 6.67 us
    pallas_call x2 -> x1, Pallas kernels: 34.4 us -> 23.2 us  [stress_and_deposit(): pl.pallas_call(stress_kernel, out_shape=[jax.ShapeDtypeStruct((80, TILE),...]
    all_gather x1 -> x0, blocking collectives: 4.58 us -> none  [local(): whole = lax.all_gather(profile, 'gz', axis=1, tiled=True)]
    pallas_call x2 -> x4, Pallas kernels: 3.99 us -> 7.5 us  [plain_call(): pl.pallas_call(kernel, out_shape=shapes, in_specs=[vmem] * len(args), out...]
    unnamed x5 -> x16, local copies, waits for them, and re-layouts: 1.38 us -> 4.88 us
    slice x2 -> x0, local copies, waits for them, and re-layouts: 1.74 us -> none  [the longest x1 0.89 us: local(): left, right = exchange(wide[:, :128], wide[:, :128], 'gx')]
    select_n x6 -> x3, other arithmetic: 1.39 us -> 0.03 us  [exchange(): return (jnp.where(even, two, one), jnp.where(even, one, two))]
    select_n x3 -> x1, other arithmetic: 0.98 us -> 0.02 us  [exchange(): jnp.where(even, high, low)]
    reshape x2 -> x1, local copies, waits for them, and re-layouts: 0.93 us -> 0.03 us  [local(): cube = near.reshape(4, 2, 2, 8, TILE)]
where the time goes in v2:
time: 72.1 us; the launch traced here: 71.6 us
  Pallas kernels  30.7 us (43%)
  waiting for transfers between devices  19.5 us (27%)
  starting transfers between devices  12.9 us (18%)
  local copies, waits for them, and re-layouts  6.67 us (9%)
  other arithmetic  1.01 us (1%)
  between operations  0.81 us (1%)
    pallas_call x1, Pallas kernels, stress_and_deposit(): pl.pallas_call(stress_kernel, out_shape=[jax.ShapeDtypeStruct((80, TILE),...  23.2 us
    ppermute x10, waiting for transfers between devices, swaps(): lax.ppermute(value, axis, links)  19.5 us
    ppermute x10, starting transfers between devices, swaps(): lax.ppermute(value, axis, links)  12.9 us
    pallas_call x4, Pallas kernels, plain_call(): pl.pallas_call(kernel, out_shape=shapes, in_specs=[vmem] * len(args), out...  7.5 us
    unnamed x16, local copies, waits for them, and re-layouts  4.88 us
  transfers between devices with their start and end apart: 10, of which 8 were waited for; matrix products, arithmetic and copies ran while one was open for 1% of the time, Pallas kernels for 0%

profile of v2, /device:TPU:10, one launch (start us, length us, event | category | flops | bytes accessed | tf_op | source)
XLA Modules:
  0.0 71.6 jit_solution(6232520845918757356)
XLA Ops:
  0.7 0.7 copy-done.6
  1.3 0.7 copy.6.pairs_ref
  2.0 1.6 %copy.5.grains_ref = f32[1,1,1,7,4096]{4,3,2,1,0:T(8,128)} copy(f32[1,1,1,7,4096]{4,2,3,1,0:T(1,128)} %param.2) | data formatting | bytes 229376 | tf_op args[0]
  3.6 1.9 %box_sort.1 = (f32[7,32,128]{2,1,0:T(8,128)}, f32[4,32,128]{2,1,0:T(8,128)}) custom-call(f32[1,1,1,7,4096]{4,3,2,1,0:T(8,128)} %copy.5.grains_ref, s32[1,1,1,32,27]{4,3,2,1,0:T(8,128)} %copy.6.pairs_ref), custom_call_target="tpu_custom_call" | custom-call | tf_op jit(solution)/shard_map/box_sort/pallas_call | solution.py:581
  5.5 0.8 %fusion.1 = (f32[4,1,2,8,128]{4,3,2,1,0:T(8,128)S(1)}, f32[4,1,2,8,128]{4,3,2,1,0:T(8,128)S(1)}) fusion(f32[4,2,2,8,128]{4,3,2,1,0:T(8,128)} %bitcast.32), kind=kLoop, calls=%fused_computation.15 | loop fusion | bytes 131072 | tf_op jit(solution)/shard_map/slice | solution.py:634
  6.3 1.6 %collective-permute-start = (f32[4,2,8,128]{3,0,2,1:T(4,128)S(1)}, f32[4,2,8,128]{3,0,2,1:T(4,128)S(1)}, u32[]{:S(2)}, u32[]{:S(2)}) collective-permute-start(f32[4,2,8,128]{3,0,2,1:T(4,128)S(1)} %fusion), channel_id=1, source_target_pairs={{0,1},{1,0},{2,3},{3,2},{4,5},{5,4},{6,7},{7,6},{8,9},{9,8},{10,11... | collective-permute-start | bytes 98312 | tf_op jit(solution)/shard_map/ppermute | solution.py:621
  8.0 2.3 %collective-permute-done = f32[4,2,8,128]{3,0,2,1:T(4,128)S(1)} collective-permute-done((f32[4,2,8,128]{3,0,2,1:T(4,128)S(1)}, f32[4,2,8,128]{3,0,2,1:T(4,128)S(1)}, u32[]{:S(2)}, u32[]{:S(2)}) %collective-permute-start) | collective-permute-done | bytes 32800 | tf_op jit(solution)/shard_map/ppermute | solution.py:621
  10.3 0.1 pad_maximum_fusion.1
  10.5 3.5 %collective-permute-start.1 = (f32[4,4,8,128]{3,1,0,2:T(4,128)S(1)}, f32[4,4,8,128]{3,1,0,2:T(4,128)S(1)}, u32[]{:S(2)}, u32[]{:S(2)}) collective-permute-start(f32[4,4,8,128]{3,1,0,2:T(4,128)S(1)} %get-tuple-element.27), channel_id=1, source_target_pairs={{2,4},{4,2},{3,5},{5,3},{10,12},{12,10},{11,13},{13,11},{18,20},{2... | collective-permute-start | bytes 196616 | tf_op jit(solution)/shard_map/ppermute | solution.py:621
  14.0 0.1 collective-permute-start.2
  14.1 0.1 copy.12
  14.2 2.5 %collective-permute-done.1 = f32[4,4,8,128]{3,1,0,2:T(4,128)S(1)} collective-permute-done((f32[4,4,8,128]{3,1,0,2:T(4,128)S(1)}, f32[4,4,8,128]{3,1,0,2:T(4,128)S(1)}, u32[]{:S(2)}, u32[]{:S(2)}) %collective-permute-start.1) | collective-permute-done | bytes 65568 | tf_op jit(solution)/shard_map/ppermute | solution.py:621
  16.6 1.7 %collective-permute-done.2 = f32[4,4,8,128]{3,1,0,2:T(4,128)S(1)} collective-permute-done((f32[4,4,8,128]{3,1,0,2:T(4,128)S(1)}, f32[4,4,8,128]{3,1,0,2:T(4,128)S(1)}, u32[]{:S(2)}, u32[]{:S(2)}) %collective-permute-start.2) | collective-permute-done | bytes 65568 | tf_op jit(solution)/shard_map/ppermute | solution.py:621
  18.3 0.2 pad_maximum_fusion
  18.5 1.9 %collective-permute-start.3 = (f32[4,4,4,128]{3,2,1,0:T(4,128)S(1)}, f32[4,4,4,128]{3,2,1,0:T(4,128)S(1)}, u32[]{:S(2)}, u32[]{:S(2)}) collective-permute-start(f32[4,4,4,128]{3,2,1,0:T(4,128)S(1)} %get-tuple-element.23), channel_id=1, source_target_pairs={{8,16},{16,8},{9,17},{17,9},{10,18},{18,10},{11,19},{19,11},{12,20... | collective-permute-start | bytes 98312 | tf_op jit(solution)/shard_map/ppermute | solution.py:621
  20.5 0.9 %copy.13 = f32[4,4,4,8,128]{4,3,2,1,0:T(8,128)} copy(f32[4,4,4,8,128]{4,2,1,0,3:T(4,128)S(1)} %pad_maximum_fusion) | data formatting | bytes 524288 | tf_op jit(solution)/shard_map/concatenate | solution.py:637
  21.4 2.4 %collective-permute-done.3 = f32[4,4,4,128]{3,2,1,0:T(4,128)S(1)} collective-permute-done((f32[4,4,4,128]{3,2,1,0:T(4,128)S(1)}, f32[4,4,4,128]{3,2,1,0:T(4,128)S(1)}, u32[]{:S(2)}, u32[]{:S(2)}) %collective-permute-start.3) | collective-permute-done | bytes 32800 | tf_op jit(solution)/shard_map/ppermute | solution.py:621
  23.8 0.6 pad_maximum_fusion.2.side_ref
  24.4 23.2 %stress_deposit.1 = (f32[80,128]{1,0:T(8,128)}, f32[80,128]{1,0:T(8,128)}, f32[160,512]{1,0:T(8,128)}) custom-call(f32[4,128,128]{2,1,0:T(8,128)} %bitcast.31, f32[2,4,16,128]{3,2,1,0:T(8,128)} %pad_maximum_fusion.2.side_ref, f32[224,128]{1,0:T(8,128)} %bitcast.40), custom_call_target="tpu_custom_call" | custom-call | tf_op jit(solution)/shard_map/stress_deposit/pallas_call | solution.py:458
  47.6 1.9 %collective-permute-start.6 = (f32[80,128]{1,0:T(8,128)}, f32[80,128]{1,0:T(8,128)S(1)}, u32[]{:S(2)}, u32[]{:S(2)}) collective-permute-start(f32[80,128]{1,0:T(8,128)} %get-tuple-element.17), channel_id=1, source_target_pairs={{8,16},{16,8},{9,17},{17,9},{10,18},{18,10},{11,19},{19,11},{12,20... | collective-permute-start | bytes 122888 | tf_op jit(solution)/shard_map/ppermute | solution.py:621
  49.5 3.6 %collective-permute-done.6.second_ref = f32[80,128]{1,0:T(8,128)S(1)} collective-permute-done((f32[80,128]{1,0:T(8,128)}, f32[80,128]{1,0:T(8,128)S(1)}, u32[]{:S(2)}, u32[]{:S(2)}) %collective-permute-start.6) | collective-permute-done | bytes 40992 | tf_op jit(solution)/shard_map/ppermute | solution.py:621
  53.1 0.6 copy-done.5
  53.7 2.1 %rim_x.1 = (f32[160,128]{1,0:T(8,128)}, f32[160,128]{1,0:T(8,128)}, f32[160,256]{1,0:T(8,128)}) custom-call(f32[160,512]{1,0:T(8,128)} %get-tuple-element.15.wide_ref, f32[80,128]{1,0:T(8,128)} %copy-done.4, f32[80,128]{1,0:T(8,128)} %copy-done.5), custom_call_target="tpu_custom_call" | custom-call | tf_op jit(solution)/shard_map/rim_x/pallas_call | solution.py:581
  55.8 2.3 %collective-permute-start.8 = (f32[160,128]{1,0:T(8,128)}, f32[160,128]{1,0:T(8,128)S(1)}, u32[]{:S(2)}, u32[]{:S(2)}) collective-permute-start(f32[160,128]{1,0:T(8,128)} %get-tuple-element.20), channel_id=1, source_target_pairs={{2,4},{4,2},{3,5},{5,3},{10,12},{12,10},{11,13},{13,11},{18,20},{2... | collective-permute-start | bytes 245768 | tf_op jit(solution)/shard_map/ppermute | solution.py:621
  58.2 2.3 %collective-permute-done.7.first_ref = f32[160,128]{1,0:T(8,128)S(1)} collective-permute-done((f32[160,128]{1,0:T(8,128)}, f32[160,128]{1,0:T(8,128)S(1)}, u32[]{:S(2)}, u32[]{:S(2)}) %collective-permute-start.7) | collective-permute-done | bytes 81952 | tf_op jit(solution)/shard_map/ppermute | solution.py:621
  60.5 1.9 %collective-permute-done.8.second_ref = f32[160,128]{1,0:T(8,128)S(1)} collective-permute-done((f32[160,128]{1,0:T(8,128)}, f32[160,128]{1,0:T(8,128)S(1)}, u32[]{:S(2)}, u32[]{:S(2)}) %collective-permute-start.8) | collective-permute-done | bytes 81952 | tf_op jit(solution)/shard_map/ppermute | solution.py:621
  62.3 0.6 copy-done.2
  63.0 2.0 %rim_y.1 = (f32[160,256]{1,0:T(8,128)}, f32[128,128]{1,0:T(8,128)}) custom-call(f32[160,256]{1,0:T(8,128)} %get-tuple-element.18.inner_ref, f32[160,128]{1,0:T(8,128)} %copy-done.1, f32[160,128]{1,0:T(8,128)} %copy-done.2), custom_call_target="tpu_custom_call" | custom-call | tf_op jit(solution)/shard_map/rim_y/pallas_call | solution.py:581
  64.9 1.5 %collective-permute-start.9 = (f32[128,128]{1,0:T(8,128)}, f32[128,128]{1,0:T(8,128)S(1)}, u32[]{:S(2)}, u32[]{:S(2)}) collective-permute-start(f32[128,128]{1,0:T(8,128)} %get-tuple-element.22), channel_id=1, source_target_pairs={{0,1},{1,0},{2,3},{3,2},{4,5},{5,4},{6,7},{7,6},{8,9},{9,8},{10,11... | collective-permute-start | bytes 196616 | tf_op jit(solution)/shard_map/ppermute | solution.py:621
  66.5 2.9 %collective-permute-done.9.got_ref = f32[128,128]{1,0:T(8,128)S(1)} collective-permute-done((f32[128,128]{1,0:T(8,128)}, f32[128,128]{1,0:T(8,128)S(1)}, u32[]{:S(2)}, u32[]{:S(2)}) %collective-permute-start.9) | collective-permute-done | bytes 65568 | tf_op jit(solution)/shard_map/ppermute | solution.py:621
  69.4 0.6 copy-done.3
  70.0 1.6 %finish.1 = (f32[1,1,1,10,8,256]{5,4,3,2,1,0:T(8,128)}, f32[1,1,2,128]{3,2,1,0:T(2,128)}, f32[1,1,16,128]{3,2,1,0:T(8,128)}) custom-call(f32[160,256]{1,0:T(8,128)} %get-tuple-element.21.total_ref, f32[128,128]{1,0:T(8,128)} %copy-done.3), custom_call_target="tpu_custom_call" | custom-call | tf_op jit(solution)/shard_map/finish/pallas_call | solution.py:581
  (22 shorter events, 0.2 us)
Async XLA Ops:
  0.6 0.7 copy-start.6
  6.3 1.6 %copy-start = (f32[4,32,128]{2,1,0:T(8,128)S(1)}, f32[4,32,128]{2,1,0:T(8,128)}, u32[]{:S(2)}) copy-start(f32[4,32,128]{2,1,0:T(8,128)} %get-tuple-element.13) | copy-start | bytes 196612
  6.3 4.0 %collective-permute-start = (f32[4,2,8,128]{3,0,2,1:T(4,128)S(1)}, f32[4,2,8,128]{3,0,2,1:T(4,128)S(1)}, u32[]{:S(2)}, u32[]{:S(2)}) collective-permute-start(f32[4,2,8,128]{3,0,2,1:T(4,128)S(1)} %fusion), channel_id=1, source_target_pairs={{0,1},{1,0},{2,3},{3,2},{4,5},{5,4},{6,7},{7,6},{8,9},{9,8},{10,11... | collective-permute-start | bytes 98312 | tf_op jit(solution)/shard_map/ppermute | solution.py:621
  10.5 6.2 %collective-permute-start.1 = (f32[4,4,8,128]{3,1,0,2:T(4,128)S(1)}, f32[4,4,8,128]{3,1,0,2:T(4,128)S(1)}, u32[]{:S(2)}, u32[]{:S(2)}) collective-permute-start(f32[4,4,8,128]{3,1,0,2:T(4,128)S(1)} %get-tuple-element.27), channel_id=1, source_target_pairs={{2,4},{4,2},{3,5},{5,3},{10,12},{12,10},{11,13},{13,11},{18,20},{2... | collective-permute-start | bytes 196616 | tf_op jit(solution)/shard_map/ppermute | solution.py:621
  14.0 4.3 %collective-permute-start.2 = (f32[4,4,8,128]{3,1,0,2:T(4,128)S(1)}, f32[4,4,8,128]{3,1,0,2:T(4,128)S(1)}, u32[]{:S(2)}, u32[]{:S(2)}) collective-permute-start(f32[4,4,8,128]{3,1,0,2:T(4,128)S(1)} %get-tuple-element.28), channel_id=1, source_target_pairs={{0,2},{2,0},{4,6},{6,4},{1,3},{3,1},{5,7},{7,5},{8,10},{10,8},{12,... | collective-permute-start | bytes 196616 | tf_op jit(solution)/shard_map/ppermute | solution.py:621
  18.5 5.2 %collective-permute-start.3 = (f32[4,4,4,128]{3,2,1,0:T(4,128)S(1)}, f32[4,4,4,128]{3,2,1,0:T(4,128)S(1)}, u32[]{:S(2)}, u32[]{:S(2)}) collective-permute-start(f32[4,4,4,128]{3,2,1,0:T(4,128)S(1)} %get-tuple-element.23), channel_id=1, source_target_pairs={{8,16},{16,8},{9,17},{17,9},{10,18},{18,10},{11,19},{19,11},{12,20... | collective-permute-start | bytes 98312 | tf_op jit(solution)/shard_map/ppermute | solution.py:621
  20.4 3.3 %collective-permute-start.4 = (f32[4,4,4,128]{3,2,1,0:T(4,128)S(1)}, f32[4,4,4,128]{3,2,1,0:T(4,128)S(1)}, u32[]{:S(2)}, u32[]{:S(2)}) collective-permute-start(f32[4,4,4,128]{3,2,1,0:T(4,128)S(1)} %get-tuple-element.24), channel_id=1, source_target_pairs={{0,8},{8,0},{16,24},{24,16},{1,9},{9,1},{17,25},{25,17},{2,10},{10... | collective-permute-start | bytes 98312 | tf_op jit(solution)/shard_map/ppermute | solution.py:621
  47.6 1.9 %collective-permute-start.5 = (f32[80,128]{1,0:T(8,128)}, f32[80,128]{1,0:T(8,128)S(1)}, u32[]{:S(2)}, u32[]{:S(2)}) collective-permute-start(f32[80,128]{1,0:T(8,128)} %get-tuple-element.16), channel_id=1, source_target_pairs={{0,8},{8,0},{16,24},{24,16},{1,9},{9,1},{17,25},{25,17},{2,10},{10... | collective-permute-start | bytes 122888 | tf_op jit(solution)/shard_map/ppermute | solution.py:621
  47.6 5.5 %collective-permute-start.6 = (f32[80,128]{1,0:T(8,128)}, f32[80,128]{1,0:T(8,128)S(1)}, u32[]{:S(2)}, u32[]{:S(2)}) collective-permute-start(f32[80,128]{1,0:T(8,128)} %get-tuple-element.17), channel_id=1, source_target_pairs={{8,16},{16,8},{9,17},{17,9},{10,18},{18,10},{11,19},{19,11},{12,20... | collective-permute-start | bytes 122888 | tf_op jit(solution)/shard_map/ppermute | solution.py:621
  49.5 3.6 %copy-start.4 = (f32[80,128]{1,0:T(8,128)}, f32[80,128]{1,0:T(8,128)S(1)}, u32[]{:S(2)}) copy-start(f32[80,128]{1,0:T(8,128)S(1)} %collective-permute-done.5.first_ref) | copy-start | bytes 122884
  53.1 0.6 copy-start.5
  55.8 4.7 %collective-permute-start.7 = (f32[160,128]{1,0:T(8,128)}, f32[160,128]{1,0:T(8,128)S(1)}, u32[]{:S(2)}, u32[]{:S(2)}) collective-permute-start(f32[160,128]{1,0:T(8,128)} %get-tuple-element.19), channel_id=1, source_target_pairs={{0,2},{2,0},{4,6},{6,4},{1,3},{3,1},{5,7},{7,5},{8,10},{10,8},{12,... | collective-permute-start | bytes 245768 | tf_op jit(solution)/shard_map/ppermute | solution.py:621
  55.8 6.5 %collective-permute-start.8 = (f32[160,128]{1,0:T(8,128)}, f32[160,128]{1,0:T(8,128)S(1)}, u32[]{:S(2)}, u32[]{:S(2)}) collective-permute-start(f32[160,128]{1,0:T(8,128)} %get-tuple-element.20), channel_id=1, source_target_pairs={{2,4},{4,2},{3,5},{5,3},{10,12},{12,10},{11,13},{13,11},{18,20},{2... | collective-permute-start | bytes 245768 | tf_op jit(solution)/shard_map/ppermute | solution.py:621
  60.4 1.9 %copy-start.1 = (f32[160,128]{1,0:T(8,128)}, f32[160,128]{1,0:T(8,128)S(1)}, u32[]{:S(2)}) copy-start(f32[160,128]{1,0:T(8,128)S(1)} %collective-permute-done.7.first_ref) | copy-start | bytes 245764
  62.3 0.6 copy-start.2
  64.9 4.5 %collective-permute-start.9 = (f32[128,128]{1,0:T(8,128)}, f32[128,128]{1,0:T(8,128)S(1)}, u32[]{:S(2)}, u32[]{:S(2)}) collective-permute-start(f32[128,128]{1,0:T(8,128)} %get-tuple-element.22), channel_id=1, source_target_pairs={{0,1},{1,0},{2,3},{3,2},{4,5},{5,4},{6,7},{7,6},{8,9},{9,8},{10,11... | collective-permute-start | bytes 196616 | tf_op jit(solution)/shard_map/ppermute | solution.py:621
  69.4 0.6 copy-start.3

commit v3 on v2

--- a/solution.py
+++ b/solution.py
@@ -62,27 +62,28 @@
 
 
 def sort_kernel(grains_ref, pairs_ref, own_ref, near_ref):
-    pairs = pairs_ref[0, 0, 0]
-    live = pairs >= 0
-    hood = jnp.where(live, pairs, 0) >> 5
-    third = (hood * 11) >> 5
-    part_c = hood - 3 * third
-    part_b = third - 3 * ((third * 11) >> 5)
-
-    def has(part, value):
-        hit = jnp.where(live & (part == value), 1.0, 0.0)
-        return jnp.max(hit, axis=1, keepdims=True) > 0.5
-
-    box_y = has(part_b, 2) | (is_last("gy") & jnp.logical_not(has(part_b, 0)))
-    box_z = has(part_c, 2) | (is_last("gz") & jnp.logical_not(has(part_c, 0)))
-    grains = grains_ref[0, 0, 0].reshape(7, NB, TILE)
-    rows = [grains[r] for r in range(7)]
+    flags = {(part, value): jnp.zeros((1, NB), F32) for part in "yz" for value in (0, 2)}
+    for n in range(pairs_ref.shape[0]):
+        pair = pairs_ref[n]
+        hood = jnp.where(pair >= 0, pair, 13 * NB) >> 5
+        third = (hood * 11) >> 5
+        parts = {"y": third - 3 * ((third * 11) >> 5), "z": hood - 3 * third}
+        flags = {k: jnp.where(parts[k[0]] == k[1], 1.0, f) for k, f in flags.items()}
+
+    def upper(part, axis):
+        alone = jnp.where(is_last(axis), 1.0 - flags[part, 0], 0.0)
+        return jnp.maximum(flags[part, 2], alone)
+
+    group = 64.0 * upper("y", "gy") + 128.0 * upper("z", "gz")
+    rows = [grains_ref[r] for r in range(7)]
     centre = 0.5 * (jnp.min(rows[0], axis=1, keepdims=True) + jnp.max(rows[0], axis=1, keepdims=True))
-    key = centre + jnp.where(box_y, 64.0, 0.0) + jnp.where(box_z, 128.0, 0.0)
     sub = iota((NB, TILE), 0)
     lane = iota((NB, TILE), 1)
+    same = sub == lane
+    group = jnp.concatenate([group, jnp.zeros((1, TILE - NB), F32)], axis=1)
+    key = centre + jnp.sum(jnp.where(same, group, 0.0), axis=1, keepdims=True)
     wide = jnp.broadcast_to(key, (NB, TILE))
-    key_row = jnp.sum(jnp.where(sub == lane, wide, 0.0), axis=0, keepdims=True)
+    key_row = jnp.sum(jnp.where(same, wide, 0.0), axis=0, keepdims=True)
     before = (wide < key_row) | ((wide == key_row) & (sub < lane))
     rank = jnp.sum(jnp.where(before, 1.0, 0.0), axis=0, keepdims=True)
     onehot = jnp.where((rank == sub.astype(F32)) & (lane < NB), 1.0, 0.0).astype(BF16)[:, :NB]
@@ -96,8 +97,9 @@
 
 
 def box_sort(grains, pairs):
-    shape = lambda rows: jax.ShapeDtypeStruct((rows, NB, TILE), F32)
-    return plain_call(sort_kernel, [shape(7), shape(4)], "box_sort", grains, pairs)
+    shapes = [on_chip((7, NB, TILE)), on_chip((4, NB, TILE))]
+    listed = pairs.transpose(0, 1, 2, 4, 3).reshape(pairs.shape[4], 1, NB)
+    return plain_call(sort_kernel, shapes, "box_sort", grains.reshape(7, NB, TILE), listed)
 
 
 def lane_take(value, index):
@@ -454,29 +456,26 @@
 
 
 def stress_and_deposit(grid, side, grains):
-    vmem = pl.BlockSpec(memory_space=pltpu.VMEM)
-    return pl.pallas_call(
+    columns = 3 * TILE + COLS
+    return plain_call(
         stress_kernel,
-        out_shape=[
-            jax.ShapeDtypeStruct((80, TILE), F32),
-            jax.ShapeDtypeStruct((80, TILE), F32),
-            jax.ShapeDtypeStruct((160, 2 * TILE + COLS), F32),
-        ],
-        in_specs=[vmem, vmem, vmem],
-        out_specs=[vmem, vmem, vmem],
-        scratch_shapes=[
+        [on_chip((80, TILE)), on_chip((80, TILE)), on_chip((160, 2 * TILE + COLS))],
+        "stress_deposit",
+        held(grid),
+        held(side),
+        held(grains),
+        scratch=[
             pltpu.VMEM((4 * NB, TILE), F32),
             pltpu.VMEM((8 * 160, TILE), F32),
             pltpu.VMEM((6 * NB, TILE), F32),
-            pltpu.VMEM((128 + 2 * 128 + COLS, NB * TILE), BF16),
+            pltpu.VMEM((columns, NB * TILE), BF16),
             pltpu.VMEM((160, NB * TILE), BF16),
             pltpu.VMEM((5 * 16 * PITCH_ROWS, TILE), F32),
             pltpu.VMEM((5 * 16 * PITCH_ROWS, TILE), F32),
             pltpu.VMEM((38 * PITCH_ROWS, TILE), F32),
             pltpu.VMEM((16 * PITCH_ROWS, TILE), F32),
         ],
-        name="stress_deposit",
-    )(grid, side, grains)
+    )
 
 
 def rim_x_kernel(wide_ref, first_ref, second_ref, rim0_ref, rim1_ref, inner_ref):
@@ -576,13 +575,22 @@
     inertial_ref[0, 0] = inertial
 
 
-def plain_call(kernel, shapes, name, *args):
+def held(array):
+    return pltpu.with_memory_space_constraint(array, pltpu.VMEM)
+
+
+def on_chip(shape):
+    return pltpu.VMEM(shape, F32)
+
+
+def plain_call(kernel, shapes, name, *args, scratch=()):
     vmem = pl.BlockSpec(memory_space=pltpu.VMEM)
     return pl.pallas_call(
         kernel,
         out_shape=shapes,
         in_specs=[vmem] * len(args),
         out_specs=jax.tree.map(lambda _: vmem, shapes),
+        scratch_shapes=scratch,
         name=name,
     )(*args)
 
@@ -639,18 +647,21 @@
     side = jnp.stack([below, above]).reshape(2, 4, 16, TILE)
     rim0, rim1, wide = stress_and_deposit(cube.reshape(4, 128, TILE), side, own.reshape(7 * NB, TILE))
     first, second = swaps(rim0, rim1, "gx")
-    block = jax.ShapeDtypeStruct((160, TILE), F32)
-    square = jax.ShapeDtypeStruct((160, COLS), F32)
-    rim0, rim1, inner = plain_call(rim_x_kernel, [block, block, square], "rim_x", wide, first, second)
+    block, square = on_chip((160, TILE)), on_chip((160, COLS))
+    rim0, rim1, inner = plain_call(
+        rim_x_kernel, [block, block, square], "rim_x", held(wide), held(first), held(second)
+    )
     first, second = swaps(rim0, rim1, "gy")
     if lax.axis_size("gz") == 2:
-        sends = jax.ShapeDtypeStruct((128, TILE), F32)
-        total, send = plain_call(rim_y_two_kernel, [square, sends], "rim_y", inner, first, second)
+        sends = on_chip((128, TILE))
+        total, send = plain_call(
+            rim_y_two_kernel, [square, sends], "rim_y", held(inner), held(first), held(second)
+        )
         got, _ = swaps(send, send, "gz")
         outs = [(1, 1, 1, 10, 8, COLS), (1, 1, 2, TILE), (1, 1, 16, TILE)]
         outs = [jax.ShapeDtypeStruct(shape, F32) for shape in outs]
-        return tuple(plain_call(finish_two_kernel, outs, "finish", total, got))
-    total = plain_call(rim_y_kernel, square, "rim_y", inner, first, second)
+        return tuple(plain_call(finish_two_kernel, outs, "finish", held(total), held(got)))
+    total = plain_call(rim_y_kernel, square, "rim_y", held(inner), held(first), held(second))
     fields = total[:80].reshape(10, 8, COLS)
     rim = total[80:].reshape(10, 8, COLS)
     from_below, from_above = exchange(rim[:, :4], rim[:, 4:], "gz")

time: 72.1 us -> 58.4 us (0.81)
  Pallas kernels: 30.7 us -> 23.9 us
  local copies, waits for them, and re-layouts: 6.67 us -> 0.31 us
    pallas_call x1 -> x0, Pallas kernels: 23.2 us -> none  [stress_and_deposit(): pl.pallas_call(stress_kernel, out_shape=[jax.ShapeDtypeStruct((80, TILE),...]
    pallas_call x4 -> x5, Pallas kernels: 7.5 us -> 23.9 us  [plain_call(): pl.pallas_call(kernel, out_shape=shapes, in_specs=[vmem] * len(args), out...]
    unnamed x16 -> x0, local copies, waits for them, and re-layouts: 4.88 us -> none
    slice x1, local copies, waits for them, and re-layouts: 0.78 us -> 0.01 us  [local(): below, above = exchange(cube[:, 0], cube[:, 1], 'gz')]
where the time goes in v3:
time: 58.4 us; the launch traced here: 58.2 us
  Pallas kernels  23.9 us (41%)
  waiting for transfers between devices  19.6 us (34%)
  starting transfers between devices  13.1 us (22%)
  between operations  0.85 us (1%)
    pallas_call x5, Pallas kernels, plain_call(): pl.pallas_call(kernel, out_shape=shapes, in_specs=[vmem] * len(args), out...  23.9 us
    ppermute x10, waiting for transfers between devices, swaps(): lax.ppermute(value, axis, links)  19.6 us
    ppermute x10, starting transfers between devices, swaps(): lax.ppermute(value, axis, links)  13.1 us
  transfers between devices with their start and end apart: 10, of which 8 were waited for; matrix products, arithmetic and copies ran while one was open for 1% of the time, Pallas kernels for 0%

profile of v3, /device:TPU:10, one launch (start us, length us, event | category | flops | bytes accessed | tf_op | source)
XLA Modules:
  0.0 58.2 jit_solution(2796820559570629890)
XLA Ops:
  0.6 1.3 %box_sort.1 = (f32[7,32,128]{2,1,0:T(8,128)S(1)}, f32[4,32,128]{2,1,0:T(8,128)S(1)}) custom-call(f32[7,32,128]{2,1,0:T(8,128)} %bitcast.47, s32[27,1,32]{2,1,0:T(1,128)} %bitcast.52), custom_call_target="tpu_custom_call" | custom-call | tf_op jit(solution)/shard_map/box_sort/pallas_call | solution.py:588
  2.0 1.6 %collective-permute-start = (f32[4,2,8,128]{3,0,2,1:T(4,128)S(1)}, f32[4,2,8,128]{3,0,2,1:T(4,128)S(1)}, u32[]{:S(2)}, u32[]{:S(2)}) collective-permute-start(f32[4,2,8,128]{3,0,2,1:T(4,128)S(1)} %fusion), channel_id=1, source_target_pairs={{0,1},{1,0},{2,3},{3,2},{4,5},{5,4},{6,7},{7,6},{8,9},{9,8},{10,11... | collective-permute-start | bytes 98312 | tf_op jit(solution)/shard_map/ppermute | solution.py:629
  3.6 2.4 %collective-permute-done = f32[4,2,8,128]{3,0,2,1:T(4,128)S(1)} collective-permute-done((f32[4,2,8,128]{3,0,2,1:T(4,128)S(1)}, f32[4,2,8,128]{3,0,2,1:T(4,128)S(1)}, u32[]{:S(2)}, u32[]{:S(2)}) %collective-permute-start) | collective-permute-done | bytes 32800 | tf_op jit(solution)/shard_map/ppermute | solution.py:629
  6.0 0.1 pad_maximum_fusion.1
  6.1 3.5 %collective-permute-start.1 = (f32[4,4,8,128]{3,1,0,2:T(4,128)S(1)}, f32[4,4,8,128]{3,1,0,2:T(4,128)S(1)}, u32[]{:S(2)}, u32[]{:S(2)}) collective-permute-start(f32[4,4,8,128]{3,1,0,2:T(4,128)S(1)} %get-tuple-element.27), channel_id=1, source_target_pairs={{2,4},{4,2},{3,5},{5,3},{10,12},{12,10},{11,13},{13,11},{18,20},{2... | collective-permute-start | bytes 196616 | tf_op jit(solution)/shard_map/ppermute | solution.py:629
  9.6 0.1 collective-permute-start.2
  9.7 0.1 copy.11
  9.8 2.5 %collective-permute-done.1 = f32[4,4,8,128]{3,1,0,2:T(4,128)S(1)} collective-permute-done((f32[4,4,8,128]{3,1,0,2:T(4,128)S(1)}, f32[4,4,8,128]{3,1,0,2:T(4,128)S(1)}, u32[]{:S(2)}, u32[]{:S(2)}) %collective-permute-start.1) | collective-permute-done | bytes 65568 | tf_op jit(solution)/shard_map/ppermute | solution.py:629
  12.2 1.7 %collective-permute-done.2 = f32[4,4,8,128]{3,1,0,2:T(4,128)S(1)} collective-permute-done((f32[4,4,8,128]{3,1,0,2:T(4,128)S(1)}, f32[4,4,8,128]{3,1,0,2:T(4,128)S(1)}, u32[]{:S(2)}, u32[]{:S(2)}) %collective-permute-start.2) | collective-permute-done | bytes 65568 | tf_op jit(solution)/shard_map/ppermute | solution.py:629
  13.9 0.2 pad_maximum_fusion
  14.1 1.9 %collective-permute-start.3 = (f32[4,4,4,128]{3,2,1,0:T(4,128)S(1)}, f32[4,4,4,128]{3,2,1,0:T(4,128)S(1)}, u32[]{:S(2)}, u32[]{:S(2)}) collective-permute-start(f32[4,4,4,128]{3,2,1,0:T(4,128)S(1)} %get-tuple-element.23), channel_id=1, source_target_pairs={{8,16},{16,8},{9,17},{17,9},{10,18},{18,10},{11,19},{19,11},{12,20... | collective-permute-start | bytes 98312 | tf_op jit(solution)/shard_map/ppermute | solution.py:629
  16.1 0.1 collective-permute-start.4
  16.1 0.2 copy.12
  16.3 3.1 %collective-permute-done.3 = f32[4,4,4,128]{3,2,1,0:T(4,128)S(1)} collective-permute-done((f32[4,4,4,128]{3,2,1,0:T(4,128)S(1)}, f32[4,4,4,128]{3,2,1,0:T(4,128)S(1)}, u32[]{:S(2)}, u32[]{:S(2)}) %collective-permute-start.3) | collective-permute-done | bytes 32800 | tf_op jit(solution)/shard_map/ppermute | solution.py:629
  19.4 0.0 collective-permute-done.4
  19.4 21.4 %stress_deposit.1 = (f32[80,128]{1,0:T(8,128)S(1)}, f32[80,128]{1,0:T(8,128)S(1)}, f32[160,512]{1,0:T(8,128)S(1)}) custom-call(f32[4,128,128]{2,1,0:T(8,128)S(1)} %bitcast.37, f32[2,4,16,128]{3,2,1,0:T(8,128)S(1)} %pad_maximum_fusion.2.side_ref, f32[224,128]{1,0:T(8,128)S(1)} %bitcast.40), custom_call_target="tpu_custom_call" | custom-call | tf_op jit(solution)/shard_map/stress_deposit/pallas_call | solution.py:588
  40.8 0.1 collective-permute-start.5
  40.9 1.9 %collective-permute-start.6 = (f32[80,128]{1,0:T(8,128)S(1)}, f32[80,128]{1,0:T(8,128)S(1)}, u32[]{:S(2)}, u32[]{:S(2)}) collective-permute-start(f32[80,128]{1,0:T(8,128)S(1)} %get-tuple-element.17), channel_id=1, source_target_pairs={{8,16},{16,8},{9,17},{17,9},{10,18},{18,10},{11,19},{19,11},{12,20... | collective-permute-start | bytes 122888 | tf_op jit(solution)/shard_map/ppermute | solution.py:629
  42.8 0.0 collective-permute-done.5.first_ref
  42.8 3.4 %collective-permute-done.6.second_ref = f32[80,128]{1,0:T(8,128)S(1)} collective-permute-done((f32[80,128]{1,0:T(8,128)S(1)}, f32[80,128]{1,0:T(8,128)S(1)}, u32[]{:S(2)}, u32[]{:S(2)}) %collective-permute-start.6) | collective-permute-done | bytes 40992 | tf_op jit(solution)/shard_map/ppermute | solution.py:629
  46.2 0.3 rim_x.1
  46.6 0.1 collective-permute-start.7
  46.7 2.4 %collective-permute-start.8 = (f32[160,128]{1,0:T(8,128)S(1)}, f32[160,128]{1,0:T(8,128)S(1)}, u32[]{:S(2)}, u32[]{:S(2)}) collective-permute-start(f32[160,128]{1,0:T(8,128)S(1)} %get-tuple-element.20), channel_id=1, source_target_pairs={{2,4},{4,2},{3,5},{5,3},{10,12},{12,10},{11,13},{13,11},{18,20},{2... | collective-permute-start | bytes 245768 | tf_op jit(solution)/shard_map/ppermute | solution.py:629
  49.0 2.1 %collective-permute-done.7.first_ref = f32[160,128]{1,0:T(8,128)S(1)} collective-permute-done((f32[160,128]{1,0:T(8,128)S(1)}, f32[160,128]{1,0:T(8,128)S(1)}, u32[]{:S(2)}, u32[]{:S(2)}) %collective-permute-start.7) | collective-permute-done | bytes 81952 | tf_op jit(solution)/shard_map/ppermute | solution.py:629
  51.1 1.9 %collective-permute-done.8.second_ref = f32[160,128]{1,0:T(8,128)S(1)} collective-permute-done((f32[160,128]{1,0:T(8,128)S(1)}, f32[160,128]{1,0:T(8,128)S(1)}, u32[]{:S(2)}, u32[]{:S(2)}) %collective-permute-start.8) | collective-permute-done | bytes 81952 | tf_op jit(solution)/shard_map/ppermute | solution.py:629
  53.0 0.3 rim_y.1
  53.3 1.6 %collective-permute-start.9 = (f32[128,128]{1,0:T(8,128)S(1)}, f32[128,128]{1,0:T(8,128)S(1)}, u32[]{:S(2)}, u32[]{:S(2)}) collective-permute-start(f32[128,128]{1,0:T(8,128)S(1)} %get-tuple-element.22), channel_id=1, source_target_pairs={{0,1},{1,0},{2,3},{3,2},{4,5},{5,4},{6,7},{7,6},{8,9},{9,8},{10,11... | collective-permute-start | bytes 196616 | tf_op jit(solution)/shard_map/ppermute | solution.py:629
  54.8 2.7 %collective-permute-done.9.got_ref = f32[128,128]{1,0:T(8,128)S(1)} collective-permute-done((f32[128,128]{1,0:T(8,128)S(1)}, f32[128,128]{1,0:T(8,128)S(1)}, u32[]{:S(2)}, u32[]{:S(2)}) %collective-permute-start.9) | collective-permute-done | bytes 65568 | tf_op jit(solution)/shard_map/ppermute | solution.py:629
  57.6 0.7 %finish.1 = (f32[1,1,1,10,8,256]{5,4,3,2,1,0:T(8,128)}, f32[1,1,2,128]{3,2,1,0:T(2,128)}, f32[1,1,16,128]{3,2,1,0:T(8,128)}) custom-call(f32[160,256]{1,0:T(8,128)S(1)} %get-tuple-element.21.total_ref, f32[128,128]{1,0:T(8,128)S(1)} %collective-permute-done.9.got_ref), custom_call_target="tpu_custom_call" | custom-call | tf_op jit(solution)/shard_map/finish/pallas_call | solution.py:588
  (9 shorter events, 0.2 us)
Async XLA Ops:
  2.0 4.0 %collective-permute-start = (f32[4,2,8,128]{3,0,2,1:T(4,128)S(1)}, f32[4,2,8,128]{3,0,2,1:T(4,128)S(1)}, u32[]{:S(2)}, u32[]{:S(2)}) collective-permute-start(f32[4,2,8,128]{3,0,2,1:T(4,128)S(1)} %fusion), channel_id=1, source_target_pairs={{0,1},{1,0},{2,3},{3,2},{4,5},{5,4},{6,7},{7,6},{8,9},{9,8},{10,11... | collective-permute-start | bytes 98312 | tf_op jit(solution)/shard_map/ppermute | solution.py:629
  6.1 6.2 %collective-permute-start.1 = (f32[4,4,8,128]{3,1,0,2:T(4,128)S(1)}, f32[4,4,8,128]{3,1,0,2:T(4,128)S(1)}, u32[]{:S(2)}, u32[]{:S(2)}) collective-permute-start(f32[4,4,8,128]{3,1,0,2:T(4,128)S(1)} %get-tuple-element.27), channel_id=1, source_target_pairs={{2,4},{4,2},{3,5},{5,3},{10,12},{12,10},{11,13},{13,11},{18,20},{2... | collective-permute-start | bytes 196616 | tf_op jit(solution)/shard_map/ppermute | solution.py:629
  9.6 4.3 %collective-permute-start.2 = (f32[4,4,8,128]{3,1,0,2:T(4,128)S(1)}, f32[4,4,8,128]{3,1,0,2:T(4,128)S(1)}, u32[]{:S(2)}, u32[]{:S(2)}) collective-permute-start(f32[4,4,8,128]{3,1,0,2:T(4,128)S(1)} %get-tuple-element.28), channel_id=1, source_target_pairs={{0,2},{2,0},{4,6},{6,4},{1,3},{3,1},{5,7},{7,5},{8,10},{10,8},{12,... | collective-permute-start | bytes 196616 | tf_op jit(solution)/shard_map/ppermute | solution.py:629
  14.1 5.2 %collective-permute-start.3 = (f32[4,4,4,128]{3,2,1,0:T(4,128)S(1)}, f32[4,4,4,128]{3,2,1,0:T(4,128)S(1)}, u32[]{:S(2)}, u32[]{:S(2)}) collective-permute-start(f32[4,4,4,128]{3,2,1,0:T(4,128)S(1)} %get-tuple-element.23), channel_id=1, source_target_pairs={{8,16},{16,8},{9,17},{17,9},{10,18},{18,10},{11,19},{19,11},{12,20... | collective-permute-start | bytes 98312 | tf_op jit(solution)/shard_map/ppermute | solution.py:629
  16.1 3.3 %collective-permute-start.4 = (f32[4,4,4,128]{3,2,1,0:T(4,128)S(1)}, f32[4,4,4,128]{3,2,1,0:T(4,128)S(1)}, u32[]{:S(2)}, u32[]{:S(2)}) collective-permute-start(f32[4,4,4,128]{3,2,1,0:T(4,128)S(1)} %get-tuple-element.24), channel_id=1, source_target_pairs={{0,8},{8,0},{16,24},{24,16},{1,9},{9,1},{17,25},{25,17},{2,10},{10... | collective-permute-start | bytes 98312 | tf_op jit(solution)/shard_map/ppermute | solution.py:629
  40.8 2.0 %collective-permute-start.5 = (f32[80,128]{1,0:T(8,128)S(1)}, f32[80,128]{1,0:T(8,128)S(1)}, u32[]{:S(2)}, u32[]{:S(2)}) collective-permute-start(f32[80,128]{1,0:T(8,128)S(1)} %get-tuple-element.16), channel_id=1, source_target_pairs={{0,8},{8,0},{16,24},{24,16},{1,9},{9,1},{17,25},{25,17},{2,10},{10... | collective-permute-start | bytes 122888 | tf_op jit(solution)/shard_map/ppermute | solution.py:629
  40.9 5.3 %collective-permute-start.6 = (f32[80,128]{1,0:T(8,128)S(1)}, f32[80,128]{1,0:T(8,128)S(1)}, u32[]{:S(2)}, u32[]{:S(2)}) collective-permute-start(f32[80,128]{1,0:T(8,128)S(1)} %get-tuple-element.17), channel_id=1, source_target_pairs={{8,16},{16,8},{9,17},{17,9},{10,18},{18,10},{11,19},{19,11},{12,20... | collective-permute-start | bytes 122888 | tf_op jit(solution)/shard_map/ppermute | solution.py:629
  46.6 4.5 %collective-permute-start.7 = (f32[160,128]{1,0:T(8,128)S(1)}, f32[160,128]{1,0:T(8,128)S(1)}, u32[]{:S(2)}, u32[]{:S(2)}) collective-permute-start(f32[160,128]{1,0:T(8,128)S(1)} %get-tuple-element.19), channel_id=1, source_target_pairs={{0,2},{2,0},{4,6},{6,4},{1,3},{3,1},{5,7},{7,5},{8,10},{10,8},{12,... | collective-permute-start | bytes 245768 | tf_op jit(solution)/shard_map/ppermute | solution.py:629
  46.7 6.3 %collective-permute-start.8 = (f32[160,128]{1,0:T(8,128)S(1)}, f32[160,128]{1,0:T(8,128)S(1)}, u32[]{:S(2)}, u32[]{:S(2)}) collective-permute-start(f32[160,128]{1,0:T(8,128)S(1)} %get-tuple-element.20), channel_id=1, source_target_pairs={{2,4},{4,2},{3,5},{5,3},{10,12},{12,10},{11,13},{13,11},{18,20},{2... | collective-permute-start | bytes 245768 | tf_op jit(solution)/shard_map/ppermute | solution.py:629
  53.3 4.3 %collective-permute-start.9 = (f32[128,128]{1,0:T(8,128)S(1)}, f32[128,128]{1,0:T(8,128)S(1)}, u32[]{:S(2)}, u32[]{:S(2)}) collective-permute-start(f32[128,128]{1,0:T(8,128)S(1)} %get-tuple-element.22), channel_id=1, source_target_pairs={{0,1},{1,0},{2,3},{3,2},{4,5},{5,4},{6,7},{7,6},{8,9},{9,8},{10,11... | collective-permute-start | bytes 196616 | tf_op jit(solution)/shard_map/ppermute | solution.py:629

commit v4 on v3

--- a/solution.py
+++ b/solution.py
@@ -27,9 +27,10 @@
 
 NB = BOXES_DOWNSLOPE * BOXES_SPANWISE * BOXES_NORMAL
 PITCH_ROWS = NB + 8
-UNROLL = 4
 COLS = CELLS_PER_EDGE * BOXES_DOWNSLOPE * CELLS_PER_EDGE * BOXES_SPANWISE
 CAPS = (16, 12, 16, 12, 14)
+
+KERNEL_VMEM = 32 * 1024 * 1024
 
 F32 = jnp.float32
 BF16 = jnp.bfloat16
@@ -99,7 +100,8 @@
 def box_sort(grains, pairs):
     shapes = [on_chip((7, NB, TILE)), on_chip((4, NB, TILE))]
     listed = pairs.transpose(0, 1, 2, 4, 3).reshape(pairs.shape[4], 1, NB)
-    return plain_call(sort_kernel, shapes, "box_sort", grains.reshape(7, NB, TILE), listed)
+    arrays = (pltpu.with_memory_space_constraint(a, pltpu.HBM) for a in (grains.reshape(7, NB, TILE), listed))
+    return plain_call(sort_kernel, shapes, "box_sort", *arrays)
 
 
 def lane_take(value, index):
@@ -154,8 +156,41 @@
     return tuple(s + t for s, t in zip(sums, terms))
 
 
-def stress_kernel(grid_ref, side_ref, grains_ref, rim0_ref, rim1_ref, out_ref, cand_ref, all_ref, contact_ref, plane_ref, height_ref,
-    feature_ref, moment_ref, own_ref, sum_ref,
+def weights(coords, centres):
+    diff = coords - centres
+    return jnp.maximum(jnp.exp(-0.5 * diff * diff) - CUT_LEVEL, 0.0) * NORM_ONE
+
+
+def centres(places):
+    return (places.astype(F32) - CELLS_PER_EDGE + 0.5) * PITCH
+
+
+def plane_kernel(own_ref, plane_ref):
+    nx = CELLS_PER_EDGE * (BOXES_DOWNSLOPE + 2)
+    ny = CELLS_PER_EDGE * (BOXES_SPANWISE + 2)
+
+    def put_plane(t):
+        wx = weights(own_ref[0, pl.ds(t, 1), :], centres(iota((nx, TILE), 0)))
+        wy = weights(own_ref[1, pl.ds(t, 1), :], centres(iota((ny, TILE), 0)))
+        parts = [wx[x : x + 1] * wy for x in list(range(4)) + list(range(nx - 4, nx))]
+        inner_x = wx[4 : nx - 4]
+        parts += [inner_x * wy[y : y + 1] for y in list(range(4)) + list(range(ny - 4, ny))]
+        inner_y = wy[4 : ny - 4]
+        parts += [wx[x : x + 1] * inner_y for x in range(4, nx - 4)]
+        lanes = pl.ds(pl.multiple_of(t * TILE, TILE), TILE)
+        plane_ref[:, lanes] = jnp.concatenate(parts, axis=0).astype(BF16)
+
+    def four_planes(q, carry):
+        for i in range(4):
+            put_plane(4 * q + i)
+        return carry
+
+    lax.fori_loop(0, NB // 4, four_planes, 0)
+
+
+def stress_kernel(
+    grid_ref, side_ref, grains_ref, plane_ref, rim0_ref, rim1_ref, out_ref,
+    cand_ref, all_ref, contact_ref, height_ref, feature_ref, moment_ref, own_ref, sum_ref, even_ref, odd_ref,
 ):
     tri_row = iota((TILE, 2 * TILE), 0)
     tri_col = iota((TILE, 2 * TILE), 1)
@@ -290,30 +325,9 @@
         overflow = jnp.maximum(overflow, w)
     overflow = jnp.max(overflow)
 
-    nx = CELLS_PER_EDGE * (BOXES_DOWNSLOPE + 2)
-    ny = CELLS_PER_EDGE * (BOXES_SPANWISE + 2)
-
-    def weights(coords, centres):
-        diff = coords - centres
-        return jnp.maximum(jnp.exp(-0.5 * diff * diff) - CUT_LEVEL, 0.0) * NORM_ONE
-
-    def centres(places):
-        return (places.astype(F32) - CELLS_PER_EDGE + 0.5) * PITCH
-
     at_z = iota((8, TILE), 0)
     centres_inner = centres(at_z + 4)
     centres_rim = centres(jnp.where(at_z < 4, at_z, at_z + 8))
-
-    def put_plane(t):
-        wx = weights(grains_ref[pl.ds(t, 1), :], centres(iota((nx, TILE), 0)))
-        wy = weights(grains_ref[pl.ds(NB + t, 1), :], centres(iota((ny, TILE), 0)))
-        parts = [wx[x : x + 1] * wy for x in list(range(4)) + list(range(nx - 4, nx))]
-        inner_x = wx[4 : nx - 4]
-        parts += [inner_x * wy[y : y + 1] for y in list(range(4)) + list(range(ny - 4, ny))]
-        inner_y = wy[4 : ny - 4]
-        parts += [wx[x : x + 1] * inner_y for x in range(4, nx - 4)]
-        lanes = pl.ds(pl.multiple_of(t * TILE, TILE), TILE)
-        plane_ref[:, lanes] = jnp.concatenate(parts, axis=0).astype(BF16)
 
     def put_height(t):
         rows = [grains_ref[pl.ds(r * NB + t, 1), :] for r in range(2, 7)]
@@ -348,53 +362,76 @@
     @pl.when(overflow <= 0.0)
     def _():
         sub = iota((8, TILE), 0)
-
-        def one_tile(t, carry):
-            put_plane(t)
+        starts = [8 * sum(CAPS[:k]) for k in range(5)]
+
+        def own_side(t):
             radii = [own_ref[pl.ds((32 + p) * PITCH_ROWS + t, 1), :] for p in range(3)]
             radii = [jnp.where(sub == 6, jnp.broadcast_to(r, (8, TILE)), 0.0) for r in radii]
             reach = [radii[0], jnp.where(sub >= 5, 1.0, 0.0), radii[1], radii[2]]
-            rhs = jnp.concatenate(
+            return jnp.concatenate(
                 [own_ref[pl.ds(t, 32, stride=PITCH_ROWS), :], jnp.concatenate(reach, axis=0)], axis=1
             ).astype(BF16)
-            highs, lows, moments = [], [], []
+
+        def measure_pairs(t, k, rhs, ref):
+            rows = feature_ref[pl.ds(16 * k * PITCH_ROWS + t, 16, stride=PITCH_ROWS), :]
+            first = rows[:8]
+            lhs = jnp.concatenate([rows, first, first], axis=0).T.astype(BF16)
+            size = 8 * CAPS[k]
+            ref[starts[k] : starts[k] + size, :] = jnp.dot(lhs[:size], rhs, preferred_element_type=F32)
+
+        def forces(k, ref):
+            size = 8 * CAPS[k]
+            square = jnp.maximum(ref[starts[k] : starts[k] + size, :TILE], 1e-12)
+            distance = square * lax.rsqrt(square)
+            overlap = jnp.maximum(ref[starts[k] : starts[k] + size, TILE:] - distance, 0.0)
+            below = distance + SOFTEN
+            guess = pl.reciprocal(below, approx=True)
+            force = overlap * (guess * (2.0 - below * guess))
+            if k == 0:
+                at = iota((TILE, TILE), 0) == iota((TILE, TILE), 1)
+                force = jnp.where(at, 0.0, force)
+            high = force.astype(BF16)
+            low = (force - high.astype(F32)).astype(BF16)
+            rest = TILE - size
+            if rest:
+                none = jnp.zeros((rest, TILE), BF16)
+                high, low = (jnp.concatenate([v, none], axis=0) for v in (high, low))
+            return high, low
+
+        def add_up(t, parts):
+            moments = []
             for k in range(5):
-                rows = feature_ref[pl.ds(16 * k * PITCH_ROWS + t, 16, stride=PITCH_ROWS), :]
-                first = rows[:8]
-                lhs = jnp.concatenate([rows, first, first], axis=0).T.astype(BF16)
-                both = jnp.dot(lhs[: 8 * CAPS[k]], rhs, preferred_element_type=F32)
-                square = jnp.maximum(both[:, :TILE], 1e-12)
-                distance = square * lax.rsqrt(square)
-                overlap = jnp.maximum(both[:, TILE:] - distance, 0.0)
-                below = distance + SOFTEN
-                guess = pl.reciprocal(below, approx=True)
-                force = overlap * (guess * (2.0 - below * guess))
-                if k == 0:
-                    at = iota((TILE, TILE), 0) == iota((TILE, TILE), 1)
-                    force = jnp.where(at, 0.0, force)
-                high = force.astype(BF16)
-                low = (force - high.astype(F32)).astype(BF16)
-                rest = TILE - 8 * CAPS[k]
-                highs.append(high)
-                lows.append(low)
-                if rest:
-                    highs.append(jnp.zeros((rest, TILE), BF16))
-                    lows.append(jnp.zeros((rest, TILE), BF16))
+                first = feature_ref[pl.ds(16 * k * PITCH_ROWS + t, 8, stride=PITCH_ROWS), :]
                 more = moment_ref[pl.ds(16 * k * PITCH_ROWS + t, 16, stride=PITCH_ROWS), :]
                 moments.append(jnp.concatenate([first, more, first], axis=0))
             lhs = jnp.concatenate(moments, axis=1).astype(BF16)
-            one = jnp.dot(lhs, jnp.concatenate(highs, axis=0), preferred_element_type=F32)
-            two = jnp.dot(lhs[:16], jnp.concatenate(lows, axis=0), preferred_element_type=F32)
+            highs = jnp.concatenate([p[0] for p in parts], axis=0)
+            lows = jnp.concatenate([p[1] for p in parts], axis=0)
+            one = jnp.dot(lhs, highs, preferred_element_type=F32)
+            two = jnp.dot(lhs[:16], lows, preferred_element_type=F32)
             sum_ref[pl.ds(t, 8, stride=PITCH_ROWS), :] = one[:8] + two[:8]
             sum_ref[pl.ds(8 * PITCH_ROWS + t, 8, stride=PITCH_ROWS), :] = one[8:16] + (one[16:24] + two[8:])
+
+        def step(t, here_ref, next_t, next_ref):
+            rhs = own_side(next_t)
+            parts = []
+            for k in range(5):
+                measure_pairs(next_t, k, rhs, next_ref)
+                parts.append(forces(k, here_ref))
+            add_up(t, parts)
+
+        first_rhs = own_side(0)
+        for k in range(5):
+            measure_pairs(0, k, first_rhs, even_ref)
+
+        def four_tiles(q, carry):
+            step(4 * q, even_ref, 4 * q + 1, odd_ref)
+            step(4 * q + 1, odd_ref, 4 * q + 2, even_ref)
+            step(4 * q + 2, even_ref, 4 * q + 3, odd_ref)
+            step(4 * q + 3, odd_ref, jnp.minimum(4 * q + 4, NB - 1), even_ref)
             return carry
 
-        def some_tiles(q, carry):
-            for i in range(UNROLL):
-                one_tile(UNROLL * q + i, carry)
-            return carry
-
-        lax.fori_loop(0, NB // UNROLL, some_tiles, 0)
+        lax.fori_loop(0, NB // 4, four_tiles, 0)
         total = [sum_ref[m * PITCH_ROWS : m * PITCH_ROWS + NB, :] for m in range(14)]
         first = [total[c] + total[3 + c] for c in range(3)]
         own_mid = [own_ref[(35 + c) * PITCH_ROWS : (35 + c) * PITCH_ROWS + NB, :] for c in range(3)]
@@ -432,7 +469,6 @@
                 return sums
 
             put(t, lax.fori_loop(0, 27, one_near, zeros))
-            put_plane(t)
             return carry
 
         lax.fori_loop(0, NB, one_tile, 0)
@@ -455,8 +491,7 @@
     rim1_ref[...] = jnp.where(left_half, pltpu.roll(upper, 64, 1), lower)
 
 
-def stress_and_deposit(grid, side, grains):
-    columns = 3 * TILE + COLS
+def stress_and_deposit(grid, side, grains, plane):
     return plain_call(
         stress_kernel,
         [on_chip((80, TILE)), on_chip((80, TILE)), on_chip((160, 2 * TILE + COLS))],
@@ -464,16 +499,18 @@
         held(grid),
         held(side),
         held(grains),
+        held(plane),
         scratch=[
             pltpu.VMEM((4 * NB, TILE), F32),
             pltpu.VMEM((8 * 160, TILE), F32),
             pltpu.VMEM((6 * NB, TILE), F32),
-            pltpu.VMEM((columns, NB * TILE), BF16),
             pltpu.VMEM((160, NB * TILE), BF16),
             pltpu.VMEM((5 * 16 * PITCH_ROWS, TILE), F32),
             pltpu.VMEM((5 * 16 * PITCH_ROWS, TILE), F32),
             pltpu.VMEM((38 * PITCH_ROWS, TILE), F32),
             pltpu.VMEM((16 * PITCH_ROWS, TILE), F32),
+            pltpu.VMEM((8 * sum(CAPS), 2 * TILE), F32),
+            pltpu.VMEM((8 * sum(CAPS), 2 * TILE), F32),
         ],
     )
 
@@ -579,8 +616,8 @@
     return pltpu.with_memory_space_constraint(array, pltpu.VMEM)
 
 
-def on_chip(shape):
-    return pltpu.VMEM(shape, F32)
+def on_chip(shape, dtype=F32):
+    return pltpu.VMEM(shape, dtype)
 
 
 def plain_call(kernel, shapes, name, *args, scratch=()):
@@ -591,6 +628,7 @@
         in_specs=[vmem] * len(args),
         out_specs=jax.tree.map(lambda _: vmem, shapes),
         scratch_shapes=scratch,
+        compiler_params=pltpu.CompilerParams(vmem_limit_bytes=KERNEL_VMEM),
         name=name,
     )(*args)
 
@@ -641,11 +679,17 @@
     cube = near.reshape(4, 2, 2, 8, TILE)
     below, above = exchange(cube[:, 0], cube[:, 1], "gz")
     cube = jnp.concatenate([below[:, None], cube, above[:, None]], axis=1)
-    below, above = exchange(cube[:, :, 0], cube[:, :, 1], "gy")
+    sends = (cube[:, :, 0], cube[:, :, 1])
+    sends, placed = lax.optimization_barrier((sends, own))
+    plane = plain_call(
+        plane_kernel, on_chip((3 * TILE + COLS, NB * TILE), BF16), "plane", held(placed)
+    )
+    below, above = exchange(*sends, "gy")
     cube = jnp.concatenate([below[:, :, None], cube, above[:, :, None]], axis=2)
+    cube, plane = lax.optimization_barrier((cube, plane))
     below, above = exchange(cube[:, :, :, 0], cube[:, :, :, 7], "gx")
     side = jnp.stack([below, above]).reshape(2, 4, 16, TILE)
-    rim0, rim1, wide = stress_and_deposit(cube.reshape(4, 128, TILE), side, own.reshape(7 * NB, TILE))
+    rim0, rim1, wide = stress_and_deposit(cube.reshape(4, 128, TILE), side, own.reshape(7 * NB, TILE), plane)
     first, second = swaps(rim0, rim1, "gx")
     block, square = on_chip((160, TILE)), on_chip((160, COLS))
     rim0, rim1, inner = plain_call(

time: 58.4 us -> 53.5 us (0.916)
  waiting for transfers between devices: 19.6 us -> 16 us
  Pallas kernels: 23.9 us -> 21.2 us
  starting transfers between devices: 13.1 us -> 14.7 us
    ppermute x10, waiting for transfers between devices: 19.6 us -> 16 us  [swaps(): lax.ppermute(value, axis, links)]
    pallas_call x5 -> x6, Pallas kernels: 23.9 us -> 21.2 us  [plain_call(): pl.pallas_call(kernel, out_shape=shapes, in_specs=[vmem] * len(args), out...]
    ppermute x10, starting transfers between devices: 13.1 us -> 14.7 us  [swaps(): lax.ppermute(value, axis, links)]
  transfers between devices with their start and end apart: 10 -> 10, of which waited for: 8 -> 7; matrix products, arithmetic and copies ran while one was open for 1% -> 1% of each run, Pallas kernels for 0% -> 7%
where the time goes in v4:
time: 53.5 us; the launch traced here: 53.3 us
  Pallas kernels  21.2 us (40%)
  waiting for transfers between devices  16 us (30%)
  starting transfers between devices  14.7 us (27%)
  between operations  0.86 us (2%)
    pallas_call x6, Pallas kernels, plain_call(): pl.pallas_call(kernel, out_shape=shapes, in_specs=[vmem] * len(args), out...  21.2 us
    ppermute x10, waiting for transfers between devices, swaps(): lax.ppermute(value, axis, links)  16 us
    ppermute x10, starting transfers between devices, swaps(): lax.ppermute(value, axis, links)  14.7 us
  transfers between devices with their start and end apart: 10, of which 7 were waited for; matrix products, arithmetic and copies ran while one was open for 1% of the time, Pallas kernels for 7%

profile of v4, /device:TPU:10, one launch (start us, length us, event | category | flops | bytes accessed | tf_op | source)
XLA Modules:
  0.0 53.3 jit_solution(7219098979728723479)
XLA Ops:
  0.6 1.3 %box_sort.1 = (f32[7,32,128]{2,1,0:T(8,128)S(1)}, f32[4,32,128]{2,1,0:T(8,128)S(1)}) custom-call(f32[7,32,128]{2,1,0:T(8,128)} %bitcast.53, s32[27,1,32]{2,1,0:T(1,128)} %bitcast.60), custom_call_target="tpu_custom_call" | custom-call | tf_op jit(solution)/shard_map/box_sort/pallas_call | solution.py:625
  2.0 1.6 %collective-permute-start = (f32[4,2,8,128]{3,0,2,1:T(4,128)S(1)}, f32[4,2,8,128]{3,0,2,1:T(4,128)S(1)}, u32[]{:S(2)}, u32[]{:S(2)}) collective-permute-start(f32[4,2,8,128]{3,0,2,1:T(4,128)S(1)} %fusion), channel_id=1, source_target_pairs={{0,1},{1,0},{2,3},{3,2},{4,5},{5,4},{6,7},{7,6},{8,9},{9,8},{10,11... | collective-permute-start | bytes 98312 | tf_op jit(solution)/shard_map/ppermute | solution.py:667
  3.6 2.4 %collective-permute-done = f32[4,2,8,128]{3,0,2,1:T(4,128)S(1)} collective-permute-done((f32[4,2,8,128]{3,0,2,1:T(4,128)S(1)}, f32[4,2,8,128]{3,0,2,1:T(4,128)S(1)}, u32[]{:S(2)}, u32[]{:S(2)}) %collective-permute-start) | collective-permute-done | bytes 32800 | tf_op jit(solution)/shard_map/ppermute | solution.py:667
  6.0 0.1 pad_maximum_fusion.1
  6.1 3.5 %collective-permute-start.1 = (f32[4,4,8,128]{3,1,0,2:T(4,128)S(1)}, f32[4,4,8,128]{3,1,0,2:T(4,128)S(1)}, u32[]{:S(2)}, u32[]{:S(2)}) collective-permute-start(f32[4,4,8,128]{3,1,0,2:T(4,128)S(1)} %bitcast.57), channel_id=1, source_target_pairs={{2,4},{4,2},{3,5},{5,3},{10,12},{12,10},{11,13},{13,11},{18,20},{2... | collective-permute-start | bytes 196616 | tf_op jit(solution)/shard_map/ppermute | solution.py:667
  9.6 0.1 collective-permute-start.2
  9.7 0.1 copy.11
  9.8 3.6 %plane.1.plane_ref = bf16[640,4096]{1,0:T(8,128)(2,1)S(1)} custom-call(f32[7,32,128]{2,1,0:T(8,128)S(1)} %get-tuple-element.22.own_ref), custom_call_target="tpu_custom_call" | custom-call | tf_op jit(solution)/shard_map/plane/pallas_call | solution.py:625
  13.4 0.0 collective-permute-done.1
  13.5 0.5 collective-permute-done.2
  13.9 0.2 pad_maximum_fusion
  14.1 1.9 %collective-permute-start.3 = (f32[4,4,4,128]{3,2,1,0:T(4,128)S(1)}, f32[4,4,4,128]{3,2,1,0:T(4,128)S(1)}, u32[]{:S(2)}, u32[]{:S(2)}) collective-permute-start(f32[4,4,4,128]{3,2,1,0:T(4,128)S(1)} %get-tuple-element.33), channel_id=1, source_target_pairs={{8,16},{16,8},{9,17},{17,9},{10,18},{18,10},{11,19},{19,11},{12,20... | collective-permute-start | bytes 98312 | tf_op jit(solution)/shard_map/ppermute | solution.py:667
  16.1 0.1 collective-permute-start.4
  16.1 0.2 copy.12
  16.3 3.1 %collective-permute-done.3 = f32[4,4,4,128]{3,2,1,0:T(4,128)S(1)} collective-permute-done((f32[4,4,4,128]{3,2,1,0:T(4,128)S(1)}, f32[4,4,4,128]{3,2,1,0:T(4,128)S(1)}, u32[]{:S(2)}, u32[]{:S(2)}) %collective-permute-start.3) | collective-permute-done | bytes 32800 | tf_op jit(solution)/shard_map/ppermute | solution.py:667
  19.4 0.0 collective-permute-done.4
  19.4 15.0 %stress_deposit.1 = (f32[80,128]{1,0:T(8,128)S(1)}, f32[80,128]{1,0:T(8,128)S(1)}, f32[160,512]{1,0:T(8,128)S(1)}) custom-call(f32[4,128,128]{2,1,0:T(8,128)S(1)} %bitcast.41, f32[2,4,16,128]{3,2,1,0:T(8,128)S(1)} %pad_maximum_fusion.2.side_ref, f32[224,128]{1,0:T(8,128)S(1)} %bitcast.42, bf16[640,4096]{1,0:T(8,128)(2,1)S(1)} %plane.1.plane_ref), custom_call_target="tpu_custom_call" | custom-call | tf_op jit(solution)/shard_map/stress_deposit/pallas_call | solution.py:625
  34.4 0.1 collective-permute-start.5
  34.5 1.9 %collective-permute-start.6 = (f32[80,128]{1,0:T(8,128)S(1)}, f32[80,128]{1,0:T(8,128)S(1)}, u32[]{:S(2)}, u32[]{:S(2)}) collective-permute-start(f32[80,128]{1,0:T(8,128)S(1)} %get-tuple-element.27), channel_id=1, source_target_pairs={{8,16},{16,8},{9,17},{17,9},{10,18},{18,10},{11,19},{19,11},{12,20... | collective-permute-start | bytes 122888 | tf_op jit(solution)/shard_map/ppermute | solution.py:667
  36.4 0.0 collective-permute-done.5.first_ref
  36.4 3.4 %collective-permute-done.6.second_ref = f32[80,128]{1,0:T(8,128)S(1)} collective-permute-done((f32[80,128]{1,0:T(8,128)S(1)}, f32[80,128]{1,0:T(8,128)S(1)}, u32[]{:S(2)}, u32[]{:S(2)}) %collective-permute-start.6) | collective-permute-done | bytes 40992 | tf_op jit(solution)/shard_map/ppermute | solution.py:667
  39.8 0.4 rim_x.1
  40.2 1.6 %collective-permute-start.7 = (f32[160,128]{1,0:T(8,128)S(1)}, f32[160,128]{1,0:T(8,128)S(1)}, u32[]{:S(2)}, u32[]{:S(2)}) collective-permute-start(f32[160,128]{1,0:T(8,128)S(1)} %get-tuple-element.29), channel_id=1, source_target_pairs={{0,2},{2,0},{4,6},{6,4},{1,3},{3,1},{5,7},{7,5},{8,10},{10,8},{12,... | collective-permute-start | bytes 245768 | tf_op jit(solution)/shard_map/ppermute | solution.py:667
  41.8 2.3 %collective-permute-start.8 = (f32[160,128]{1,0:T(8,128)S(1)}, f32[160,128]{1,0:T(8,128)S(1)}, u32[]{:S(2)}, u32[]{:S(2)}) collective-permute-start(f32[160,128]{1,0:T(8,128)S(1)} %get-tuple-element.30), channel_id=1, source_target_pairs={{2,4},{4,2},{3,5},{5,3},{10,12},{12,10},{11,13},{13,11},{18,20},{2... | collective-permute-start | bytes 245768 | tf_op jit(solution)/shard_map/ppermute | solution.py:667
  44.1 0.5 %collective-permute-done.7.first_ref = f32[160,128]{1,0:T(8,128)S(1)} collective-permute-done((f32[160,128]{1,0:T(8,128)S(1)}, f32[160,128]{1,0:T(8,128)S(1)}, u32[]{:S(2)}, u32[]{:S(2)}) %collective-permute-start.7) | collective-permute-done | bytes 81952 | tf_op jit(solution)/shard_map/ppermute | solution.py:667
  44.7 3.4 %collective-permute-done.8.second_ref = f32[160,128]{1,0:T(8,128)S(1)} collective-permute-done((f32[160,128]{1,0:T(8,128)S(1)}, f32[160,128]{1,0:T(8,128)S(1)}, u32[]{:S(2)}, u32[]{:S(2)}) %collective-permute-start.8) | collective-permute-done | bytes 81952 | tf_op jit(solution)/shard_map/ppermute | solution.py:667
  48.1 0.3 rim_y.1
  48.3 1.6 %collective-permute-start.9 = (f32[128,128]{1,0:T(8,128)S(1)}, f32[128,128]{1,0:T(8,128)S(1)}, u32[]{:S(2)}, u32[]{:S(2)}) collective-permute-start(f32[128,128]{1,0:T(8,128)S(1)} %get-tuple-element.32), channel_id=1, source_target_pairs={{0,1},{1,0},{2,3},{3,2},{4,5},{5,4},{6,7},{7,6},{8,9},{9,8},{10,11... | collective-permute-start | bytes 196616 | tf_op jit(solution)/shard_map/ppermute | solution.py:667
  49.9 2.7 %collective-permute-done.9.got_ref = f32[128,128]{1,0:T(8,128)S(1)} collective-permute-done((f32[128,128]{1,0:T(8,128)S(1)}, f32[128,128]{1,0:T(8,128)S(1)}, u32[]{:S(2)}, u32[]{:S(2)}) %collective-permute-start.9) | collective-permute-done | bytes 65568 | tf_op jit(solution)/shard_map/ppermute | solution.py:667
  52.7 0.7 %finish.1 = (f32[1,1,1,10,8,256]{5,4,3,2,1,0:T(8,128)}, f32[1,1,2,128]{3,2,1,0:T(2,128)}, f32[1,1,16,128]{3,2,1,0:T(8,128)}) custom-call(f32[160,256]{1,0:T(8,128)S(1)} %get-tuple-element.31.total_ref, f32[128,128]{1,0:T(8,128)S(1)} %collective-permute-done.9.got_ref), custom_call_target="tpu_custom_call" | custom-call | tf_op jit(solution)/shard_map/finish/pallas_call | solution.py:625
  (10 shorter events, 0.2 us)
Async XLA Ops:
  2.0 4.0 %collective-permute-start = (f32[4,2,8,128]{3,0,2,1:T(4,128)S(1)}, f32[4,2,8,128]{3,0,2,1:T(4,128)S(1)}, u32[]{:S(2)}, u32[]{:S(2)}) collective-permute-start(f32[4,2,8,128]{3,0,2,1:T(4,128)S(1)} %fusion), channel_id=1, source_target_pairs={{0,1},{1,0},{2,3},{3,2},{4,5},{5,4},{6,7},{7,6},{8,9},{9,8},{10,11... | collective-permute-start | bytes 98312 | tf_op jit(solution)/shard_map/ppermute | solution.py:667
  6.1 7.4 %collective-permute-start.1 = (f32[4,4,8,128]{3,1,0,2:T(4,128)S(1)}, f32[4,4,8,128]{3,1,0,2:T(4,128)S(1)}, u32[]{:S(2)}, u32[]{:S(2)}) collective-permute-start(f32[4,4,8,128]{3,1,0,2:T(4,128)S(1)} %bitcast.57), channel_id=1, source_target_pairs={{2,4},{4,2},{3,5},{5,3},{10,12},{12,10},{11,13},{13,11},{18,20},{2... | collective-permute-start | bytes 196616 | tf_op jit(solution)/shard_map/ppermute | solution.py:667
  9.6 4.3 %collective-permute-start.2 = (f32[4,4,8,128]{3,1,0,2:T(4,128)S(1)}, f32[4,4,8,128]{3,1,0,2:T(4,128)S(1)}, u32[]{:S(2)}, u32[]{:S(2)}) collective-permute-start(f32[4,4,8,128]{3,1,0,2:T(4,128)S(1)} %bitcast.55), channel_id=1, source_target_pairs={{0,2},{2,0},{4,6},{6,4},{1,3},{3,1},{5,7},{7,5},{8,10},{10,8},{12,... | collective-permute-start | bytes 196616 | tf_op jit(solution)/shard_map/ppermute | solution.py:667
  14.1 5.2 %collective-permute-start.3 = (f32[4,4,4,128]{3,2,1,0:T(4,128)S(1)}, f32[4,4,4,128]{3,2,1,0:T(4,128)S(1)}, u32[]{:S(2)}, u32[]{:S(2)}) collective-permute-start(f32[4,4,4,128]{3,2,1,0:T(4,128)S(1)} %get-tuple-element.33), channel_id=1, source_target_pairs={{8,16},{16,8},{9,17},{17,9},{10,18},{18,10},{11,19},{19,11},{12,20... | collective-permute-start | bytes 98312 | tf_op jit(solution)/shard_map/ppermute | solution.py:667
  16.1 3.3 %collective-permute-start.4 = (f32[4,4,4,128]{3,2,1,0:T(4,128)S(1)}, f32[4,4,4,128]{3,2,1,0:T(4,128)S(1)}, u32[]{:S(2)}, u32[]{:S(2)}) collective-permute-start(f32[4,4,4,128]{3,2,1,0:T(4,128)S(1)} %get-tuple-element.34), channel_id=1, source_target_pairs={{0,8},{8,0},{16,24},{24,16},{1,9},{9,1},{17,25},{25,17},{2,10},{10... | collective-permute-start | bytes 98312 | tf_op jit(solution)/shard_map/ppermute | solution.py:667
  34.4 2.0 %collective-permute-start.5 = (f32[80,128]{1,0:T(8,128)S(1)}, f32[80,128]{1,0:T(8,128)S(1)}, u32[]{:S(2)}, u32[]{:S(2)}) collective-permute-start(f32[80,128]{1,0:T(8,128)S(1)} %get-tuple-element.26), channel_id=1, source_target_pairs={{0,8},{8,0},{16,24},{24,16},{1,9},{9,1},{17,25},{25,17},{2,10},{10... | collective-permute-start | bytes 122888 | tf_op jit(solution)/shard_map/ppermute | solution.py:667
  34.5 5.3 %collective-permute-start.6 = (f32[80,128]{1,0:T(8,128)S(1)}, f32[80,128]{1,0:T(8,128)S(1)}, u32[]{:S(2)}, u32[]{:S(2)}) collective-permute-start(f32[80,128]{1,0:T(8,128)S(1)} %get-tuple-element.27), channel_id=1, source_target_pairs={{8,16},{16,8},{9,17},{17,9},{10,18},{18,10},{11,19},{19,11},{12,20... | collective-permute-start | bytes 122888 | tf_op jit(solution)/shard_map/ppermute | solution.py:667
  40.2 4.5 %collective-permute-start.7 = (f32[160,128]{1,0:T(8,128)S(1)}, f32[160,128]{1,0:T(8,128)S(1)}, u32[]{:S(2)}, u32[]{:S(2)}) collective-permute-start(f32[160,128]{1,0:T(8,128)S(1)} %get-tuple-element.29), channel_id=1, source_target_pairs={{0,2},{2,0},{4,6},{6,4},{1,3},{3,1},{5,7},{7,5},{8,10},{10,8},{12,... | collective-permute-start | bytes 245768 | tf_op jit(solution)/shard_map/ppermute | solution.py:667
  41.8 6.3 %collective-permute-start.8 = (f32[160,128]{1,0:T(8,128)S(1)}, f32[160,128]{1,0:T(8,128)S(1)}, u32[]{:S(2)}, u32[]{:S(2)}) collective-permute-start(f32[160,128]{1,0:T(8,128)S(1)} %get-tuple-element.30), channel_id=1, source_target_pairs={{2,4},{4,2},{3,5},{5,3},{10,12},{12,10},{11,13},{13,11},{18,20},{2... | collective-permute-start | bytes 245768 | tf_op jit(solution)/shard_map/ppermute | solution.py:667
  48.3 4.3 %collective-permute-start.9 = (f32[128,128]{1,0:T(8,128)S(1)}, f32[128,128]{1,0:T(8,128)S(1)}, u32[]{:S(2)}, u32[]{:S(2)}) collective-permute-start(f32[128,128]{1,0:T(8,128)S(1)} %get-tuple-element.32), channel_id=1, source_target_pairs={{0,1},{1,0},{2,3},{3,2},{4,5},{5,4},{6,7},{7,6},{8,9},{9,8},{10,11... | collective-permute-start | bytes 196616 | tf_op jit(solution)/shard_map/ppermute | solution.py:667

commit v5 on v4

--- a/solution.py
+++ b/solution.py
@@ -121,23 +121,30 @@
     masks = [jnp.where(mask, 1.0, 0.0).astype(BF16) for lists in groups for mask, _ in lists]
     both = jnp.dot(jnp.concatenate(masks, axis=0), tri, preferred_element_type=F32)
     rows = masks[0].shape[0]
-    lane_f = iota((rows, TILE), 1).astype(F32)
-    packed, at = [], 0
+    ranks = both[:, :TILE]
+    totals = [both[n * rows : (n + 1) * rows, TILE:] for n in range(len(masks))]
+    offsets, ends, at = [], [], 0
     for lists in groups:
         offset = jnp.zeros((rows, TILE), F32)
+        for _ in lists:
+            offsets.append(offset)
+            offset = offset + totals[at]
+            at += 1
+        ends.append(offset)
+    lane_f = iota((rows, TILE), 1).astype(F32)
+    wanted = jnp.concatenate([lane_f - offset for offset in offsets], axis=0)
+    place = jnp.zeros(wanted.shape, jnp.int32)
+    for bit in (64, 32, 16, 8, 4, 2, 1):
+        place = jnp.where(lane_take(ranks, place + (bit - 1)) <= wanted, place + bit, place)
+    packed, at = [], 0
+    for lists, end in zip(groups, ends):
         outs = [jnp.zeros((rows, TILE), F32)] * 3 + [jnp.full((rows, TILE), ABSENT, F32)]
         for _, arrays in lists:
-            ranks, total = both[at : at + rows, :TILE], both[at : at + rows, TILE:]
-            at += rows
-            wanted = lane_f - offset
-            place = jnp.zeros((rows, TILE), jnp.int32)
-            for bit in (64, 32, 16, 8, 4, 2, 1):
-                probe = lane_take(ranks, place + (bit - 1))
-                place = jnp.where(probe <= wanted, place + bit, place)
-            ours = (wanted >= 0.0) & (wanted < total)
-            outs = [jnp.where(ours, lane_take(a, place), o) for a, o in zip(arrays, outs)]
-            offset = offset + total
-        packed.append((outs, offset))
+            here = slice(at * rows, (at + 1) * rows)
+            ours = (wanted[here] >= 0.0) & (wanted[here] < totals[at])
+            outs = [jnp.where(ours, lane_take(v, place[here]), o) for v, o in zip(arrays, outs)]
+            at += 1
+        packed.append((outs, end))
     return packed
 
 
@@ -188,113 +195,73 @@
     lax.fori_loop(0, NB // 4, four_planes, 0)
 
 
-def stress_kernel(
-    grid_ref, side_ref, grains_ref, plane_ref, rim0_ref, rim1_ref, out_ref,
-    cand_ref, all_ref, contact_ref, height_ref, feature_ref, moment_ref, own_ref, sum_ref, even_ref, odd_ref,
-):
-    tri_row = iota((TILE, 2 * TILE), 0)
-    tri_col = iota((TILE, 2 * TILE), 1)
-    tri = jnp.where((tri_row <= tri_col) | (tri_col >= TILE), 1.0, 0.0).astype(BF16)
-
-    span_x = BOXES_DOWNSLOPE * TILE_BOX_EDGE
-    span_y = BOXES_SPANWISE * TILE_BOX_EDGE
-    span_z = BOXES_NORMAL * TILE_BOX_EDGE
-
-    def shifts(place, span):
-        return jnp.where(place == 0, -span, jnp.where(place == 3, span, 0.0))
-
-    def alive(radius):
-        return jnp.where(radius == 0.0, ABSENT, radius)
-
+SPAN_X = BOXES_DOWNSLOPE * TILE_BOX_EDGE
+SPAN_Y = BOXES_SPANWISE * TILE_BOX_EDGE
+SPAN_Z = BOXES_NORMAL * TILE_BOX_EDGE
+
+
+def running_sums():
+    row, col = iota((TILE, 2 * TILE), 0), iota((TILE, 2 * TILE), 1)
+    return jnp.where((row <= col) | (col >= TILE), 1.0, 0.0).astype(BF16)
+
+
+def shifts(place, span):
+    return jnp.where(place == 0, -span, jnp.where(place == 3, span, 0.0))
+
+
+def alive(radius):
+    return jnp.where(radius == 0.0, ABSENT, radius)
+
+
+def near(arrays, axis, low, step):
+    limit = arrays[axis] >= low - REACH if step < 0 else arrays[axis] <= low + (TILE_BOX_EDGE + REACH)
+    return limit & (arrays[3] > 0.0), arrays
+
+
+def in_this_frame(grid_ref):
     row = iota((128, TILE), 0)
-    low_x = TILE_BOX_EDGE * (row & 7).astype(F32)
-    low_y = TILE_BOX_EDGE * ((iota((64, TILE), 0) >> 3) & 1).astype(F32)
-    low_z = TILE_BOX_EDGE * (iota((32, TILE), 0) >> 4).astype(F32)
-    here = [
+    return [
         grid_ref[0],
-        grid_ref[1] + shifts((row >> 3) & 3, span_y),
-        grid_ref[2] + shifts(row >> 5, span_z),
+        grid_ref[1] + shifts((row >> 3) & 3, SPAN_Y),
+        grid_ref[2] + shifts(row >> 5, SPAN_Z),
         alive(grid_ref[3]),
     ]
-    side_row = iota((16, TILE), 0)
-    sides = []
-    for k, shift_x in ((0, -span_x), (1, span_x)):
-        sides.append(
-            [
-                side_ref[k, 0] + shift_x,
-                side_ref[k, 1] + shifts(side_row & 3, span_y),
-                side_ref[k, 2] + shifts(side_row >> 2, span_z),
-                alive(side_ref[k, 3]),
-            ]
-        )
-    in_box_x = iota((16, 8, TILE), 1)
-
-    def neighbours(centre, edge, step):
-        cube = centre.reshape(16, 8, TILE)
-        moved = pltpu.roll(cube, 1 if step < 0 else 7, 1)
-        at_edge = in_box_x == (0 if step < 0 else 7)
-        return jnp.where(at_edge, edge[:, None, :], moved).reshape(128, TILE)
-
-    def near(arrays, axis, low, step):
-        limit = arrays[axis] >= low - REACH if step < 0 else arrays[axis] <= low + (TILE_BOX_EDGE + REACH)
-        return limit & (arrays[3] > 0.0), arrays
-
-    def cut_y(arrays, start):
-        return [a.reshape(4, 4, 8, TILE)[:, start : start + 2].reshape(64, TILE) for a in arrays]
-
-    def cut_z(arrays, start):
-        return [a[16 * start : 16 * start + 32] for a in arrays]
-
-    before = [neighbours(c, e, -1) for c, e in zip(here, sides[0])]
-    after = [neighbours(c, e, 1) for c, e in zip(here, sides[1])]
-    ((beside_x, count_x),) = pack([[near(before, 0, low_x, -1), near(after, 0, low_x, 1)]], tri)
-    ((beside_y, count_y),) = pack(
+
+
+def beside_in_this_frame(side_ref):
+    row = iota((16, TILE), 0)
+    return [
         [
-            [
-                near(cut_y(here, 0), 1, low_y, -1),
-                near(cut_y(beside_x, 0), 1, low_y, -1),
-                near(cut_y(here, 2), 1, low_y, 1),
-                near(cut_y(beside_x, 2), 1, low_y, 1),
-            ]
-        ],
-        tri,
-    )
-    mid, mid_x = cut_y(here, 1), cut_y(beside_x, 1)
-    (above, count_z), (above_rest, count_w) = pack(
-        [
-            [near(cut_z(mid, 0), 2, low_z, -1), near(cut_z(mid, 2), 2, low_z, 1)],
-            [
-                near(cut_z(mid_x, 0), 2, low_z, -1),
-                near(cut_z(beside_y, 0), 2, low_z, -1),
-                near(cut_z(mid_x, 2), 2, low_z, 1),
-                near(cut_z(beside_y, 2), 2, low_z, 1),
-            ],
-        ],
-        tri,
-    )
-    worst = [
-        jnp.max(count, axis=0, keepdims=True) - 8.0 * cap
-        for count, cap in zip((count_x, count_y, count_z, count_w), CAPS[1:])
+            side_ref[k, 0] + shift_x,
+            side_ref[k, 1] + shifts(row & 3, SPAN_Y),
+            side_ref[k, 2] + shifts(row >> 2, SPAN_Z),
+            alive(side_ref[k, 3]),
+        ]
+        for k, shift_x in ((0, -SPAN_X), (1, SPAN_X))
     ]
 
-    def keep(ref, first, values):
-        for f, value in enumerate(values):
-            at = (first + f) * PITCH_ROWS
-            ref[at : at + NB, :] = value
-
+
+def parts(value):
+    return [p.astype(F32) for p in split3(value)]
+
+
+def keep(ref, first, values):
+    for f, value in enumerate(values):
+        at = (first + f) * PITCH_ROWS
+        ref[at : at + NB, :] = value
+
+
+def keep_chunks(chunks, feature_ref, moment_ref, own_ref=None):
     half_box = 0.5 * TILE_BOX_EDGE
     ones = jnp.ones((NB, TILE), F32)
     none = jnp.zeros((NB, TILE), F32)
-
-    def parts(value):
-        return [p.astype(F32) for p in split3(value)]
-
+    tile = iota((NB, TILE), 0)
     middle = [
-        TILE_BOX_EDGE * (iota((NB, TILE), 0) & 7).astype(F32) + half_box,
-        TILE_BOX_EDGE * ((iota((NB, TILE), 0) >> 3) & 1).astype(F32) + half_box,
-        low_z + half_box,
+        TILE_BOX_EDGE * (tile & 7).astype(F32) + half_box,
+        TILE_BOX_EDGE * ((tile >> 3) & 1).astype(F32) + half_box,
+        TILE_BOX_EDGE * (tile >> 4).astype(F32) + half_box,
     ]
-    for k, chunk in enumerate((cut_z(mid, 1), cut_z(mid_x, 1), cut_z(beside_y, 1), above, above_rest)):
+    for k, chunk in enumerate(chunks):
         x, y, z = (chunk[c] - middle[c] for c in range(3))
         squares = [x * x, y * y, z * z]
         norm = squares[0] + squares[1] + squares[2]
@@ -308,9 +275,7 @@
         highs = [v.astype(BF16).astype(F32) for v in products]
         lows = [v - h for v, h in zip(products, highs)]
         keep(moment_ref, 16 * k, highs + [none] * 2 + lows + [none] * 2)
-        if k == 0:
-            for c in range(4):
-                cand_ref[c * NB : c * NB + NB, :] = chunk[c]
+        if own_ref is not None and k == 0:
             xi, yi, zi = ([-2.0 * p for p in v] for v in (xs, ys, zs))
             keep(
                 own_ref, 0,
@@ -320,10 +285,116 @@
                 + [xi[2], yi[2], zi[2], none, none, none, ns[2], none]
                 + rs + [x, y, z],
             )
-    overflow = worst[0]
-    for w in worst[1:]:
-        overflow = jnp.maximum(overflow, w)
+
+
+def excess(counts, caps):
+    worst = [jnp.max(n, axis=0, keepdims=True) - 8.0 * cap for n, cap in zip(counts, caps)]
+    while len(worst) > 1:
+        worst = [jnp.maximum(worst[0], worst[1])] + worst[2:]
+    return worst[0]
+
+
+def pick_rows(arrays, starts, size):
+    return [jnp.concatenate([v[at : at + size] for at in starts], axis=0) for v in arrays]
+
+
+def near_kernel(grid_ref, lists_ref, excess_ref, feature_ref, moment_ref, own_ref):
+    tri = running_sums()
+    here = in_this_frame(grid_ref)
+    low_z = TILE_BOX_EDGE * (iota((64, TILE), 0) >> 5).astype(F32)
+    low_y = TILE_BOX_EDGE * ((iota((32, TILE), 0) >> 3) & 1).astype(F32)
+    cut_z = lambda start: [v[32 * start : 32 * start + 64] for v in here]
+    cut_y = lambda arrays, start: pick_rows(arrays, (8 * start, 32 + 8 * start), 16)
+    level = cut_z(1)
+    ((beside_z, count_z),) = pack([[near(cut_z(0), 2, low_z, -1), near(cut_z(2), 2, low_z, 1)]], tri)
+    ((beside_y, count_y),) = pack(
+        [
+            [
+                near(cut_y(level, 0), 1, low_y, -1),
+                near(cut_y(beside_z, 0), 1, low_y, -1),
+                near(cut_y(level, 2), 1, low_y, 1),
+                near(cut_y(beside_z, 2), 1, low_y, 1),
+            ]
+        ],
+        tri,
+    )
+    excess_ref[...] = excess((count_z, count_y), CAPS[1:3])
+    chunks = [cut_y(level, 1), cut_y(beside_z, 1), beside_y]
+    for k in range(2):
+        for c in range(4):
+            lists_ref[4 * k + c] = chunks[1 + k][c]
+    keep_chunks(chunks, feature_ref, moment_ref, own_ref)
+
+
+def find_near(grid):
+    table = lambda rows: on_chip((rows * PITCH_ROWS, TILE))
+    shapes = [on_chip((8, NB, TILE)), on_chip((1, TILE)), table(3 * 16), table(3 * 16), table(38)]
+    return plain_call(near_kernel, shapes, "near", held(grid))
+
+
+def stress_kernel(
+    grid_ref, side_ref, grains_ref, plane_ref, lists_ref, excess_ref, feature_near_ref, moment_near_ref, own_ref,
+    rim0_ref, rim1_ref, out_ref,
+    all_ref, contact_ref, height_ref, feature_far_ref, moment_far_ref, sum_ref, even_ref, odd_ref,
+):
+    tri = running_sums()
+    sides = beside_in_this_frame(side_ref)
+
+    edge = [jnp.concatenate([low, high], axis=0) for low, high in zip(*sides)]
+    low_z = TILE_BOX_EDGE * ((iota((16, TILE), 0) >> 2) & 1).astype(F32)
+    low_y = TILE_BOX_EDGE * (iota((8, TILE), 0) & 1).astype(F32)
+    cut_z = lambda start: pick_rows(edge, (4 * start, 16 + 4 * start), 8)
+    cut_y = lambda arrays, start: pick_rows(arrays, [4 * i + start for i in range(4)], 2)
+    level = cut_z(1)
+    ((edge_z, count_ez),) = pack([[near(cut_z(0), 2, low_z, -1), near(cut_z(2), 2, low_z, 1)]], tri)
+    ((edge_y, count_ey),) = pack(
+        [
+            [
+                near(cut_y(level, 0), 1, low_y, -1),
+                near(cut_y(edge_z, 0), 1, low_y, -1),
+                near(cut_y(level, 2), 1, low_y, 1),
+                near(cut_y(edge_z, 2), 1, low_y, 1),
+            ]
+        ],
+        tri,
+    )
+    edge_own, edge_z = cut_y(level, 1), cut_y(edge_z, 1)
+
+    low_x = TILE_BOX_EDGE * (iota((NB, TILE), 0) & 7).astype(F32)
+    in_box_x = iota((4, 8, TILE), 1)
+
+    def along_x(arrays, edges, step):
+        found = []
+        for value, rim in zip(arrays, edges):
+            moved = pltpu.roll(value.reshape(4, 8, TILE), 1 if step < 0 else 7, 1)
+            rim = rim[:4] if step < 0 else rim[4:]
+            at_edge = in_box_x == (0 if step < 0 else 7)
+            found.append(jnp.where(at_edge, rim[:, None, :], moved).reshape(NB, TILE))
+        return near(found, 0, low_x, step)
+
+    own = [grains_ref[c * NB : (c + 1) * NB, :] for c in range(4)]
+    list_z = [lists_ref[c] for c in range(4)]
+    list_y = [lists_ref[4 + c] for c in range(4)]
+    (beside, count_x), (beside_rest, count_w) = pack(
+        [
+            [along_x(own, edge_own, -1), along_x(own, edge_own, 1)],
+            [
+                along_x(list_z, edge_z, -1),
+                along_x(list_y, edge_y, -1),
+                along_x(list_z, edge_z, 1),
+                along_x(list_y, edge_y, 1),
+            ],
+        ],
+        tri,
+    )
+    keep_chunks([beside, beside_rest], feature_far_ref, moment_far_ref)
+    overflow = jnp.maximum(
+        excess_ref[...], excess((count_ez, count_ey, count_x, count_w), CAPS[1:])
+    )
     overflow = jnp.max(overflow)
+
+    def table(near_ref, far_ref, k):
+        return (near_ref, k) if k < 3 else (far_ref, k - 3)
 
     at_z = iota((8, TILE), 0)
     centres_inner = centres(at_z + 4)
@@ -345,7 +416,7 @@
 
     def own_rows(t):
         return tuple(
-            jnp.broadcast_to(cand_ref[pl.ds(c * NB + t, 1), :], (8, TILE)) for c in range(4)
+            jnp.broadcast_to(grains_ref[pl.ds(c * NB + t, 1), :], (8, TILE)) for c in range(4)
         )
 
     def group(columns, first, g):
@@ -373,7 +444,8 @@
             ).astype(BF16)
 
         def measure_pairs(t, k, rhs, ref):
-            rows = feature_ref[pl.ds(16 * k * PITCH_ROWS + t, 16, stride=PITCH_ROWS), :]
+            source, n = table(feature_near_ref, feature_far_ref, k)
+            rows = source[pl.ds(16 * n * PITCH_ROWS + t, 16, stride=PITCH_ROWS), :]
             first = rows[:8]
             lhs = jnp.concatenate([rows, first, first], axis=0).T.astype(BF16)
             size = 8 * CAPS[k]
@@ -401,8 +473,10 @@
         def add_up(t, parts):
             moments = []
             for k in range(5):
-                first = feature_ref[pl.ds(16 * k * PITCH_ROWS + t, 8, stride=PITCH_ROWS), :]
-                more = moment_ref[pl.ds(16 * k * PITCH_ROWS + t, 16, stride=PITCH_ROWS), :]
+                source, n = table(feature_near_ref, feature_far_ref, k)
+                first = source[pl.ds(16 * n * PITCH_ROWS + t, 8, stride=PITCH_ROWS), :]
+                source, n = table(moment_near_ref, moment_far_ref, k)
+                more = source[pl.ds(16 * n * PITCH_ROWS + t, 16, stride=PITCH_ROWS), :]
                 moments.append(jnp.concatenate([first, more, first], axis=0))
             lhs = jnp.concatenate(moments, axis=1).astype(BF16)
             highs = jnp.concatenate([p[0] for p in parts], axis=0)
@@ -444,6 +518,7 @@
     @pl.when(overflow > 0.0)
     def _():
         stride = 16 * 8 + 32
+        here = in_this_frame(grid_ref)
         for c in range(4):
             all_ref[c * stride : c * stride + 128, :] = here[c]
             all_ref[c * stride + 128 : c * stride + 144, :] = sides[0][c]
@@ -491,7 +566,7 @@
     rim1_ref[...] = jnp.where(left_half, pltpu.roll(upper, 64, 1), lower)
 
 
-def stress_and_deposit(grid, side, grains, plane):
+def stress_and_deposit(grid, side, grains, plane, *tables):
     return plain_call(
         stress_kernel,
         [on_chip((80, TILE)), on_chip((80, TILE)), on_chip((160, 2 * TILE + COLS))],
@@ -500,14 +575,13 @@
         held(side),
         held(grains),
         held(plane),
+        *(held(v) for v in tables),
         scratch=[
-            pltpu.VMEM((4 * NB, TILE), F32),
             pltpu.VMEM((8 * 160, TILE), F32),
             pltpu.VMEM((6 * NB, TILE), F32),
             pltpu.VMEM((160, NB * TILE), BF16),
-            pltpu.VMEM((5 * 16 * PITCH_ROWS, TILE), F32),
-            pltpu.VMEM((5 * 16 * PITCH_ROWS, TILE), F32),
-            pltpu.VMEM((38 * PITCH_ROWS, TILE), F32),
+            pltpu.VMEM((2 * 16 * PITCH_ROWS, TILE), F32),
+            pltpu.VMEM((2 * 16 * PITCH_ROWS, TILE), F32),
             pltpu.VMEM((16 * PITCH_ROWS, TILE), F32),
             pltpu.VMEM((8 * sum(CAPS), 2 * TILE), F32),
             pltpu.VMEM((8 * sum(CAPS), 2 * TILE), F32),
@@ -687,9 +761,12 @@
     below, above = exchange(*sends, "gy")
     cube = jnp.concatenate([below[:, :, None], cube, above[:, :, None]], axis=2)
     cube, plane = lax.optimization_barrier((cube, plane))
-    below, above = exchange(cube[:, :, :, 0], cube[:, :, :, 7], "gx")
+    sends = (cube[:, :, :, 0], cube[:, :, :, 7])
+    sends, placed = lax.optimization_barrier((sends, cube))
+    tables = find_near(placed.reshape(4, 128, TILE))
+    below, above = exchange(*sends, "gx")
     side = jnp.stack([below, above]).reshape(2, 4, 16, TILE)
-    rim0, rim1, wide = stress_and_deposit(cube.reshape(4, 128, TILE), side, own.reshape(7 * NB, TILE), plane)
+    rim0, rim1, wide = stress_and_deposit(cube.reshape(4, 128, TILE), side, own.reshape(7 * NB, TILE), plane, *tables)
     first, second = swaps(rim0, rim1, "gx")
     block, square = on_chip((160, TILE)), on_chip((160, COLS))
     rim0, rim1, inner = plain_call(

time: 53.5 us -> 51.5 us (0.963)
  waiting for transfers between devices: 16 us -> 13 us
  starting transfers between devices: 14.7 us -> 15.8 us
    ppermute x10, waiting for transfers between devices: 16 us -> 13 us  [swaps(): lax.ppermute(value, axis, links)]
    ppermute x10, starting transfers between devices: 14.7 us -> 15.8 us  [swaps(): lax.ppermute(value, axis, links)]
    pallas_call x6 -> x7, Pallas kernels: 21.2 us -> 20.9 us  [plain_call(): pl.pallas_call(kernel, out_shape=shapes, in_specs=[vmem] * len(args), out...]
  transfers between devices with their start and end apart: 10 -> 10, of which waited for: 7 -> 7; matrix products, arithmetic and copies ran while one was open for 1% -> 1% of each run, Pallas kernels for 7% -> 11%
where the time goes in v5:
time: 51.5 us; the launch traced here: 51.3 us
  Pallas kernels  20.9 us (41%)
  starting transfers between devices  15.8 us (31%)
  waiting for transfers between devices  13 us (25%)
  between operations  0.88 us (2%)
    pallas_call x7, Pallas kernels, plain_call(): pl.pallas_call(kernel, out_shape=shapes, in_specs=[vmem] * len(args), out...  20.9 us
    ppermute x10, starting transfers between devices, swaps(): lax.ppermute(value, axis, links)  15.8 us
    ppermute x10, waiting for transfers between devices, swaps(): lax.ppermute(value, axis, links)  13 us
  transfers between devices with their start and end apart: 10, of which 7 were waited for; matrix products, arithmetic and copies ran while one was open for 1% of the time, Pallas kernels for 11%

profile of v5, /device:TPU:10, one launch (start us, length us, event | category | flops | bytes accessed | tf_op | source)
XLA Modules:
  0.0 51.3 jit_solution(663029654217995324)
XLA Ops:
  0.6 1.3 %box_sort.1 = (f32[7,32,128]{2,1,0:T(8,128)S(1)}, f32[4,32,128]{2,1,0:T(8,128)S(1)}) custom-call(f32[7,32,128]{2,1,0:T(8,128)} %bitcast.61, s32[27,1,32]{2,1,0:T(1,128)} %bitcast.70), custom_call_target="tpu_custom_call" | custom-call | tf_op jit(solution)/shard_map/box_sort/pallas_call | solution.py:699
  2.0 1.6 %collective-permute-start = (f32[4,2,8,128]{3,0,2,1:T(4,128)S(1)}, f32[4,2,8,128]{3,0,2,1:T(4,128)S(1)}, u32[]{:S(2)}, u32[]{:S(2)}) collective-permute-start(f32[4,2,8,128]{3,0,2,1:T(4,128)S(1)} %fusion), channel_id=1, source_target_pairs={{0,1},{1,0},{2,3},{3,2},{4,5},{5,4},{6,7},{7,6},{8,9},{9,8},{10,11... | collective-permute-start | bytes 98312 | tf_op jit(solution)/shard_map/ppermute | solution.py:741
  3.6 2.4 %collective-permute-done = f32[4,2,8,128]{3,0,2,1:T(4,128)S(1)} collective-permute-done((f32[4,2,8,128]{3,0,2,1:T(4,128)S(1)}, f32[4,2,8,128]{3,0,2,1:T(4,128)S(1)}, u32[]{:S(2)}, u32[]{:S(2)}) %collective-permute-start) | collective-permute-done | bytes 32800 | tf_op jit(solution)/shard_map/ppermute | solution.py:741
  6.0 0.1 pad_maximum_fusion.1
  6.1 3.5 %collective-permute-start.1 = (f32[4,4,8,128]{3,1,0,2:T(4,128)S(1)}, f32[4,4,8,128]{3,1,0,2:T(4,128)S(1)}, u32[]{:S(2)}, u32[]{:S(2)}) collective-permute-start(f32[4,4,8,128]{3,1,0,2:T(4,128)S(1)} %bitcast.65), channel_id=1, source_target_pairs={{2,4},{4,2},{3,5},{5,3},{10,12},{12,10},{11,13},{13,11},{18,20},{2... | collective-permute-start | bytes 196616 | tf_op jit(solution)/shard_map/ppermute | solution.py:741
  9.6 0.1 collective-permute-start.2
  9.7 0.1 copy.11
  9.8 3.6 %plane.1.plane_ref = bf16[640,4096]{1,0:T(8,128)(2,1)S(1)} custom-call(f32[7,32,128]{2,1,0:T(8,128)S(1)} %get-tuple-element.30.own_ref), custom_call_target="tpu_custom_call" | custom-call | tf_op jit(solution)/shard_map/plane/pallas_call | solution.py:699
  13.4 0.0 collective-permute-done.1
  13.5 0.5 collective-permute-done.2
  13.9 0.2 pad_maximum_fusion
  14.2 1.9 %collective-permute-start.3 = (f32[4,4,4,128]{3,2,1,0:T(4,128)S(1)}, f32[4,4,4,128]{3,2,1,0:T(4,128)S(1)}, u32[]{:S(2)}, u32[]{:S(2)}) collective-permute-start(f32[4,4,4,128]{3,2,1,0:T(4,128)S(1)} %bitcast.69), channel_id=1, source_target_pairs={{8,16},{16,8},{9,17},{17,9},{10,18},{18,10},{11,19},{19,11},{12,20... | collective-permute-start | bytes 98312 | tf_op jit(solution)/shard_map/ppermute | solution.py:741
  16.1 0.1 collective-permute-start.4
  16.2 0.2 copy.12
  16.3 0.2 copy.13
  16.5 1.8 %near.1 = (f32[8,32,128]{2,1,0:T(8,128)S(1)}, f32[1,128]{1,0:T(1,128)S(1)}, f32[1920,128]{1,0:T(8,128)S(1)}, f32[1920,128]{1,0:T(8,128)S(1)}, f32[1520,128]{1,0:T(8,128)S(1)}) custom-call(f32[4,128,128]{2,1,0:T(8,128)S(1)} %bitcast.47), custom_call_target="tpu_custom_call" | custom-call | tf_op jit(solution)/shard_map/near/pallas_call | solution.py:699
  18.3 1.1 %collective-permute-done.3 = f32[4,4,4,128]{3,2,1,0:T(4,128)S(1)} collective-permute-done((f32[4,4,4,128]{3,2,1,0:T(4,128)S(1)}, f32[4,4,4,128]{3,2,1,0:T(4,128)S(1)}, u32[]{:S(2)}, u32[]{:S(2)}) %collective-permute-start.3) | collective-permute-done | bytes 32800 | tf_op jit(solution)/shard_map/ppermute | solution.py:741
  19.4 0.0 collective-permute-done.4
  19.4 13.0 %stress_deposit.1 = (f32[80,128]{1,0:T(8,128)S(1)}, f32[80,128]{1,0:T(8,128)S(1)}, f32[160,512]{1,0:T(8,128)S(1)}) custom-call(f32[4,128,128]{2,1,0:T(8,128)S(1)} %bitcast.46, f32[2,4,16,128]{3,2,1,0:T(8,128)S(1)} %pad_maximum_fusion.2.side_ref, f32[224,128]{1,0:T(8,128)S(1)} %bitcast.48, bf16[640,4096]{1,0:T(8,128)(2,1)S(1)} %plane.1.plane_ref, ...), custom_call_target="tpu_custom_call" | custom-call | tf_op jit(solution)/shard_map/stress_deposit/pallas_call | solution.py:699
  32.4 0.1 collective-permute-start.5
  32.5 3.0 %collective-permute-start.6 = (f32[80,128]{1,0:T(8,128)S(1)}, f32[80,128]{1,0:T(8,128)S(1)}, u32[]{:S(2)}, u32[]{:S(2)}) collective-permute-start(f32[80,128]{1,0:T(8,128)S(1)} %get-tuple-element.43), channel_id=1, source_target_pairs={{8,16},{16,8},{9,17},{17,9},{10,18},{18,10},{11,19},{19,11},{12,20... | collective-permute-start | bytes 122888 | tf_op jit(solution)/shard_map/ppermute | solution.py:741
  35.5 0.0 collective-permute-done.5.first_ref
  35.5 2.3 %collective-permute-done.6.second_ref = f32[80,128]{1,0:T(8,128)S(1)} collective-permute-done((f32[80,128]{1,0:T(8,128)S(1)}, f32[80,128]{1,0:T(8,128)S(1)}, u32[]{:S(2)}, u32[]{:S(2)}) %collective-permute-start.6) | collective-permute-done | bytes 40992 | tf_op jit(solution)/shard_map/ppermute | solution.py:741
  37.8 0.3 rim_x.1
  38.1 1.6 %collective-permute-start.7 = (f32[160,128]{1,0:T(8,128)S(1)}, f32[160,128]{1,0:T(8,128)S(1)}, u32[]{:S(2)}, u32[]{:S(2)}) collective-permute-start(f32[160,128]{1,0:T(8,128)S(1)} %get-tuple-element.45), channel_id=1, source_target_pairs={{0,2},{2,0},{4,6},{6,4},{1,3},{3,1},{5,7},{7,5},{8,10},{10,8},{12,... | collective-permute-start | bytes 245768 | tf_op jit(solution)/shard_map/ppermute | solution.py:741
  39.8 2.3 %collective-permute-start.8 = (f32[160,128]{1,0:T(8,128)S(1)}, f32[160,128]{1,0:T(8,128)S(1)}, u32[]{:S(2)}, u32[]{:S(2)}) collective-permute-start(f32[160,128]{1,0:T(8,128)S(1)} %get-tuple-element.46), channel_id=1, source_target_pairs={{2,4},{4,2},{3,5},{5,3},{10,12},{12,10},{11,13},{13,11},{18,20},{2... | collective-permute-start | bytes 245768 | tf_op jit(solution)/shard_map/ppermute | solution.py:741
  42.1 0.5 %collective-permute-done.7.first_ref = f32[160,128]{1,0:T(8,128)S(1)} collective-permute-done((f32[160,128]{1,0:T(8,128)S(1)}, f32[160,128]{1,0:T(8,128)S(1)}, u32[]{:S(2)}, u32[]{:S(2)}) %collective-permute-start.7) | collective-permute-done | bytes 81952 | tf_op jit(solution)/shard_map/ppermute | solution.py:741
  42.6 3.4 %collective-permute-done.8.second_ref = f32[160,128]{1,0:T(8,128)S(1)} collective-permute-done((f32[160,128]{1,0:T(8,128)S(1)}, f32[160,128]{1,0:T(8,128)S(1)}, u32[]{:S(2)}, u32[]{:S(2)}) %collective-permute-start.8) | collective-permute-done | bytes 81952 | tf_op jit(solution)/shard_map/ppermute | solution.py:741
  46.1 0.3 rim_y.1
  46.3 1.6 %collective-permute-start.9 = (f32[128,128]{1,0:T(8,128)S(1)}, f32[128,128]{1,0:T(8,128)S(1)}, u32[]{:S(2)}, u32[]{:S(2)}) collective-permute-start(f32[128,128]{1,0:T(8,128)S(1)} %get-tuple-element.48), channel_id=1, source_target_pairs={{0,1},{1,0},{2,3},{3,2},{4,5},{5,4},{6,7},{7,6},{8,9},{9,8},{10,11... | collective-permute-start | bytes 196616 | tf_op jit(solution)/shard_map/ppermute | solution.py:741
  47.9 2.7 %collective-permute-done.9.got_ref = f32[128,128]{1,0:T(8,128)S(1)} collective-permute-done((f32[128,128]{1,0:T(8,128)S(1)}, f32[128,128]{1,0:T(8,128)S(1)}, u32[]{:S(2)}, u32[]{:S(2)}) %collective-permute-start.9) | collective-permute-done | bytes 65568 | tf_op jit(solution)/shard_map/ppermute | solution.py:741
  50.7 0.7 %finish.1 = (f32[1,1,1,10,8,256]{5,4,3,2,1,0:T(8,128)}, f32[1,1,2,128]{3,2,1,0:T(2,128)}, f32[1,1,16,128]{3,2,1,0:T(8,128)}) custom-call(f32[160,256]{1,0:T(8,128)S(1)} %get-tuple-element.47.total_ref, f32[128,128]{1,0:T(8,128)S(1)} %collective-permute-done.9.got_ref), custom_call_target="tpu_custom_call" | custom-call | tf_op jit(solution)/shard_map/finish/pallas_call | solution.py:699
  (11 shorter events, 0.2 us)
Async XLA Ops:
  2.0 4.0 %collective-permute-start = (f32[4,2,8,128]{3,0,2,1:T(4,128)S(1)}, f32[4,2,8,128]{3,0,2,1:T(4,128)S(1)}, u32[]{:S(2)}, u32[]{:S(2)}) collective-permute-start(f32[4,2,8,128]{3,0,2,1:T(4,128)S(1)} %fusion), channel_id=1, source_target_pairs={{0,1},{1,0},{2,3},{3,2},{4,5},{5,4},{6,7},{7,6},{8,9},{9,8},{10,11... | collective-permute-start | bytes 98312 | tf_op jit(solution)/shard_map/ppermute | solution.py:741
  6.1 7.4 %collective-permute-start.1 = (f32[4,4,8,128]{3,1,0,2:T(4,128)S(1)}, f32[4,4,8,128]{3,1,0,2:T(4,128)S(1)}, u32[]{:S(2)}, u32[]{:S(2)}) collective-permute-start(f32[4,4,8,128]{3,1,0,2:T(4,128)S(1)} %bitcast.65), channel_id=1, source_target_pairs={{2,4},{4,2},{3,5},{5,3},{10,12},{12,10},{11,13},{13,11},{18,20},{2... | collective-permute-start | bytes 196616 | tf_op jit(solution)/shard_map/ppermute | solution.py:741
  9.6 4.3 %collective-permute-start.2 = (f32[4,4,8,128]{3,1,0,2:T(4,128)S(1)}, f32[4,4,8,128]{3,1,0,2:T(4,128)S(1)}, u32[]{:S(2)}, u32[]{:S(2)}) collective-permute-start(f32[4,4,8,128]{3,1,0,2:T(4,128)S(1)} %bitcast.63), channel_id=1, source_target_pairs={{0,2},{2,0},{4,6},{6,4},{1,3},{3,1},{5,7},{7,5},{8,10},{10,8},{12,... | collective-permute-start | bytes 196616 | tf_op jit(solution)/shard_map/ppermute | solution.py:741
  14.2 5.2 %collective-permute-start.3 = (f32[4,4,4,128]{3,2,1,0:T(4,128)S(1)}, f32[4,4,4,128]{3,2,1,0:T(4,128)S(1)}, u32[]{:S(2)}, u32[]{:S(2)}) collective-permute-start(f32[4,4,4,128]{3,2,1,0:T(4,128)S(1)} %bitcast.69), channel_id=1, source_target_pairs={{8,16},{16,8},{9,17},{17,9},{10,18},{18,10},{11,19},{19,11},{12,20... | collective-permute-start | bytes 98312 | tf_op jit(solution)/shard_map/ppermute | solution.py:741
  16.1 3.3 %collective-permute-start.4 = (f32[4,4,4,128]{3,2,1,0:T(4,128)S(1)}, f32[4,4,4,128]{3,2,1,0:T(4,128)S(1)}, u32[]{:S(2)}, u32[]{:S(2)}) collective-permute-start(f32[4,4,4,128]{3,2,1,0:T(4,128)S(1)} %bitcast.67), channel_id=1, source_target_pairs={{0,8},{8,0},{16,24},{24,16},{1,9},{9,1},{17,25},{25,17},{2,10},{10... | collective-permute-start | bytes 98312 | tf_op jit(solution)/shard_map/ppermute | solution.py:741
  32.4 3.1 %collective-permute-start.5 = (f32[80,128]{1,0:T(8,128)S(1)}, f32[80,128]{1,0:T(8,128)S(1)}, u32[]{:S(2)}, u32[]{:S(2)}) collective-permute-start(f32[80,128]{1,0:T(8,128)S(1)} %get-tuple-element.42), channel_id=1, source_target_pairs={{0,8},{8,0},{16,24},{24,16},{1,9},{9,1},{17,25},{25,17},{2,10},{10... | collective-permute-start | bytes 122888 | tf_op jit(solution)/shard_map/ppermute | solution.py:741
  32.5 5.3 %collective-permute-start.6 = (f32[80,128]{1,0:T(8,128)S(1)}, f32[80,128]{1,0:T(8,128)S(1)}, u32[]{:S(2)}, u32[]{:S(2)}) collective-permute-start(f32[80,128]{1,0:T(8,128)S(1)} %get-tuple-element.43), channel_id=1, source_target_pairs={{8,16},{16,8},{9,17},{17,9},{10,18},{18,10},{11,19},{19,11},{12,20... | collective-permute-start | bytes 122888 | tf_op jit(solution)/shard_map/ppermute | solution.py:741
  38.1 4.5 %collective-permute-start.7 = (f32[160,128]{1,0:T(8,128)S(1)}, f32[160,128]{1,0:T(8,128)S(1)}, u32[]{:S(2)}, u32[]{:S(2)}) collective-permute-start(f32[160,128]{1,0:T(8,128)S(1)} %get-tuple-element.45), channel_id=1, source_target_pairs={{0,2},{2,0},{4,6},{6,4},{1,3},{3,1},{5,7},{7,5},{8,10},{10,8},{12,... | collective-permute-start | bytes 245768 | tf_op jit(solution)/shard_map/ppermute | solution.py:741
  39.8 6.3 %collective-permute-start.8 = (f32[160,128]{1,0:T(8,128)S(1)}, f32[160,128]{1,0:T(8,128)S(1)}, u32[]{:S(2)}, u32[]{:S(2)}) collective-permute-start(f32[160,128]{1,0:T(8,128)S(1)} %get-tuple-element.46), channel_id=1, source_target_pairs={{2,4},{4,2},{3,5},{5,3},{10,12},{12,10},{11,13},{13,11},{18,20},{2... | collective-permute-start | bytes 245768 | tf_op jit(solution)/shard_map/ppermute | solution.py:741
  46.3 4.3 %collective-permute-start.9 = (f32[128,128]{1,0:T(8,128)S(1)}, f32[128,128]{1,0:T(8,128)S(1)}, u32[]{:S(2)}, u32[]{:S(2)}) collective-permute-start(f32[128,128]{1,0:T(8,128)S(1)} %get-tuple-element.48), channel_id=1, source_target_pairs={{0,1},{1,0},{2,3},{3,2},{4,5},{5,4},{6,7},{7,6},{8,9},{9,8},{10,11... | collective-permute-start | bytes 196616 | tf_op jit(solution)/shard_map/ppermute | solution.py:741

commit v6 on v5

--- a/solution.py
+++ b/solution.py
@@ -332,6 +332,14 @@
     return plain_call(near_kernel, shapes, "near", held(grid))
 
 
+def two_along_z():
+    return lax.axis_size("gz") == 2
+
+
+def field_rows():
+    return 80 + (48 if two_along_z() else 80)
+
+
 def stress_kernel(
     grid_ref, side_ref, grains_ref, plane_ref, lists_ref, excess_ref, feature_near_ref, moment_near_ref, own_ref,
     rim0_ref, rim1_ref, out_ref,
@@ -341,24 +349,26 @@
     sides = beside_in_this_frame(side_ref)
 
     edge = [jnp.concatenate([low, high], axis=0) for low, high in zip(*sides)]
-    low_z = TILE_BOX_EDGE * ((iota((16, TILE), 0) >> 2) & 1).astype(F32)
-    low_y = TILE_BOX_EDGE * (iota((8, TILE), 0) & 1).astype(F32)
-    cut_z = lambda start: pick_rows(edge, (4 * start, 16 + 4 * start), 8)
-    cut_y = lambda arrays, start: pick_rows(arrays, [4 * i + start for i in range(4)], 2)
-    level = cut_z(1)
-    ((edge_z, count_ez),) = pack([[near(cut_z(0), 2, low_z, -1), near(cut_z(2), 2, low_z, 1)]], tri)
-    ((edge_y, count_ey),) = pack(
-        [
-            [
-                near(cut_y(level, 0), 1, low_y, -1),
-                near(cut_y(edge_z, 0), 1, low_y, -1),
-                near(cut_y(level, 2), 1, low_y, 1),
-                near(cut_y(edge_z, 2), 1, low_y, 1),
-            ]
-        ],
-        tri,
-    )
-    edge_own, edge_z = cut_y(level, 1), cut_y(edge_z, 1)
+    row = iota((8, TILE), 0)
+    low_z = TILE_BOX_EDGE * ((row >> 1) & 1).astype(F32)
+    low_y = TILE_BOX_EDGE * (row & 1).astype(F32)
+
+    def around(dz, dy):
+        return pick_rows(edge, [16 * s + 4 * (z + 1 + dz) + 1 + dy for s in range(2) for z in range(2)], 2)
+
+    def near_edge(dz, dy):
+        arrays = around(dz, dy)
+        mask = jnp.where(row < 4, arrays[0], SPAN_X - arrays[0]) >= -REACH
+        for axis, low, step in ((2, low_z, dz), (1, low_y, dy)):
+            if step:
+                mask = mask & near(arrays, axis, low, step)[0]
+        return mask & (arrays[3] > 0.0), arrays
+
+    beside_edge = [(dz, dy) for dz in (-1, 0, 1) for dy in (-1, 0, 1) if dz or dy]
+    ((edge_z, count_e),) = pack([[near_edge(dz, dy) for dz, dy in beside_edge]], tri)
+    edge_own = around(0, 0)
+    empty = jnp.zeros((8, TILE), F32)
+    edge_y = [empty, empty, empty, empty + ABSENT]
 
     low_x = TILE_BOX_EDGE * (iota((NB, TILE), 0) & 7).astype(F32)
     in_box_x = iota((4, 8, TILE), 1)
@@ -389,7 +399,7 @@
     )
     keep_chunks([beside, beside_rest], feature_far_ref, moment_far_ref)
     overflow = jnp.maximum(
-        excess_ref[...], excess((count_ez, count_ey, count_x, count_w), CAPS[1:])
+        excess_ref[...], excess((count_e, count_x, count_w), (TILE // 8,) + CAPS[3:])
     )
     overflow = jnp.max(overflow)
 
@@ -398,7 +408,10 @@
 
     at_z = iota((8, TILE), 0)
     centres_inner = centres(at_z + 4)
-    centres_rim = centres(jnp.where(at_z < 4, at_z, at_z + 8))
+    if two_along_z():
+        centres_rim = centres((at_z & 3) + jnp.where(lax.axis_index("gz") == 0, 12, 0))
+    else:
+        centres_rim = centres(jnp.where(at_z < 4, at_z, at_z + 8))
 
     def put_height(t):
         rows = [grains_ref[pl.ds(r * NB + t, 1), :] for r in range(2, 7)]
@@ -410,7 +423,12 @@
         loads = [masses, masses * vel[0], masses * vel[1], masses * vel[2]]
         for k, (i, j) in enumerate(((0, 0), (1, 1), (2, 2), (0, 1), (0, 2), (1, 2))):
             loads.append(cont[k] + masses * (vel[i] * vel[j]))
-        height = [load * wz_inner for load in loads] + [load * wz_rim for load in loads]
+        height = [load * wz_inner for load in loads]
+        if two_along_z():
+            height += [jnp.where(at_z < 4, loads[c], loads[c + 1]) * wz_rim for c in range(0, 10, 2)]
+            height.append(jnp.zeros((8, TILE), F32))
+        else:
+            height += [load * wz_rim for load in loads]
         lanes = pl.ds(pl.multiple_of(t * TILE, TILE), TILE)
         height_ref[:, lanes] = jnp.concatenate(height, axis=0).astype(BF16)
 
@@ -498,14 +516,14 @@
         for k in range(5):
             measure_pairs(0, k, first_rhs, even_ref)
 
-        def four_tiles(q, carry):
-            step(4 * q, even_ref, 4 * q + 1, odd_ref)
-            step(4 * q + 1, odd_ref, 4 * q + 2, even_ref)
-            step(4 * q + 2, even_ref, 4 * q + 3, odd_ref)
-            step(4 * q + 3, odd_ref, jnp.minimum(4 * q + 4, NB - 1), even_ref)
+        def eight_tiles(q, carry):
+            refs = (even_ref, odd_ref)
+            for i in range(8):
+                t = 8 * q + i
+                step(t, refs[i % 2], t + 1 if i < 7 else jnp.minimum(t + 1, NB - 1), refs[1 - i % 2])
             return carry
 
-        lax.fori_loop(0, NB // 4, four_tiles, 0)
+        lax.fori_loop(0, NB // 8, eight_tiles, 0)
         total = [sum_ref[m * PITCH_ROWS : m * PITCH_ROWS + NB, :] for m in range(14)]
         first = [total[c] + total[3 + c] for c in range(3)]
         own_mid = [own_ref[(35 + c) * PITCH_ROWS : (35 + c) * PITCH_ROWS + NB, :] for c in range(3)]
@@ -560,16 +578,18 @@
     out_ref[...] = wide[:, TILE:]
     rim = wide[:, :TILE]
     rim = jnp.where(is_even("gx"), pltpu.roll(rim, 64, 1), rim)
-    upper, lower = rim[:80], rim[80:]
-    left_half = iota((80, TILE), 1) < 64
+    half = field_rows() // 2
+    upper, lower = rim[:half], rim[half:]
+    left_half = iota((half, TILE), 1) < 64
     rim0_ref[...] = jnp.where(left_half, upper, pltpu.roll(lower, 64, 1))
     rim1_ref[...] = jnp.where(left_half, pltpu.roll(upper, 64, 1), lower)
 
 
 def stress_and_deposit(grid, side, grains, plane, *tables):
+    rows = field_rows()
     return plain_call(
         stress_kernel,
-        [on_chip((80, TILE)), on_chip((80, TILE)), on_chip((160, 2 * TILE + COLS))],
+        [on_chip((rows // 2, TILE)), on_chip((rows // 2, TILE)), on_chip((rows, 2 * TILE + COLS))],
         "stress_deposit",
         held(grid),
         held(side),
@@ -579,7 +599,7 @@
         scratch=[
             pltpu.VMEM((8 * 160, TILE), F32),
             pltpu.VMEM((6 * NB, TILE), F32),
-            pltpu.VMEM((160, NB * TILE), BF16),
+            pltpu.VMEM((rows, NB * TILE), BF16),
             pltpu.VMEM((2 * 16 * PITCH_ROWS, TILE), F32),
             pltpu.VMEM((2 * 16 * PITCH_ROWS, TILE), F32),
             pltpu.VMEM((16 * PITCH_ROWS, TILE), F32),
@@ -593,7 +613,7 @@
     even = is_even("gx")
     right = jnp.where(even, first_ref[...], second_ref[...])
     left = jnp.where(even, second_ref[...], first_ref[...])
-    left_half = iota((80, TILE), 1) < 64
+    left_half = iota(left.shape, 1) < 64
     got = jnp.concatenate(
         [
             jnp.where(left_half, right, pltpu.roll(left, 64, 1)),
@@ -637,15 +657,8 @@
     total = add_rim_y(inner_ref, first_ref, second_ref)
     out_ref[...] = total
     lower = lax.axis_index("gz") == 0
-    top = iota((8, COLS), 0) < 4
-    for p in range(5):
-        one = total[80 + 16 * p : 88 + 16 * p]
-        two = total[88 + 16 * p : 96 + 16 * p]
-        to_upper = jnp.where(top, pltpu.roll(one, 4, 0), two)
-        to_lower = jnp.where(top, one, pltpu.roll(two, 4, 0))
-        both = jnp.where(lower, to_upper, to_lower)
-        send_ref[8 * p : 8 * p + 8, :] = both[:, :TILE]
-        send_ref[40 + 8 * p : 48 + 8 * p, :] = both[:, TILE:]
+    send_ref[:40, :] = total[80:120, :TILE]
+    send_ref[40:80, :] = total[80:120, TILE:]
     for i, c in enumerate(PROFILED):
         rows = total[8 * c : 8 * c + 8]
         send_ref[80 + 8 * i : 88 + 8 * i, :] = jnp.where(lower, rows[:, TILE:], rows[:, :TILE])
@@ -672,8 +685,9 @@
     column = {}
     for i, c in enumerate(PROFILED):
         mine = jnp.where(lower, fields[c][:, :TILE], fields[c][:, TILE:])
-        rim = total_ref[80 + 8 * c : 88 + 8 * c, :]
-        rim = pltpu.roll(jnp.where(lower, rim[:, :TILE], rim[:, TILE:]), 4, 0)
+        rim = total_ref[80 + 8 * (c // 2) : 88 + 8 * (c // 2), :]
+        rim = jnp.where(lower, rim[:, :TILE], rim[:, TILE:])
+        rim = jnp.where(lower == (c % 2 == 0), rim, pltpu.roll(rim, 4, 0))
         other = got_ref[80 + 8 * i : 88 + 8 * i, :] + jnp.where(theirs, rim, 0.0)
         column[c] = jnp.concatenate(
             [jnp.where(lower, mine, other), jnp.where(lower, other, mine)], axis=0
@@ -768,12 +782,13 @@
     side = jnp.stack([below, above]).reshape(2, 4, 16, TILE)
     rim0, rim1, wide = stress_and_deposit(cube.reshape(4, 128, TILE), side, own.reshape(7 * NB, TILE), plane, *tables)
     first, second = swaps(rim0, rim1, "gx")
-    block, square = on_chip((160, TILE)), on_chip((160, COLS))
+    rows = field_rows()
+    block, square = on_chip((rows, TILE)), on_chip((rows, COLS))
     rim0, rim1, inner = plain_call(
         rim_x_kernel, [block, block, square], "rim_x", held(wide), held(first), held(second)
     )
     first, second = swaps(rim0, rim1, "gy")
-    if lax.axis_size("gz") == 2:
+    if two_along_z():
         sends = on_chip((128, TILE))
         total, send = plain_call(
             rim_y_two_kernel, [square, sends], "rim_y", held(inner), held(first), held(second)

time: 51.5 us -> 49.8 us (0.967)
  Pallas kernels: 20.9 us -> 19.4 us
    pallas_call x7, Pallas kernels: 20.9 us -> 19.4 us  [plain_call(): pl.pallas_call(kernel, out_shape=shapes, in_specs=[vmem] * len(args), out...]
where the time goes in v6:
time: 49.8 us; the launch traced here: 49.6 us
  Pallas kernels  19.4 us (39%)
  starting transfers between devices  15.8 us (32%)
  waiting for transfers between devices  12.7 us (26%)
  between operations  0.88 us (2%)
    pallas_call x7, Pallas kernels, plain_call(): pl.pallas_call(kernel, out_shape=shapes, in_specs=[vmem] * len(args), out...  19.4 us
    ppermute x10, starting transfers between devices, swaps(): lax.ppermute(value, axis, links)  15.8 us
    ppermute x10, waiting for transfers between devices, swaps(): lax.ppermute(value, axis, links)  12.7 us
  transfers between devices with their start and end apart: 10, of which 7 were waited for; matrix products, arithmetic and copies ran while one was open for 1% of the time, Pallas kernels for 11%

profile of v6, /device:TPU:10, one launch (start us, length us, event | category | flops | bytes accessed | tf_op | source)
XLA Modules:
  0.0 49.6 jit_solution(2010106391624531823)
XLA Ops:
  0.6 1.3 %box_sort.1 = (f32[7,32,128]{2,1,0:T(8,128)S(1)}, f32[4,32,128]{2,1,0:T(8,128)S(1)}) custom-call(f32[7,32,128]{2,1,0:T(8,128)} %bitcast.61, s32[27,1,32]{2,1,0:T(1,128)} %bitcast.70), custom_call_target="tpu_custom_call" | custom-call | tf_op jit(solution)/shard_map/box_sort/pallas_call | solution.py:713
  2.0 1.6 %collective-permute-start = (f32[4,2,8,128]{3,0,2,1:T(4,128)S(1)}, f32[4,2,8,128]{3,0,2,1:T(4,128)S(1)}, u32[]{:S(2)}, u32[]{:S(2)}) collective-permute-start(f32[4,2,8,128]{3,0,2,1:T(4,128)S(1)} %fusion), channel_id=1, source_target_pairs={{0,1},{1,0},{2,3},{3,2},{4,5},{5,4},{6,7},{7,6},{8,9},{9,8},{10,11... | collective-permute-start | bytes 98312 | tf_op jit(solution)/shard_map/ppermute | solution.py:755
  3.6 2.4 %collective-permute-done = f32[4,2,8,128]{3,0,2,1:T(4,128)S(1)} collective-permute-done((f32[4,2,8,128]{3,0,2,1:T(4,128)S(1)}, f32[4,2,8,128]{3,0,2,1:T(4,128)S(1)}, u32[]{:S(2)}, u32[]{:S(2)}) %collective-permute-start) | collective-permute-done | bytes 32800 | tf_op jit(solution)/shard_map/ppermute | solution.py:755
  6.0 0.1 pad_maximum_fusion.1
  6.1 3.5 %collective-permute-start.1 = (f32[4,4,8,128]{3,1,0,2:T(4,128)S(1)}, f32[4,4,8,128]{3,1,0,2:T(4,128)S(1)}, u32[]{:S(2)}, u32[]{:S(2)}) collective-permute-start(f32[4,4,8,128]{3,1,0,2:T(4,128)S(1)} %bitcast.65), channel_id=1, source_target_pairs={{2,4},{4,2},{3,5},{5,3},{10,12},{12,10},{11,13},{13,11},{18,20},{2... | collective-permute-start | bytes 196616 | tf_op jit(solution)/shard_map/ppermute | solution.py:755
  9.6 0.1 collective-permute-start.2
  9.7 0.1 copy.11
  9.8 3.6 %plane.1.plane_ref = bf16[640,4096]{1,0:T(8,128)(2,1)S(1)} custom-call(f32[7,32,128]{2,1,0:T(8,128)S(1)} %get-tuple-element.30.own_ref), custom_call_target="tpu_custom_call" | custom-call | tf_op jit(solution)/shard_map/plane/pallas_call | solution.py:713
  13.4 0.0 collective-permute-done.1
  13.5 0.5 collective-permute-done.2
  13.9 0.2 pad_maximum_fusion
  14.2 1.9 %collective-permute-start.3 = (f32[4,4,4,128]{3,2,1,0:T(4,128)S(1)}, f32[4,4,4,128]{3,2,1,0:T(4,128)S(1)}, u32[]{:S(2)}, u32[]{:S(2)}) collective-permute-start(f32[4,4,4,128]{3,2,1,0:T(4,128)S(1)} %bitcast.69), channel_id=1, source_target_pairs={{8,16},{16,8},{9,17},{17,9},{10,18},{18,10},{11,19},{19,11},{12,20... | collective-permute-start | bytes 98312 | tf_op jit(solution)/shard_map/ppermute | solution.py:755
  16.1 0.1 collective-permute-start.4
  16.2 0.2 copy.12
  16.3 0.2 copy.13
  16.5 1.8 %near.1 = (f32[8,32,128]{2,1,0:T(8,128)S(1)}, f32[1,128]{1,0:T(1,128)S(1)}, f32[1920,128]{1,0:T(8,128)S(1)}, f32[1920,128]{1,0:T(8,128)S(1)}, f32[1520,128]{1,0:T(8,128)S(1)}) custom-call(f32[4,128,128]{2,1,0:T(8,128)S(1)} %bitcast.47), custom_call_target="tpu_custom_call" | custom-call | tf_op jit(solution)/shard_map/near/pallas_call | solution.py:713
  18.3 1.1 %collective-permute-done.3 = f32[4,4,4,128]{3,2,1,0:T(4,128)S(1)} collective-permute-done((f32[4,4,4,128]{3,2,1,0:T(4,128)S(1)}, f32[4,4,4,128]{3,2,1,0:T(4,128)S(1)}, u32[]{:S(2)}, u32[]{:S(2)}) %collective-permute-start.3) | collective-permute-done | bytes 32800 | tf_op jit(solution)/shard_map/ppermute | solution.py:755
  19.4 0.0 collective-permute-done.4
  19.4 11.5 %stress_deposit.1 = (f32[64,128]{1,0:T(8,128)S(1)}, f32[64,128]{1,0:T(8,128)S(1)}, f32[128,512]{1,0:T(8,128)S(1)}) custom-call(f32[4,128,128]{2,1,0:T(8,128)S(1)} %bitcast.46, f32[2,4,16,128]{3,2,1,0:T(8,128)S(1)} %pad_maximum_fusion.2.side_ref, f32[224,128]{1,0:T(8,128)S(1)} %bitcast.48, bf16[640,4096]{1,0:T(8,128)(2,1)S(1)} %plane.1.plane_ref, ...), custom_call_target="tpu_custom_call" | custom-call | tf_op jit(solution)/shard_map/stress_deposit/pallas_call | solution.py:713
  30.9 0.1 collective-permute-start.5
  31.0 3.0 %collective-permute-start.6 = (f32[64,128]{1,0:T(8,128)S(1)}, f32[64,128]{1,0:T(8,128)S(1)}, u32[]{:S(2)}, u32[]{:S(2)}) collective-permute-start(f32[64,128]{1,0:T(8,128)S(1)} %get-tuple-element.43), channel_id=1, source_target_pairs={{8,16},{16,8},{9,17},{17,9},{10,18},{18,10},{11,19},{19,11},{12,20... | collective-permute-start | bytes 98312 | tf_op jit(solution)/shard_map/ppermute | solution.py:755
  34.0 0.0 collective-permute-done.5.first_ref
  34.0 2.2 %collective-permute-done.6.second_ref = f32[64,128]{1,0:T(8,128)S(1)} collective-permute-done((f32[64,128]{1,0:T(8,128)S(1)}, f32[64,128]{1,0:T(8,128)S(1)}, u32[]{:S(2)}, u32[]{:S(2)}) %collective-permute-start.6) | collective-permute-done | bytes 32800 | tf_op jit(solution)/shard_map/ppermute | solution.py:755
  36.2 0.3 rim_x.1
  36.5 1.6 %collective-permute-start.7 = (f32[128,128]{1,0:T(8,128)S(1)}, f32[128,128]{1,0:T(8,128)S(1)}, u32[]{:S(2)}, u32[]{:S(2)}) collective-permute-start(f32[128,128]{1,0:T(8,128)S(1)} %get-tuple-element.45), channel_id=1, source_target_pairs={{0,2},{2,0},{4,6},{6,4},{1,3},{3,1},{5,7},{7,5},{8,10},{10,8},{12,... | collective-permute-start | bytes 196616 | tf_op jit(solution)/shard_map/ppermute | solution.py:755
  38.2 2.3 %collective-permute-start.8 = (f32[128,128]{1,0:T(8,128)S(1)}, f32[128,128]{1,0:T(8,128)S(1)}, u32[]{:S(2)}, u32[]{:S(2)}) collective-permute-start(f32[128,128]{1,0:T(8,128)S(1)} %get-tuple-element.46), channel_id=1, source_target_pairs={{2,4},{4,2},{3,5},{5,3},{10,12},{12,10},{11,13},{13,11},{18,20},{2... | collective-permute-start | bytes 196616 | tf_op jit(solution)/shard_map/ppermute | solution.py:755
  40.5 0.4 collective-permute-done.7.first_ref
  40.9 3.4 %collective-permute-done.8.second_ref = f32[128,128]{1,0:T(8,128)S(1)} collective-permute-done((f32[128,128]{1,0:T(8,128)S(1)}, f32[128,128]{1,0:T(8,128)S(1)}, u32[]{:S(2)}, u32[]{:S(2)}) %collective-permute-start.8) | collective-permute-done | bytes 65568 | tf_op jit(solution)/shard_map/ppermute | solution.py:755
  44.3 0.2 rim_y.1
  44.6 1.6 %collective-permute-start.9 = (f32[128,128]{1,0:T(8,128)S(1)}, f32[128,128]{1,0:T(8,128)S(1)}, u32[]{:S(2)}, u32[]{:S(2)}) collective-permute-start(f32[128,128]{1,0:T(8,128)S(1)} %get-tuple-element.48), channel_id=1, source_target_pairs={{0,1},{1,0},{2,3},{3,2},{4,5},{5,4},{6,7},{7,6},{8,9},{9,8},{10,11... | collective-permute-start | bytes 196616 | tf_op jit(solution)/shard_map/ppermute | solution.py:755
  46.1 2.7 %collective-permute-done.9.got_ref = f32[128,128]{1,0:T(8,128)S(1)} collective-permute-done((f32[128,128]{1,0:T(8,128)S(1)}, f32[128,128]{1,0:T(8,128)S(1)}, u32[]{:S(2)}, u32[]{:S(2)}) %collective-permute-start.9) | collective-permute-done | bytes 65568 | tf_op jit(solution)/shard_map/ppermute | solution.py:755
  48.9 0.7 %finish.1 = (f32[1,1,1,10,8,256]{5,4,3,2,1,0:T(8,128)}, f32[1,1,2,128]{3,2,1,0:T(2,128)}, f32[1,1,16,128]{3,2,1,0:T(8,128)}) custom-call(f32[128,256]{1,0:T(8,128)S(1)} %get-tuple-element.47.total_ref, f32[128,128]{1,0:T(8,128)S(1)} %collective-permute-done.9.got_ref), custom_call_target="tpu_custom_call" | custom-call | tf_op jit(solution)/shard_map/finish/pallas_call | solution.py:713
  (11 shorter events, 0.2 us)
Async XLA Ops:
  2.0 4.0 %collective-permute-start = (f32[4,2,8,128]{3,0,2,1:T(4,128)S(1)}, f32[4,2,8,128]{3,0,2,1:T(4,128)S(1)}, u32[]{:S(2)}, u32[]{:S(2)}) collective-permute-start(f32[4,2,8,128]{3,0,2,1:T(4,128)S(1)} %fusion), channel_id=1, source_target_pairs={{0,1},{1,0},{2,3},{3,2},{4,5},{5,4},{6,7},{7,6},{8,9},{9,8},{10,11... | collective-permute-start | bytes 98312 | tf_op jit(solution)/shard_map/ppermute | solution.py:755
  6.1 7.4 %collective-permute-start.1 = (f32[4,4,8,128]{3,1,0,2:T(4,128)S(1)}, f32[4,4,8,128]{3,1,0,2:T(4,128)S(1)}, u32[]{:S(2)}, u32[]{:S(2)}) collective-permute-start(f32[4,4,8,128]{3,1,0,2:T(4,128)S(1)} %bitcast.65), channel_id=1, source_target_pairs={{2,4},{4,2},{3,5},{5,3},{10,12},{12,10},{11,13},{13,11},{18,20},{2... | collective-permute-start | bytes 196616 | tf_op jit(solution)/shard_map/ppermute | solution.py:755
  9.6 4.3 %collective-permute-start.2 = (f32[4,4,8,128]{3,1,0,2:T(4,128)S(1)}, f32[4,4,8,128]{3,1,0,2:T(4,128)S(1)}, u32[]{:S(2)}, u32[]{:S(2)}) collective-permute-start(f32[4,4,8,128]{3,1,0,2:T(4,128)S(1)} %bitcast.63), channel_id=1, source_target_pairs={{0,2},{2,0},{4,6},{6,4},{1,3},{3,1},{5,7},{7,5},{8,10},{10,8},{12,... | collective-permute-start | bytes 196616 | tf_op jit(solution)/shard_map/ppermute | solution.py:755
  14.2 5.2 %collective-permute-start.3 = (f32[4,4,4,128]{3,2,1,0:T(4,128)S(1)}, f32[4,4,4,128]{3,2,1,0:T(4,128)S(1)}, u32[]{:S(2)}, u32[]{:S(2)}) collective-permute-start(f32[4,4,4,128]{3,2,1,0:T(4,128)S(1)} %bitcast.69), channel_id=1, source_target_pairs={{8,16},{16,8},{9,17},{17,9},{10,18},{18,10},{11,19},{19,11},{12,20... | collective-permute-start | bytes 98312 | tf_op jit(solution)/shard_map/ppermute | solution.py:755
  16.1 3.3 %collective-permute-start.4 = (f32[4,4,4,128]{3,2,1,0:T(4,128)S(1)}, f32[4,4,4,128]{3,2,1,0:T(4,128)S(1)}, u32[]{:S(2)}, u32[]{:S(2)}) collective-permute-start(f32[4,4,4,128]{3,2,1,0:T(4,128)S(1)} %bitcast.67), channel_id=1, source_target_pairs={{0,8},{8,0},{16,24},{24,16},{1,9},{9,1},{17,25},{25,17},{2,10},{10... | collective-permute-start | bytes 98312 | tf_op jit(solution)/shard_map/ppermute | solution.py:755
  30.9 3.1 %collective-permute-start.5 = (f32[64,128]{1,0:T(8,128)S(1)}, f32[64,128]{1,0:T(8,128)S(1)}, u32[]{:S(2)}, u32[]{:S(2)}) collective-permute-start(f32[64,128]{1,0:T(8,128)S(1)} %get-tuple-element.42), channel_id=1, source_target_pairs={{0,8},{8,0},{16,24},{24,16},{1,9},{9,1},{17,25},{25,17},{2,10},{10... | collective-permute-start | bytes 98312 | tf_op jit(solution)/shard_map/ppermute | solution.py:755
  31.0 5.2 %collective-permute-start.6 = (f32[64,128]{1,0:T(8,128)S(1)}, f32[64,128]{1,0:T(8,128)S(1)}, u32[]{:S(2)}, u32[]{:S(2)}) collective-permute-start(f32[64,128]{1,0:T(8,128)S(1)} %get-tuple-element.43), channel_id=1, source_target_pairs={{8,16},{16,8},{9,17},{17,9},{10,18},{18,10},{11,19},{19,11},{12,20... | collective-permute-start | bytes 98312 | tf_op jit(solution)/shard_map/ppermute | solution.py:755
  36.5 4.3 %collective-permute-start.7 = (f32[128,128]{1,0:T(8,128)S(1)}, f32[128,128]{1,0:T(8,128)S(1)}, u32[]{:S(2)}, u32[]{:S(2)}) collective-permute-start(f32[128,128]{1,0:T(8,128)S(1)} %get-tuple-element.45), channel_id=1, source_target_pairs={{0,2},{2,0},{4,6},{6,4},{1,3},{3,1},{5,7},{7,5},{8,10},{10,8},{12,... | collective-permute-start | bytes 196616 | tf_op jit(solution)/shard_map/ppermute | solution.py:755
  38.2 6.1 %collective-permute-start.8 = (f32[128,128]{1,0:T(8,128)S(1)}, f32[128,128]{1,0:T(8,128)S(1)}, u32[]{:S(2)}, u32[]{:S(2)}) collective-permute-start(f32[128,128]{1,0:T(8,128)S(1)} %get-tuple-element.46), channel_id=1, source_target_pairs={{2,4},{4,2},{3,5},{5,3},{10,12},{12,10},{11,13},{13,11},{18,20},{2... | collective-permute-start | bytes 196616 | tf_op jit(solution)/shard_map/ppermute | solution.py:755
  44.6 4.3 %collective-permute-start.9 = (f32[128,128]{1,0:T(8,128)S(1)}, f32[128,128]{1,0:T(8,128)S(1)}, u32[]{:S(2)}, u32[]{:S(2)}) collective-permute-start(f32[128,128]{1,0:T(8,128)S(1)} %get-tuple-element.48), channel_id=1, source_target_pairs={{0,1},{1,0},{2,3},{3,2},{4,5},{5,4},{6,7},{7,6},{8,9},{9,8},{10,11... | collective-permute-start | bytes 196616 | tf_op jit(solution)/shard_map/ppermute | solution.py:755

commit v7 on v6

--- a/solution.py
+++ b/solution.py
@@ -298,7 +298,100 @@
     return [jnp.concatenate([v[at : at + size] for at in starts], axis=0) for v in arrays]
 
 
-def near_kernel(grid_ref, lists_ref, excess_ref, feature_ref, moment_ref, own_ref):
+def pair_loop(chunks, first_chunk, own_ref, sum_ref, even_ref, odd_ref):
+    caps = CAPS[first_chunk : first_chunk + len(chunks)]
+    starts = [8 * sum(caps[:k]) for k in range(len(caps))]
+    sub = iota((8, TILE), 0)
+
+    def own_side(t):
+        radii = [own_ref[pl.ds((32 + p) * PITCH_ROWS + t, 1), :] for p in range(3)]
+        radii = [jnp.where(sub == 6, jnp.broadcast_to(r, (8, TILE)), 0.0) for r in radii]
+        reach = [radii[0], jnp.where(sub >= 5, 1.0, 0.0), radii[1], radii[2]]
+        return jnp.concatenate(
+            [own_ref[pl.ds(t, 32, stride=PITCH_ROWS), :], jnp.concatenate(reach, axis=0)], axis=1
+        ).astype(BF16)
+
+    def measure_pairs(t, k, rhs, ref):
+        source, _, n = chunks[k]
+        rows = source[pl.ds(16 * n * PITCH_ROWS + t, 16, stride=PITCH_ROWS), :]
+        first = rows[:8]
+        lhs = jnp.concatenate([rows, first, first], axis=0).T.astype(BF16)
+        size = 8 * caps[k]
+        ref[starts[k] : starts[k] + size, :] = jnp.dot(lhs[:size], rhs, preferred_element_type=F32)
+
+    def forces(k, ref):
+        size = 8 * caps[k]
+        square = jnp.maximum(ref[starts[k] : starts[k] + size, :TILE], 1e-12)
+        distance = square * lax.rsqrt(square)
+        overlap = jnp.maximum(ref[starts[k] : starts[k] + size, TILE:] - distance, 0.0)
+        below = distance + SOFTEN
+        guess = pl.reciprocal(below, approx=True)
+        force = overlap * (guess * (2.0 - below * guess))
+        if first_chunk + k == 0:
+            at = iota((TILE, TILE), 0) == iota((TILE, TILE), 1)
+            force = jnp.where(at, 0.0, force)
+        high = force.astype(BF16)
+        low = (force - high.astype(F32)).astype(BF16)
+        rest = TILE - size
+        if rest:
+            none = jnp.zeros((rest, TILE), BF16)
+            high, low = (jnp.concatenate([v, none], axis=0) for v in (high, low))
+        return high, low
+
+    def add_up(t, found):
+        moments = []
+        for features, products, n in chunks:
+            first = features[pl.ds(16 * n * PITCH_ROWS + t, 8, stride=PITCH_ROWS), :]
+            more = products[pl.ds(16 * n * PITCH_ROWS + t, 16, stride=PITCH_ROWS), :]
+            moments.append(jnp.concatenate([first, more, first], axis=0))
+        lhs = jnp.concatenate(moments, axis=1).astype(BF16)
+        highs = jnp.concatenate([p[0] for p in found], axis=0)
+        lows = jnp.concatenate([p[1] for p in found], axis=0)
+        one = jnp.dot(lhs, highs, preferred_element_type=F32)
+        two = jnp.dot(lhs[:16], lows, preferred_element_type=F32)
+        sum_ref[pl.ds(t, 8, stride=PITCH_ROWS), :] = one[:8] + two[:8]
+        sum_ref[pl.ds(8 * PITCH_ROWS + t, 8, stride=PITCH_ROWS), :] = one[8:16] + (one[16:24] + two[8:])
+
+    def step(t, here_ref, next_t, next_ref):
+        rhs = own_side(next_t)
+        found = []
+        for k in range(len(chunks)):
+            measure_pairs(next_t, k, rhs, next_ref)
+            found.append(forces(k, here_ref))
+        add_up(t, found)
+
+    first_rhs = own_side(0)
+    for k in range(len(chunks)):
+        measure_pairs(0, k, first_rhs, even_ref)
+
+    def eight_tiles(q, carry):
+        refs = (even_ref, odd_ref)
+        for i in range(8):
+            t = 8 * q + i
+            step(t, refs[i % 2], t + 1 if i < 7 else jnp.minimum(t + 1, NB - 1), refs[1 - i % 2])
+        return carry
+
+    lax.fori_loop(0, NB // 8, eight_tiles, 0)
+
+
+def table(rows):
+    return on_chip((rows * PITCH_ROWS, TILE))
+
+
+def pair_space(chunks, groups):
+    return [table(16 * chunks), table(16 * chunks)] + [pltpu.VMEM((8 * groups, 2 * TILE), F32)] * 2
+
+
+def own_kernel(grains_ref, own_ref, sum_ref, feature_ref, moment_ref, even_ref, odd_ref):
+    keep_chunks([[grains_ref[c] for c in range(4)]], feature_ref, moment_ref, own_ref)
+    pair_loop([(feature_ref, moment_ref, 0)], 0, own_ref, sum_ref, even_ref, odd_ref)
+
+
+def pair_own(grains):
+    return plain_call(own_kernel, [table(38), table(16)], "own", held(grains), scratch=pair_space(1, CAPS[0]))
+
+
+def near_kernel(grid_ref, lists_ref, excess_ref, feature_ref, moment_ref):
     tri = running_sums()
     here = in_this_frame(grid_ref)
     low_z = TILE_BOX_EDGE * (iota((64, TILE), 0) >> 5).astype(F32)
@@ -319,16 +412,15 @@
         tri,
     )
     excess_ref[...] = excess((count_z, count_y), CAPS[1:3])
-    chunks = [cut_y(level, 1), cut_y(beside_z, 1), beside_y]
+    chunks = [cut_y(beside_z, 1), beside_y]
     for k in range(2):
         for c in range(4):
-            lists_ref[4 * k + c] = chunks[1 + k][c]
-    keep_chunks(chunks, feature_ref, moment_ref, own_ref)
+            lists_ref[4 * k + c] = chunks[k][c]
+    keep_chunks(chunks, feature_ref, moment_ref)
 
 
 def find_near(grid):
-    table = lambda rows: on_chip((rows * PITCH_ROWS, TILE))
-    shapes = [on_chip((8, NB, TILE)), on_chip((1, TILE)), table(3 * 16), table(3 * 16), table(38)]
+    shapes = [on_chip((8, NB, TILE)), on_chip((1, TILE)), table(2 * 16), table(2 * 16)]
     return plain_call(near_kernel, shapes, "near", held(grid))
 
 
@@ -341,7 +433,8 @@
 
 
 def stress_kernel(
-    grid_ref, side_ref, grains_ref, plane_ref, lists_ref, excess_ref, feature_near_ref, moment_near_ref, own_ref,
+    grid_ref, side_ref, grains_ref, plane_ref, own_ref, own_sum_ref,
+    lists_ref, excess_ref, feature_near_ref, moment_near_ref,
     rim0_ref, rim1_ref, out_ref,
     all_ref, contact_ref, height_ref, feature_far_ref, moment_far_ref, sum_ref, even_ref, odd_ref,
 ):
@@ -402,9 +495,6 @@
         excess_ref[...], excess((count_e, count_x, count_w), (TILE // 8,) + CAPS[3:])
     )
     overflow = jnp.max(overflow)
-
-    def table(near_ref, far_ref, k):
-        return (near_ref, k) if k < 3 else (far_ref, k - 3)
 
     at_z = iota((8, TILE), 0)
     centres_inner = centres(at_z + 4)
@@ -450,81 +540,11 @@
 
     @pl.when(overflow <= 0.0)
     def _():
-        sub = iota((8, TILE), 0)
-        starts = [8 * sum(CAPS[:k]) for k in range(5)]
-
-        def own_side(t):
-            radii = [own_ref[pl.ds((32 + p) * PITCH_ROWS + t, 1), :] for p in range(3)]
-            radii = [jnp.where(sub == 6, jnp.broadcast_to(r, (8, TILE)), 0.0) for r in radii]
-            reach = [radii[0], jnp.where(sub >= 5, 1.0, 0.0), radii[1], radii[2]]
-            return jnp.concatenate(
-                [own_ref[pl.ds(t, 32, stride=PITCH_ROWS), :], jnp.concatenate(reach, axis=0)], axis=1
-            ).astype(BF16)
-
-        def measure_pairs(t, k, rhs, ref):
-            source, n = table(feature_near_ref, feature_far_ref, k)
-            rows = source[pl.ds(16 * n * PITCH_ROWS + t, 16, stride=PITCH_ROWS), :]
-            first = rows[:8]
-            lhs = jnp.concatenate([rows, first, first], axis=0).T.astype(BF16)
-            size = 8 * CAPS[k]
-            ref[starts[k] : starts[k] + size, :] = jnp.dot(lhs[:size], rhs, preferred_element_type=F32)
-
-        def forces(k, ref):
-            size = 8 * CAPS[k]
-            square = jnp.maximum(ref[starts[k] : starts[k] + size, :TILE], 1e-12)
-            distance = square * lax.rsqrt(square)
-            overlap = jnp.maximum(ref[starts[k] : starts[k] + size, TILE:] - distance, 0.0)
-            below = distance + SOFTEN
-            guess = pl.reciprocal(below, approx=True)
-            force = overlap * (guess * (2.0 - below * guess))
-            if k == 0:
-                at = iota((TILE, TILE), 0) == iota((TILE, TILE), 1)
-                force = jnp.where(at, 0.0, force)
-            high = force.astype(BF16)
-            low = (force - high.astype(F32)).astype(BF16)
-            rest = TILE - size
-            if rest:
-                none = jnp.zeros((rest, TILE), BF16)
-                high, low = (jnp.concatenate([v, none], axis=0) for v in (high, low))
-            return high, low
-
-        def add_up(t, parts):
-            moments = []
-            for k in range(5):
-                source, n = table(feature_near_ref, feature_far_ref, k)
-                first = source[pl.ds(16 * n * PITCH_ROWS + t, 8, stride=PITCH_ROWS), :]
-                source, n = table(moment_near_ref, moment_far_ref, k)
-                more = source[pl.ds(16 * n * PITCH_ROWS + t, 16, stride=PITCH_ROWS), :]
-                moments.append(jnp.concatenate([first, more, first], axis=0))
-            lhs = jnp.concatenate(moments, axis=1).astype(BF16)
-            highs = jnp.concatenate([p[0] for p in parts], axis=0)
-            lows = jnp.concatenate([p[1] for p in parts], axis=0)
-            one = jnp.dot(lhs, highs, preferred_element_type=F32)
-            two = jnp.dot(lhs[:16], lows, preferred_element_type=F32)
-            sum_ref[pl.ds(t, 8, stride=PITCH_ROWS), :] = one[:8] + two[:8]
-            sum_ref[pl.ds(8 * PITCH_ROWS + t, 8, stride=PITCH_ROWS), :] = one[8:16] + (one[16:24] + two[8:])
-
-        def step(t, here_ref, next_t, next_ref):
-            rhs = own_side(next_t)
-            parts = []
-            for k in range(5):
-                measure_pairs(next_t, k, rhs, next_ref)
-                parts.append(forces(k, here_ref))
-            add_up(t, parts)
-
-        first_rhs = own_side(0)
-        for k in range(5):
-            measure_pairs(0, k, first_rhs, even_ref)
-
-        def eight_tiles(q, carry):
-            refs = (even_ref, odd_ref)
-            for i in range(8):
-                t = 8 * q + i
-                step(t, refs[i % 2], t + 1 if i < 7 else jnp.minimum(t + 1, NB - 1), refs[1 - i % 2])
-            return carry
-
-        lax.fori_loop(0, NB // 8, eight_tiles, 0)
-        total = [sum_ref[m * PITCH_ROWS : m * PITCH_ROWS + NB, :] for m in range(14)]
+        tables = [(feature_near_ref, moment_near_ref, k) for k in range(2)]
+        tables += [(feature_far_ref, moment_far_ref, k) for k in range(2)]
+        pair_loop(tables, 1, own_ref, sum_ref, even_ref, odd_ref)
+        rows = lambda ref, m: ref[m * PITCH_ROWS : m * PITCH_ROWS + NB, :]
+        total = [rows(sum_ref, m) + rows(own_sum_ref, m) for m in range(14)]
         first = [total[c] + total[3 + c] for c in range(3)]
         own_mid = [own_ref[(35 + c) * PITCH_ROWS : (35 + c) * PITCH_ROWS + NB, :] for c in range(3)]
         for k, (i, j) in enumerate(((0, 0), (1, 1), (2, 2), (0, 1), (0, 2), (1, 2))):
@@ -603,8 +623,8 @@
             pltpu.VMEM((2 * 16 * PITCH_ROWS, TILE), F32),
             pltpu.VMEM((2 * 16 * PITCH_ROWS, TILE), F32),
             pltpu.VMEM((16 * PITCH_ROWS, TILE), F32),
-            pltpu.VMEM((8 * sum(CAPS), 2 * TILE), F32),
-            pltpu.VMEM((8 * sum(CAPS), 2 * TILE), F32),
+            pltpu.VMEM((8 * sum(CAPS[1:]), 2 * TILE), F32),
+            pltpu.VMEM((8 * sum(CAPS[1:]), 2 * TILE), F32),
         ],
     )
 
@@ -765,10 +785,12 @@
 def local(grains, pairs):
     own, near = box_sort(grains, pairs)
     cube = near.reshape(4, 2, 2, 8, TILE)
-    below, above = exchange(cube[:, 0], cube[:, 1], "gz")
+    sends, placed = lax.optimization_barrier(((cube[:, 0], cube[:, 1]), own))
+    own_table, own_sums = pair_own(placed)
+    below, above = exchange(*sends, "gz")
     cube = jnp.concatenate([below[:, None], cube, above[:, None]], axis=1)
     sends = (cube[:, :, 0], cube[:, :, 1])
-    sends, placed = lax.optimization_barrier((sends, own))
+    sends, placed, own_table, own_sums = lax.optimization_barrier((sends, own, own_table, own_sums))
     plane = plain_call(
         plane_kernel, on_chip((3 * TILE + COLS, NB * TILE), BF16), "plane", held(placed)
     )
@@ -780,7 +802,9 @@
     tables = find_near(placed.reshape(4, 128, TILE))
     below, above = exchange(*sends, "gx")
     side = jnp.stack([below, above]).reshape(2, 4, 16, TILE)
-    rim0, rim1, wide = stress_and_deposit(cube.reshape(4, 128, TILE), side, own.reshape(7 * NB, TILE), plane, *tables)
+    rim0, rim1, wide = stress_and_deposit(
+        cube.reshape(4, 128, TILE), side, own.reshape(7 * NB, TILE), plane, own_table, own_sums, *tables
+    )
     first, second = swaps(rim0, rim1, "gx")
     rows = field_rows()
     block, square = on_chip((rows, TILE)), on_chip((rows, COLS))

time: 49.8 us -> 48.9 us (0.982)
  waiting for transfers between devices: 12.7 us -> 10.9 us
  Pallas kernels: 19.4 us -> 20.8 us
  starting transfers between devices: 15.8 us -> 15.2 us
    ppermute x10, waiting for transfers between devices: 12.7 us -> 10.9 us  [swaps(): lax.ppermute(value, axis, links)]
    pallas_call x7 -> x8, Pallas kernels: 19.4 us -> 20.8 us  [plain_call(): pl.pallas_call(kernel, out_shape=shapes, in_specs=[vmem] * len(args), out...]
    ppermute x10, starting transfers between devices: 15.8 us -> 15.2 us  [swaps(): lax.ppermute(value, axis, links)]
  transfers between devices with their start and end apart: 10 -> 10, of which waited for: 7 -> 6; matrix products, arithmetic and copies ran while one was open for 1% -> 1% of each run, Pallas kernels for 11% -> 17%
where the time goes in v7:
time: 48.9 us; the launch traced here: 48.7 us
  Pallas kernels  20.8 us (43%)
  starting transfers between devices  15.2 us (31%)
  waiting for transfers between devices  10.9 us (22%)
  between operations  0.9 us (2%)
  local copies, waits for them, and re-layouts  0.51 us (1%)
    pallas_call x8, Pallas kernels, plain_call(): pl.pallas_call(kernel, out_shape=shapes, in_specs=[vmem] * len(args), out...  20.8 us
    ppermute x10, starting transfers between devices, swaps(): lax.ppermute(value, axis, links)  15.2 us
    ppermute x10, waiting for transfers between devices, swaps(): lax.ppermute(value, axis, links)  10.9 us
  transfers between devices with their start and end apart: 10, of which 6 were waited for; matrix products, arithmetic and copies ran while one was open for 1% of the time, Pallas kernels for 17%

profile of v7, /device:TPU:10, one launch (start us, length us, event | category | flops | bytes accessed | tf_op | source)
XLA Modules:
  0.0 48.7 jit_solution(6780404000514104947)
XLA Ops:
  0.6 1.3 %box_sort.1 = (f32[7,32,128]{2,1,0:T(8,128)S(1)}, f32[4,32,128]{2,1,0:T(8,128)S(1)}) custom-call(f32[7,32,128]{2,1,0:T(8,128)} %bitcast.68, s32[27,1,32]{2,1,0:T(1,128)} %bitcast.78), custom_call_target="tpu_custom_call" | custom-call | tf_op jit(solution)/shard_map/box_sort/pallas_call | solution.py:733
  2.0 1.6 %collective-permute-start = (f32[4,2,8,128]{3,0,2,1:T(4,128)S(1)}, f32[4,2,8,128]{3,0,2,1:T(4,128)S(1)}, u32[]{:S(2)}, u32[]{:S(2)}) collective-permute-start(f32[4,2,8,128]{3,0,2,1:T(4,128)S(1)} %bitcast.73), channel_id=1, source_target_pairs={{0,1},{1,0},{2,3},{3,2},{4,5},{5,4},{6,7},{7,6},{8,9},{9,8},{10,11... | collective-permute-start | bytes 98312 | tf_op jit(solution)/shard_map/ppermute | solution.py:775
  3.6 2.9 %own.1 = (f32[1520,128]{1,0:T(8,128)S(1)}, f32[640,128]{1,0:T(8,128)S(1)}) custom-call(f32[7,32,128]{2,1,0:T(8,128)S(1)} %get-tuple-element.41.grains_ref.own_ref), custom_call_target="tpu_custom_call" | custom-call | tf_op jit(solution)/shard_map/own/pallas_call | solution.py:733
  6.5 0.0 collective-permute-done
  6.5 0.1 pad_maximum_fusion.1
  6.6 3.5 %collective-permute-start.1 = (f32[4,4,8,128]{3,1,0,2:T(4,128)S(1)}, f32[4,4,8,128]{3,1,0,2:T(4,128)S(1)}, u32[]{:S(2)}, u32[]{:S(2)}) collective-permute-start(f32[4,4,8,128]{3,1,0,2:T(4,128)S(1)} %bitcast.72), channel_id=1, source_target_pairs={{2,4},{4,2},{3,5},{5,3},{10,12},{12,10},{11,13},{13,11},{18,20},{2... | collective-permute-start | bytes 196616 | tf_op jit(solution)/shard_map/ppermute | solution.py:775
  10.1 0.1 collective-permute-start.2
  10.2 0.1 copy.11
  10.3 3.6 %plane.1.plane_ref = bf16[640,4096]{1,0:T(8,128)(2,1)S(1)} custom-call(f32[7,32,128]{2,1,0:T(8,128)S(1)} %get-tuple-element.41.grains_ref.own_ref), custom_call_target="tpu_custom_call" | custom-call | tf_op jit(solution)/shard_map/plane/pallas_call | solution.py:733
  14.0 0.5 collective-permute-done.2
  14.5 0.2 pad_maximum_fusion
  14.7 1.9 %collective-permute-start.3 = (f32[4,4,4,128]{3,2,1,0:T(4,128)S(1)}, f32[4,4,4,128]{3,2,1,0:T(4,128)S(1)}, u32[]{:S(2)}, u32[]{:S(2)}) collective-permute-start(f32[4,4,4,128]{3,2,1,0:T(4,128)S(1)} %bitcast.77), channel_id=1, source_target_pairs={{8,16},{16,8},{9,17},{17,9},{10,18},{18,10},{11,19},{19,11},{12,20... | collective-permute-start | bytes 98312 | tf_op jit(solution)/shard_map/ppermute | solution.py:775
  16.6 0.1 collective-permute-start.4
  16.7 0.2 copy.12
  16.9 0.2 copy.13
  17.0 1.8 %near.1 = (f32[8,32,128]{2,1,0:T(8,128)S(1)}, f32[1,128]{1,0:T(1,128)S(1)}, f32[1280,128]{1,0:T(8,128)S(1)}, f32[1280,128]{1,0:T(8,128)S(1)}) custom-call(f32[4,128,128]{2,1,0:T(8,128)S(1)} %bitcast.52), custom_call_target="tpu_custom_call" | custom-call | tf_op jit(solution)/shard_map/near/pallas_call | solution.py:733
  18.8 1.1 %collective-permute-done.3 = f32[4,4,4,128]{3,2,1,0:T(4,128)S(1)} collective-permute-done((f32[4,4,4,128]{3,2,1,0:T(4,128)S(1)}, f32[4,4,4,128]{3,2,1,0:T(4,128)S(1)}, u32[]{:S(2)}, u32[]{:S(2)}) %collective-permute-start.3) | collective-permute-done | bytes 32800 | tf_op jit(solution)/shard_map/ppermute | solution.py:775
  19.9 0.0 collective-permute-done.4
  20.0 10.0 %stress_deposit.1 = (f32[64,128]{1,0:T(8,128)S(1)}, f32[64,128]{1,0:T(8,128)S(1)}, f32[128,512]{1,0:T(8,128)S(1)}) custom-call(f32[4,128,128]{2,1,0:T(8,128)S(1)} %bitcast.51, f32[2,4,16,128]{3,2,1,0:T(8,128)S(1)} %pad_maximum_fusion.2.side_ref, f32[224,128]{1,0:T(8,128)S(1)} %bitcast.53, bf16[640,4096]{1,0:T(8,128)(2,1)S(1)} %plane.1.plane_ref, ...), custom_call_target="tpu_custom_call" | custom-call | tf_op jit(solution)/shard_map/stress_deposit/pallas_call | solution.py:733
  30.0 0.1 collective-permute-start.5
  30.1 3.0 %collective-permute-start.6 = (f32[64,128]{1,0:T(8,128)S(1)}, f32[64,128]{1,0:T(8,128)S(1)}, u32[]{:S(2)}, u32[]{:S(2)}) collective-permute-start(f32[64,128]{1,0:T(8,128)S(1)} %get-tuple-element.55), channel_id=1, source_target_pairs={{8,16},{16,8},{9,17},{17,9},{10,18},{18,10},{11,19},{19,11},{12,20... | collective-permute-start | bytes 98312 | tf_op jit(solution)/shard_map/ppermute | solution.py:775
  33.1 0.0 collective-permute-done.5.first_ref
  33.1 2.2 %collective-permute-done.6.second_ref = f32[64,128]{1,0:T(8,128)S(1)} collective-permute-done((f32[64,128]{1,0:T(8,128)S(1)}, f32[64,128]{1,0:T(8,128)S(1)}, u32[]{:S(2)}, u32[]{:S(2)}) %collective-permute-start.6) | collective-permute-done | bytes 32800 | tf_op jit(solution)/shard_map/ppermute | solution.py:775
  35.3 0.3 rim_x.1
  35.7 1.6 %collective-permute-start.7 = (f32[128,128]{1,0:T(8,128)S(1)}, f32[128,128]{1,0:T(8,128)S(1)}, u32[]{:S(2)}, u32[]{:S(2)}) collective-permute-start(f32[128,128]{1,0:T(8,128)S(1)} %get-tuple-element.57), channel_id=1, source_target_pairs={{0,2},{2,0},{4,6},{6,4},{1,3},{3,1},{5,7},{7,5},{8,10},{10,8},{12,... | collective-permute-start | bytes 196616 | tf_op jit(solution)/shard_map/ppermute | solution.py:775
  37.3 2.3 %collective-permute-start.8 = (f32[128,128]{1,0:T(8,128)S(1)}, f32[128,128]{1,0:T(8,128)S(1)}, u32[]{:S(2)}, u32[]{:S(2)}) collective-permute-start(f32[128,128]{1,0:T(8,128)S(1)} %get-tuple-element.58), channel_id=1, source_target_pairs={{2,4},{4,2},{3,5},{5,3},{10,12},{12,10},{11,13},{13,11},{18,20},{2... | collective-permute-start | bytes 196616 | tf_op jit(solution)/shard_map/ppermute | solution.py:775
  39.6 0.4 collective-permute-done.7.first_ref
  40.0 3.4 %collective-permute-done.8.second_ref = f32[128,128]{1,0:T(8,128)S(1)} collective-permute-done((f32[128,128]{1,0:T(8,128)S(1)}, f32[128,128]{1,0:T(8,128)S(1)}, u32[]{:S(2)}, u32[]{:S(2)}) %collective-permute-start.8) | collective-permute-done | bytes 65568 | tf_op jit(solution)/shard_map/ppermute | solution.py:775
  43.4 0.2 rim_y.1
  43.7 1.1 %collective-permute-start.9 = (f32[128,128]{1,0:T(8,128)S(1)}, f32[128,128]{1,0:T(8,128)S(1)}, u32[]{:S(2)}, u32[]{:S(2)}) collective-permute-start(f32[128,128]{1,0:T(8,128)S(1)} %get-tuple-element.60), channel_id=1, source_target_pairs={{0,1},{1,0},{2,3},{3,2},{4,5},{5,4},{6,7},{7,6},{8,9},{9,8},{10,11... | collective-permute-start | bytes 196616 | tf_op jit(solution)/shard_map/ppermute | solution.py:775
  44.7 3.3 %collective-permute-done.9.got_ref = f32[128,128]{1,0:T(8,128)S(1)} collective-permute-done((f32[128,128]{1,0:T(8,128)S(1)}, f32[128,128]{1,0:T(8,128)S(1)}, u32[]{:S(2)}, u32[]{:S(2)}) %collective-permute-start.9) | collective-permute-done | bytes 65568 | tf_op jit(solution)/shard_map/ppermute | solution.py:775
  48.0 0.7 %finish.1 = (f32[1,1,1,10,8,256]{5,4,3,2,1,0:T(8,128)}, f32[1,1,2,128]{3,2,1,0:T(2,128)}, f32[1,1,16,128]{3,2,1,0:T(8,128)}) custom-call(f32[128,256]{1,0:T(8,128)S(1)} %get-tuple-element.59.total_ref, f32[128,128]{1,0:T(8,128)S(1)} %collective-permute-done.9.got_ref), custom_call_target="tpu_custom_call" | custom-call | tf_op jit(solution)/shard_map/finish/pallas_call | solution.py:733
  (13 shorter events, 0.2 us)
Async XLA Ops:
  2.0 4.5 %collective-permute-start = (f32[4,2,8,128]{3,0,2,1:T(4,128)S(1)}, f32[4,2,8,128]{3,0,2,1:T(4,128)S(1)}, u32[]{:S(2)}, u32[]{:S(2)}) collective-permute-start(f32[4,2,8,128]{3,0,2,1:T(4,128)S(1)} %bitcast.73), channel_id=1, source_target_pairs={{0,1},{1,0},{2,3},{3,2},{4,5},{5,4},{6,7},{7,6},{8,9},{9,8},{10,11... | collective-permute-start | bytes 98312 | tf_op jit(solution)/shard_map/ppermute | solution.py:775
  6.6 7.4 %collective-permute-start.1 = (f32[4,4,8,128]{3,1,0,2:T(4,128)S(1)}, f32[4,4,8,128]{3,1,0,2:T(4,128)S(1)}, u32[]{:S(2)}, u32[]{:S(2)}) collective-permute-start(f32[4,4,8,128]{3,1,0,2:T(4,128)S(1)} %bitcast.72), channel_id=1, source_target_pairs={{2,4},{4,2},{3,5},{5,3},{10,12},{12,10},{11,13},{13,11},{18,20},{2... | collective-permute-start | bytes 196616 | tf_op jit(solution)/shard_map/ppermute | solution.py:775
  10.1 4.3 %collective-permute-start.2 = (f32[4,4,8,128]{3,1,0,2:T(4,128)S(1)}, f32[4,4,8,128]{3,1,0,2:T(4,128)S(1)}, u32[]{:S(2)}, u32[]{:S(2)}) collective-permute-start(f32[4,4,8,128]{3,1,0,2:T(4,128)S(1)} %bitcast.70), channel_id=1, source_target_pairs={{0,2},{2,0},{4,6},{6,4},{1,3},{3,1},{5,7},{7,5},{8,10},{10,8},{12,... | collective-permute-start | bytes 196616 | tf_op jit(solution)/shard_map/ppermute | solution.py:775
  14.7 5.2 %collective-permute-start.3 = (f32[4,4,4,128]{3,2,1,0:T(4,128)S(1)}, f32[4,4,4,128]{3,2,1,0:T(4,128)S(1)}, u32[]{:S(2)}, u32[]{:S(2)}) collective-permute-start(f32[4,4,4,128]{3,2,1,0:T(4,128)S(1)} %bitcast.77), channel_id=1, source_target_pairs={{8,16},{16,8},{9,17},{17,9},{10,18},{18,10},{11,19},{19,11},{12,20... | collective-permute-start | bytes 98312 | tf_op jit(solution)/shard_map/ppermute | solution.py:775
  16.6 3.3 %collective-permute-start.4 = (f32[4,4,4,128]{3,2,1,0:T(4,128)S(1)}, f32[4,4,4,128]{3,2,1,0:T(4,128)S(1)}, u32[]{:S(2)}, u32[]{:S(2)}) collective-permute-start(f32[4,4,4,128]{3,2,1,0:T(4,128)S(1)} %bitcast.75), channel_id=1, source_target_pairs={{0,8},{8,0},{16,24},{24,16},{1,9},{9,1},{17,25},{25,17},{2,10},{10... | collective-permute-start | bytes 98312 | tf_op jit(solution)/shard_map/ppermute | solution.py:775
  30.0 3.1 %collective-permute-start.5 = (f32[64,128]{1,0:T(8,128)S(1)}, f32[64,128]{1,0:T(8,128)S(1)}, u32[]{:S(2)}, u32[]{:S(2)}) collective-permute-start(f32[64,128]{1,0:T(8,128)S(1)} %get-tuple-element.54), channel_id=1, source_target_pairs={{0,8},{8,0},{16,24},{24,16},{1,9},{9,1},{17,25},{25,17},{2,10},{10... | collective-permute-start | bytes 98312 | tf_op jit(solution)/shard_map/ppermute | solution.py:775
  30.1 5.2 %collective-permute-start.6 = (f32[64,128]{1,0:T(8,128)S(1)}, f32[64,128]{1,0:T(8,128)S(1)}, u32[]{:S(2)}, u32[]{:S(2)}) collective-permute-start(f32[64,128]{1,0:T(8,128)S(1)} %get-tuple-element.55), channel_id=1, source_target_pairs={{8,16},{16,8},{9,17},{17,9},{10,18},{18,10},{11,19},{19,11},{12,20... | collective-permute-start | bytes 98312 | tf_op jit(solution)/shard_map/ppermute | solution.py:775
  35.7 4.3 %collective-permute-start.7 = (f32[128,128]{1,0:T(8,128)S(1)}, f32[128,128]{1,0:T(8,128)S(1)}, u32[]{:S(2)}, u32[]{:S(2)}) collective-permute-start(f32[128,128]{1,0:T(8,128)S(1)} %get-tuple-element.57), channel_id=1, source_target_pairs={{0,2},{2,0},{4,6},{6,4},{1,3},{3,1},{5,7},{7,5},{8,10},{10,8},{12,... | collective-permute-start | bytes 196616 | tf_op jit(solution)/shard_map/ppermute | solution.py:775
  37.3 6.1 %collective-permute-start.8 = (f32[128,128]{1,0:T(8,128)S(1)}, f32[128,128]{1,0:T(8,128)S(1)}, u32[]{:S(2)}, u32[]{:S(2)}) collective-permute-start(f32[128,128]{1,0:T(8,128)S(1)} %get-tuple-element.58), channel_id=1, source_target_pairs={{2,4},{4,2},{3,5},{5,3},{10,12},{12,10},{11,13},{13,11},{18,20},{2... | collective-permute-start | bytes 196616 | tf_op jit(solution)/shard_map/ppermute | solution.py:775
  43.7 4.3 %collective-permute-start.9 = (f32[128,128]{1,0:T(8,128)S(1)}, f32[128,128]{1,0:T(8,128)S(1)}, u32[]{:S(2)}, u32[]{:S(2)}) collective-permute-start(f32[128,128]{1,0:T(8,128)S(1)} %get-tuple-element.60), channel_id=1, source_target_pairs={{0,1},{1,0},{2,3},{3,2},{4,5},{5,4},{6,7},{7,6},{8,9},{9,8},{10,11... | collective-permute-start | bytes 196616 | tf_op jit(solution)/shard_map/ppermute | solution.py:775

commit v8 on v7

--- a/solution.py
+++ b/solution.py
@@ -122,7 +122,8 @@
     both = jnp.dot(jnp.concatenate(masks, axis=0), tri, preferred_element_type=F32)
     rows = masks[0].shape[0]
     ranks = both[:, :TILE]
-    totals = [both[n * rows : (n + 1) * rows, TILE:] for n in range(len(masks))]
+    totals = [both[n * rows : (n + 1) * rows, TILE : 2 * TILE] for n in range(len(masks))]
+    upto = {m: both[:, (2 + i) * TILE : (3 + i) * TILE] for i, m in enumerate(LANDMARKS)}
     offsets, ends, at = [], [], 0
     for lists in groups:
         offset = jnp.zeros((rows, TILE), F32)
@@ -133,8 +134,11 @@
         ends.append(offset)
     lane_f = iota((rows, TILE), 1).astype(F32)
     wanted = jnp.concatenate([lane_f - offset for offset in offsets], axis=0)
-    place = jnp.zeros(wanted.shape, jnp.int32)
-    for bit in (64, 32, 16, 8, 4, 2, 1):
+    by_64 = upto[63] <= wanted
+    by_32 = jnp.where(by_64, upto[95], upto[31]) <= wanted
+    probe = jnp.where(by_64, jnp.where(by_32, upto[111], upto[79]), jnp.where(by_32, upto[47], upto[15]))
+    place = jnp.where(by_64, 64, 0) + jnp.where(by_32, 32, 0) + jnp.where(probe <= wanted, 16, 0)
+    for bit in (8, 4, 2, 1):
         place = jnp.where(lane_take(ranks, place + (bit - 1)) <= wanted, place + bit, place)
     packed, at = [], 0
     for lists, end in zip(groups, ends):
@@ -200,9 +204,13 @@
 SPAN_Z = BOXES_NORMAL * TILE_BOX_EDGE
 
 
+LANDMARKS = (15, 31, 47, 63, 79, 95, 111)
+
+
 def running_sums():
-    row, col = iota((TILE, 2 * TILE), 0), iota((TILE, 2 * TILE), 1)
-    return jnp.where((row <= col) | (col >= TILE), 1.0, 0.0).astype(BF16)
+    row, col = iota((TILE, TILE), 0), iota((TILE, TILE), 1)
+    blocks = [row <= col] + [row <= last for last in (TILE - 1,) + LANDMARKS]
+    return jnp.concatenate([jnp.where(b, 1.0, 0.0) for b in blocks], axis=1).astype(BF16)
 
 
 def shifts(place, span):

time: 48.9 us -> 48.4 us (0.990)
  Pallas kernels: 20.8 us -> 19.9 us
  waiting for transfers between devices: 10.9 us -> 11.7 us
    pallas_call x8, Pallas kernels: 20.8 us -> 19.9 us  [plain_call(): pl.pallas_call(kernel, out_shape=shapes, in_specs=[vmem] * len(args), out...]
    ppermute x10, waiting for transfers between devices: 10.9 us -> 11.7 us  [swaps(): lax.ppermute(value, axis, links)]
  transfers between devices with their start and end apart: 10 -> 10, of which waited for: 6 -> 6; matrix products, arithmetic and copies ran while one was open for 1% -> 1% of each run, Pallas kernels for 17% -> 16%
where the time goes in v8:
time: 48.4 us; the launch traced here: 48.2 us
  Pallas kernels  19.9 us (41%)
  starting transfers between devices  14.8 us (31%)
  waiting for transfers between devices  11.7 us (24%)
  between operations  0.9 us (2%)
  local copies, waits for them, and re-layouts  0.51 us (1%)
    pallas_call x8, Pallas kernels, plain_call(): pl.pallas_call(kernel, out_shape=shapes, in_specs=[vmem] * len(args), out...  19.9 us
    ppermute x10, starting transfers between devices, swaps(): lax.ppermute(value, axis, links)  14.8 us
    ppermute x10, waiting for transfers between devices, swaps(): lax.ppermute(value, axis, links)  11.7 us
  transfers between devices with their start and end apart: 10, of which 6 were waited for; matrix products, arithmetic and copies ran while one was open for 1% of the time, Pallas kernels for 16%

profile of v8, /device:TPU:10, one launch (start us, length us, event | category | flops | bytes accessed | tf_op | source)
XLA Modules:
  0.0 48.2 jit_solution(2865973869968047207)
XLA Ops:
  0.6 1.3 %box_sort.1 = (f32[7,32,128]{2,1,0:T(8,128)S(1)}, f32[4,32,128]{2,1,0:T(8,128)S(1)}) custom-call(f32[7,32,128]{2,1,0:T(8,128)} %bitcast.68, s32[27,1,32]{2,1,0:T(1,128)} %bitcast.78), custom_call_target="tpu_custom_call" | custom-call | tf_op jit(solution)/shard_map/box_sort/pallas_call | solution.py:741
  2.0 1.6 %collective-permute-start = (f32[4,2,8,128]{3,0,2,1:T(4,128)S(1)}, f32[4,2,8,128]{3,0,2,1:T(4,128)S(1)}, u32[]{:S(2)}, u32[]{:S(2)}) collective-permute-start(f32[4,2,8,128]{3,0,2,1:T(4,128)S(1)} %bitcast.73), channel_id=1, source_target_pairs={{0,1},{1,0},{2,3},{3,2},{4,5},{5,4},{6,7},{7,6},{8,9},{9,8},{10,11... | collective-permute-start | bytes 98312 | tf_op jit(solution)/shard_map/ppermute | solution.py:783
  3.6 2.9 %own.1 = (f32[1520,128]{1,0:T(8,128)S(1)}, f32[640,128]{1,0:T(8,128)S(1)}) custom-call(f32[7,32,128]{2,1,0:T(8,128)S(1)} %get-tuple-element.41.grains_ref.own_ref), custom_call_target="tpu_custom_call" | custom-call | tf_op jit(solution)/shard_map/own/pallas_call | solution.py:741
  6.5 0.0 collective-permute-done
  6.5 0.1 pad_maximum_fusion.1
  6.6 3.5 %collective-permute-start.1 = (f32[4,4,8,128]{3,1,0,2:T(4,128)S(1)}, f32[4,4,8,128]{3,1,0,2:T(4,128)S(1)}, u32[]{:S(2)}, u32[]{:S(2)}) collective-permute-start(f32[4,4,8,128]{3,1,0,2:T(4,128)S(1)} %bitcast.72), channel_id=1, source_target_pairs={{2,4},{4,2},{3,5},{5,3},{10,12},{12,10},{11,13},{13,11},{18,20},{2... | collective-permute-start | bytes 196616 | tf_op jit(solution)/shard_map/ppermute | solution.py:783
  10.1 0.1 collective-permute-start.2
  10.2 0.1 copy.11
  10.3 3.6 %plane.1.plane_ref = bf16[640,4096]{1,0:T(8,128)(2,1)S(1)} custom-call(f32[7,32,128]{2,1,0:T(8,128)S(1)} %get-tuple-element.41.grains_ref.own_ref), custom_call_target="tpu_custom_call" | custom-call | tf_op jit(solution)/shard_map/plane/pallas_call | solution.py:741
  14.0 0.5 collective-permute-done.2
  14.5 0.2 pad_maximum_fusion
  14.7 1.9 %collective-permute-start.3 = (f32[4,4,4,128]{3,2,1,0:T(4,128)S(1)}, f32[4,4,4,128]{3,2,1,0:T(4,128)S(1)}, u32[]{:S(2)}, u32[]{:S(2)}) collective-permute-start(f32[4,4,4,128]{3,2,1,0:T(4,128)S(1)} %bitcast.77), channel_id=1, source_target_pairs={{8,16},{16,8},{9,17},{17,9},{10,18},{18,10},{11,19},{19,11},{12,20... | collective-permute-start | bytes 98312 | tf_op jit(solution)/shard_map/ppermute | solution.py:783
  16.6 0.1 collective-permute-start.4
  16.7 0.2 copy.12
  16.9 0.2 copy.13
  17.0 1.3 %near.1 = (f32[8,32,128]{2,1,0:T(8,128)S(1)}, f32[1,128]{1,0:T(1,128)S(1)}, f32[1280,128]{1,0:T(8,128)S(1)}, f32[1280,128]{1,0:T(8,128)S(1)}) custom-call(f32[4,128,128]{2,1,0:T(8,128)S(1)} %bitcast.52), custom_call_target="tpu_custom_call" | custom-call | tf_op jit(solution)/shard_map/near/pallas_call | solution.py:741
  18.4 1.6 %collective-permute-done.3 = f32[4,4,4,128]{3,2,1,0:T(4,128)S(1)} collective-permute-done((f32[4,4,4,128]{3,2,1,0:T(4,128)S(1)}, f32[4,4,4,128]{3,2,1,0:T(4,128)S(1)}, u32[]{:S(2)}, u32[]{:S(2)}) %collective-permute-start.3) | collective-permute-done | bytes 32800 | tf_op jit(solution)/shard_map/ppermute | solution.py:783
  19.9 0.0 collective-permute-done.4
  20.0 9.5 %stress_deposit.1 = (f32[64,128]{1,0:T(8,128)S(1)}, f32[64,128]{1,0:T(8,128)S(1)}, f32[128,512]{1,0:T(8,128)S(1)}) custom-call(f32[4,128,128]{2,1,0:T(8,128)S(1)} %bitcast.51, f32[2,4,16,128]{3,2,1,0:T(8,128)S(1)} %pad_maximum_fusion.2.side_ref, f32[224,128]{1,0:T(8,128)S(1)} %bitcast.53, bf16[640,4096]{1,0:T(8,128)(2,1)S(1)} %plane.1.plane_ref, ...), custom_call_target="tpu_custom_call" | custom-call | tf_op jit(solution)/shard_map/stress_deposit/pallas_call | solution.py:741
  29.5 0.1 collective-permute-start.5
  29.6 2.6 %collective-permute-start.6 = (f32[64,128]{1,0:T(8,128)S(1)}, f32[64,128]{1,0:T(8,128)S(1)}, u32[]{:S(2)}, u32[]{:S(2)}) collective-permute-start(f32[64,128]{1,0:T(8,128)S(1)} %get-tuple-element.55), channel_id=1, source_target_pairs={{8,16},{16,8},{9,17},{17,9},{10,18},{18,10},{11,19},{19,11},{12,20... | collective-permute-start | bytes 98312 | tf_op jit(solution)/shard_map/ppermute | solution.py:783
  32.2 0.0 collective-permute-done.5.first_ref
  32.2 2.6 %collective-permute-done.6.second_ref = f32[64,128]{1,0:T(8,128)S(1)} collective-permute-done((f32[64,128]{1,0:T(8,128)S(1)}, f32[64,128]{1,0:T(8,128)S(1)}, u32[]{:S(2)}, u32[]{:S(2)}) %collective-permute-start.6) | collective-permute-done | bytes 32800 | tf_op jit(solution)/shard_map/ppermute | solution.py:783
  34.8 0.3 rim_x.1
  35.1 1.6 %collective-permute-start.7 = (f32[128,128]{1,0:T(8,128)S(1)}, f32[128,128]{1,0:T(8,128)S(1)}, u32[]{:S(2)}, u32[]{:S(2)}) collective-permute-start(f32[128,128]{1,0:T(8,128)S(1)} %get-tuple-element.57), channel_id=1, source_target_pairs={{0,2},{2,0},{4,6},{6,4},{1,3},{3,1},{5,7},{7,5},{8,10},{10,8},{12,... | collective-permute-start | bytes 196616 | tf_op jit(solution)/shard_map/ppermute | solution.py:783
  36.8 2.3 %collective-permute-start.8 = (f32[128,128]{1,0:T(8,128)S(1)}, f32[128,128]{1,0:T(8,128)S(1)}, u32[]{:S(2)}, u32[]{:S(2)}) collective-permute-start(f32[128,128]{1,0:T(8,128)S(1)} %get-tuple-element.58), channel_id=1, source_target_pairs={{2,4},{4,2},{3,5},{5,3},{10,12},{12,10},{11,13},{13,11},{18,20},{2... | collective-permute-start | bytes 196616 | tf_op jit(solution)/shard_map/ppermute | solution.py:783
  39.1 0.4 collective-permute-done.7.first_ref
  39.5 3.4 %collective-permute-done.8.second_ref = f32[128,128]{1,0:T(8,128)S(1)} collective-permute-done((f32[128,128]{1,0:T(8,128)S(1)}, f32[128,128]{1,0:T(8,128)S(1)}, u32[]{:S(2)}, u32[]{:S(2)}) %collective-permute-start.8) | collective-permute-done | bytes 65568 | tf_op jit(solution)/shard_map/ppermute | solution.py:783
  42.9 0.2 rim_y.1
  43.2 1.1 %collective-permute-start.9 = (f32[128,128]{1,0:T(8,128)S(1)}, f32[128,128]{1,0:T(8,128)S(1)}, u32[]{:S(2)}, u32[]{:S(2)}) collective-permute-start(f32[128,128]{1,0:T(8,128)S(1)} %get-tuple-element.60), channel_id=1, source_target_pairs={{0,1},{1,0},{2,3},{3,2},{4,5},{5,4},{6,7},{7,6},{8,9},{9,8},{10,11... | collective-permute-start | bytes 196616 | tf_op jit(solution)/shard_map/ppermute | solution.py:783
  44.2 3.3 %collective-permute-done.9.got_ref = f32[128,128]{1,0:T(8,128)S(1)} collective-permute-done((f32[128,128]{1,0:T(8,128)S(1)}, f32[128,128]{1,0:T(8,128)S(1)}, u32[]{:S(2)}, u32[]{:S(2)}) %collective-permute-start.9) | collective-permute-done | bytes 65568 | tf_op jit(solution)/shard_map/ppermute | solution.py:783
  47.5 0.7 %finish.1 = (f32[1,1,1,10,8,256]{5,4,3,2,1,0:T(8,128)}, f32[1,1,2,128]{3,2,1,0:T(2,128)}, f32[1,1,16,128]{3,2,1,0:T(8,128)}) custom-call(f32[128,256]{1,0:T(8,128)S(1)} %get-tuple-element.59.total_ref, f32[128,128]{1,0:T(8,128)S(1)} %collective-permute-done.9.got_ref), custom_call_target="tpu_custom_call" | custom-call | tf_op jit(solution)/shard_map/finish/pallas_call | solution.py:741
  (13 shorter events, 0.2 us)
Async XLA Ops:
  2.0 4.5 %collective-permute-start = (f32[4,2,8,128]{3,0,2,1:T(4,128)S(1)}, f32[4,2,8,128]{3,0,2,1:T(4,128)S(1)}, u32[]{:S(2)}, u32[]{:S(2)}) collective-permute-start(f32[4,2,8,128]{3,0,2,1:T(4,128)S(1)} %bitcast.73), channel_id=1, source_target_pairs={{0,1},{1,0},{2,3},{3,2},{4,5},{5,4},{6,7},{7,6},{8,9},{9,8},{10,11... | collective-permute-start | bytes 98312 | tf_op jit(solution)/shard_map/ppermute | solution.py:783
  6.6 7.4 %collective-permute-start.1 = (f32[4,4,8,128]{3,1,0,2:T(4,128)S(1)}, f32[4,4,8,128]{3,1,0,2:T(4,128)S(1)}, u32[]{:S(2)}, u32[]{:S(2)}) collective-permute-start(f32[4,4,8,128]{3,1,0,2:T(4,128)S(1)} %bitcast.72), channel_id=1, source_target_pairs={{2,4},{4,2},{3,5},{5,3},{10,12},{12,10},{11,13},{13,11},{18,20},{2... | collective-permute-start | bytes 196616 | tf_op jit(solution)/shard_map/ppermute | solution.py:783
  10.1 4.3 %collective-permute-start.2 = (f32[4,4,8,128]{3,1,0,2:T(4,128)S(1)}, f32[4,4,8,128]{3,1,0,2:T(4,128)S(1)}, u32[]{:S(2)}, u32[]{:S(2)}) collective-permute-start(f32[4,4,8,128]{3,1,0,2:T(4,128)S(1)} %bitcast.70), channel_id=1, source_target_pairs={{0,2},{2,0},{4,6},{6,4},{1,3},{3,1},{5,7},{7,5},{8,10},{10,8},{12,... | collective-permute-start | bytes 196616 | tf_op jit(solution)/shard_map/ppermute | solution.py:783
  14.7 5.2 %collective-permute-start.3 = (f32[4,4,4,128]{3,2,1,0:T(4,128)S(1)}, f32[4,4,4,128]{3,2,1,0:T(4,128)S(1)}, u32[]{:S(2)}, u32[]{:S(2)}) collective-permute-start(f32[4,4,4,128]{3,2,1,0:T(4,128)S(1)} %bitcast.77), channel_id=1, source_target_pairs={{8,16},{16,8},{9,17},{17,9},{10,18},{18,10},{11,19},{19,11},{12,20... | collective-permute-start | bytes 98312 | tf_op jit(solution)/shard_map/ppermute | solution.py:783
  16.6 3.3 %collective-permute-start.4 = (f32[4,4,4,128]{3,2,1,0:T(4,128)S(1)}, f32[4,4,4,128]{3,2,1,0:T(4,128)S(1)}, u32[]{:S(2)}, u32[]{:S(2)}) collective-permute-start(f32[4,4,4,128]{3,2,1,0:T(4,128)S(1)} %bitcast.75), channel_id=1, source_target_pairs={{0,8},{8,0},{16,24},{24,16},{1,9},{9,1},{17,25},{25,17},{2,10},{10... | collective-permute-start | bytes 98312 | tf_op jit(solution)/shard_map/ppermute | solution.py:783
  29.5 2.7 %collective-permute-start.5 = (f32[64,128]{1,0:T(8,128)S(1)}, f32[64,128]{1,0:T(8,128)S(1)}, u32[]{:S(2)}, u32[]{:S(2)}) collective-permute-start(f32[64,128]{1,0:T(8,128)S(1)} %get-tuple-element.54), channel_id=1, source_target_pairs={{0,8},{8,0},{16,24},{24,16},{1,9},{9,1},{17,25},{25,17},{2,10},{10... | collective-permute-start | bytes 98312 | tf_op jit(solution)/shard_map/ppermute | solution.py:783
  29.6 5.2 %collective-permute-start.6 = (f32[64,128]{1,0:T(8,128)S(1)}, f32[64,128]{1,0:T(8,128)S(1)}, u32[]{:S(2)}, u32[]{:S(2)}) collective-permute-start(f32[64,128]{1,0:T(8,128)S(1)} %get-tuple-element.55), channel_id=1, source_target_pairs={{8,16},{16,8},{9,17},{17,9},{10,18},{18,10},{11,19},{19,11},{12,20... | collective-permute-start | bytes 98312 | tf_op jit(solution)/shard_map/ppermute | solution.py:783
  35.1 4.3 %collective-permute-start.7 = (f32[128,128]{1,0:T(8,128)S(1)}, f32[128,128]{1,0:T(8,128)S(1)}, u32[]{:S(2)}, u32[]{:S(2)}) collective-permute-start(f32[128,128]{1,0:T(8,128)S(1)} %get-tuple-element.57), channel_id=1, source_target_pairs={{0,2},{2,0},{4,6},{6,4},{1,3},{3,1},{5,7},{7,5},{8,10},{10,8},{12,... | collective-permute-start | bytes 196616 | tf_op jit(solution)/shard_map/ppermute | solution.py:783
  36.8 6.1 %collective-permute-start.8 = (f32[128,128]{1,0:T(8,128)S(1)}, f32[128,128]{1,0:T(8,128)S(1)}, u32[]{:S(2)}, u32[]{:S(2)}) collective-permute-start(f32[128,128]{1,0:T(8,128)S(1)} %get-tuple-element.58), channel_id=1, source_target_pairs={{2,4},{4,2},{3,5},{5,3},{10,12},{12,10},{11,13},{13,11},{18,20},{2... | collective-permute-start | bytes 196616 | tf_op jit(solution)/shard_map/ppermute | solution.py:783
  43.2 4.3 %collective-permute-start.9 = (f32[128,128]{1,0:T(8,128)S(1)}, f32[128,128]{1,0:T(8,128)S(1)}, u32[]{:S(2)}, u32[]{:S(2)}) collective-permute-start(f32[128,128]{1,0:T(8,128)S(1)} %get-tuple-element.60), channel_id=1, source_target_pairs={{0,1},{1,0},{2,3},{3,2},{4,5},{5,4},{6,7},{7,6},{8,9},{9,8},{10,11... | collective-permute-start | bytes 196616 | tf_op jit(solution)/shard_map/ppermute | solution.py:783

commit v9 on v8

--- a/solution.py
+++ b/solution.py
@@ -444,7 +444,7 @@
     grid_ref, side_ref, grains_ref, plane_ref, own_ref, own_sum_ref,
     lists_ref, excess_ref, feature_near_ref, moment_near_ref,
     rim0_ref, rim1_ref, out_ref,
-    all_ref, contact_ref, height_ref, feature_far_ref, moment_far_ref, sum_ref, even_ref, odd_ref,
+    all_ref, contact_ref, height_ref, wide_ref, feature_far_ref, moment_far_ref, sum_ref, even_ref, odd_ref,
 ):
     tri = running_sums()
     sides = beside_in_this_frame(side_ref)
@@ -600,9 +600,25 @@
         return carry
 
     lax.fori_loop(0, NB // 4, four_heights, 0)
-    wide = lax.dot_general(
-        height_ref[...], plane_ref[...], (((1,), (1,)), ((), ())), preferred_element_type=F32
-    )
+    wide_ref[...] = jnp.zeros(wide_ref.shape, F32)
+    for pair in range(BOXES_DOWNSLOPE // 2):
+        first, last = max(0, 8 * pair - 4), min(32, 8 * pair + 12)
+        begin, end = first // 16 * 16, -(-last // 16) * 16
+        spans = [(64 * side, 64) for side, at in ((0, 0), (1, BOXES_DOWNSLOPE // 2 - 1)) if pair == at]
+        spans += [(TILE + 32 * y + begin, end - begin) for y in range(8)]
+        spans.append((3 * TILE + 8 * first, 8 * (last - first)))
+        found = 0.0
+        for row in range(NB // BOXES_DOWNSLOPE):
+            lanes = slice(TILE * (BOXES_DOWNSLOPE * row + 2 * pair), TILE * (BOXES_DOWNSLOPE * row + 2 * pair + 2))
+            planes = jnp.concatenate([plane_ref[at : at + size, lanes] for at, size in spans], axis=0)
+            found = found + lax.dot_general(
+                planes, height_ref[:, lanes], (((1,), (1,)), ((), ())), preferred_element_type=F32
+            )
+        done = 0
+        for at, size in spans:
+            wide_ref[at : at + size, :] += found[done : done + size]
+            done += size
+    wide = wide_ref[...].T
     out_ref[...] = wide[:, TILE:]
     rim = wide[:, :TILE]
     rim = jnp.where(is_even("gx"), pltpu.roll(rim, 64, 1), rim)
@@ -628,6 +644,7 @@
             pltpu.VMEM((8 * 160, TILE), F32),
             pltpu.VMEM((6 * NB, TILE), F32),
             pltpu.VMEM((rows, NB * TILE), BF16),
+            pltpu.VMEM((3 * TILE + COLS, rows), F32),
             pltpu.VMEM((2 * 16 * PITCH_ROWS, TILE), F32),
             pltpu.VMEM((2 * 16 * PITCH_ROWS, TILE), F32),
             pltpu.VMEM((16 * PITCH_ROWS, TILE), F32),

time: 48.4 us -> 47.7 us (0.986)
  Pallas kernels: 19.9 us -> 19.2 us
    pallas_call x8, Pallas kernels: 19.9 us -> 19.2 us  [plain_call(): pl.pallas_call(kernel, out_shape=shapes, in_specs=[vmem] * len(args), out...]
  transfers between devices with their start and end apart: 10 -> 10, of which waited for: 6 -> 6; matrix products, arithmetic and copies ran while one was open for 1% -> 1% of each run, Pallas kernels for 16% -> 17%
where the time goes in v9:
time: 47.7 us; the launch traced here: 47.5 us
  Pallas kernels  19.2 us (40%)
  starting transfers between devices  14.8 us (31%)
  waiting for transfers between devices  11.7 us (25%)
  between operations  0.89 us (2%)
  local copies, waits for them, and re-layouts  0.51 us (1%)
    pallas_call x8, Pallas kernels, plain_call(): pl.pallas_call(kernel, out_shape=shapes, in_specs=[vmem] * len(args), out...  19.2 us
    ppermute x10, starting transfers between devices, swaps(): lax.ppermute(value, axis, links)  14.8 us
    ppermute x10, waiting for transfers between devices, swaps(): lax.ppermute(value, axis, links)  11.7 us
  transfers between devices with their start and end apart: 10, of which 6 were waited for; matrix products, arithmetic and copies ran while one was open for 1% of the time, Pallas kernels for 17%

profile of v9, /device:TPU:10, one launch (start us, length us, event | category | flops | bytes accessed | tf_op | source)
XLA Modules:
  0.0 47.5 jit_solution(10717282674007425543)
XLA Ops:
  0.6 1.3 %box_sort.1 = (f32[7,32,128]{2,1,0:T(8,128)S(1)}, f32[4,32,128]{2,1,0:T(8,128)S(1)}) custom-call(f32[7,32,128]{2,1,0:T(8,128)} %bitcast.68, s32[27,1,32]{2,1,0:T(1,128)} %bitcast.78), custom_call_target="tpu_custom_call" | custom-call | tf_op jit(solution)/shard_map/box_sort/pallas_call | solution.py:758
  2.0 1.6 %collective-permute-start = (f32[4,2,8,128]{3,0,2,1:T(4,128)S(1)}, f32[4,2,8,128]{3,0,2,1:T(4,128)S(1)}, u32[]{:S(2)}, u32[]{:S(2)}) collective-permute-start(f32[4,2,8,128]{3,0,2,1:T(4,128)S(1)} %bitcast.73), channel_id=1, source_target_pairs={{0,1},{1,0},{2,3},{3,2},{4,5},{5,4},{6,7},{7,6},{8,9},{9,8},{10,11... | collective-permute-start | bytes 98312 | tf_op jit(solution)/shard_map/ppermute | solution.py:800
  3.6 2.9 %own.1 = (f32[1520,128]{1,0:T(8,128)S(1)}, f32[640,128]{1,0:T(8,128)S(1)}) custom-call(f32[7,32,128]{2,1,0:T(8,128)S(1)} %get-tuple-element.41.grains_ref.own_ref), custom_call_target="tpu_custom_call" | custom-call | tf_op jit(solution)/shard_map/own/pallas_call | solution.py:758
  6.5 0.0 collective-permute-done
  6.5 0.1 pad_maximum_fusion.1
  6.6 3.5 %collective-permute-start.1 = (f32[4,4,8,128]{3,1,0,2:T(4,128)S(1)}, f32[4,4,8,128]{3,1,0,2:T(4,128)S(1)}, u32[]{:S(2)}, u32[]{:S(2)}) collective-permute-start(f32[4,4,8,128]{3,1,0,2:T(4,128)S(1)} %bitcast.72), channel_id=1, source_target_pairs={{2,4},{4,2},{3,5},{5,3},{10,12},{12,10},{11,13},{13,11},{18,20},{2... | collective-permute-start | bytes 196616 | tf_op jit(solution)/shard_map/ppermute | solution.py:800
  10.1 0.1 collective-permute-start.2
  10.2 0.1 copy.11
  10.3 3.6 %plane.1.plane_ref = bf16[640,4096]{1,0:T(8,128)(2,1)S(1)} custom-call(f32[7,32,128]{2,1,0:T(8,128)S(1)} %get-tuple-element.41.grains_ref.own_ref), custom_call_target="tpu_custom_call" | custom-call | tf_op jit(solution)/shard_map/plane/pallas_call | solution.py:758
  14.0 0.5 collective-permute-done.2
  14.5 0.2 pad_maximum_fusion
  14.7 1.9 %collective-permute-start.3 = (f32[4,4,4,128]{3,2,1,0:T(4,128)S(1)}, f32[4,4,4,128]{3,2,1,0:T(4,128)S(1)}, u32[]{:S(2)}, u32[]{:S(2)}) collective-permute-start(f32[4,4,4,128]{3,2,1,0:T(4,128)S(1)} %bitcast.77), channel_id=1, source_target_pairs={{8,16},{16,8},{9,17},{17,9},{10,18},{18,10},{11,19},{19,11},{12,20... | collective-permute-start | bytes 98312 | tf_op jit(solution)/shard_map/ppermute | solution.py:800
  16.6 0.1 collective-permute-start.4
  16.7 0.2 copy.12
  16.9 0.2 copy.13
  17.0 1.3 %near.1 = (f32[8,32,128]{2,1,0:T(8,128)S(1)}, f32[1,128]{1,0:T(1,128)S(1)}, f32[1280,128]{1,0:T(8,128)S(1)}, f32[1280,128]{1,0:T(8,128)S(1)}) custom-call(f32[4,128,128]{2,1,0:T(8,128)S(1)} %bitcast.52), custom_call_target="tpu_custom_call" | custom-call | tf_op jit(solution)/shard_map/near/pallas_call | solution.py:758
  18.4 1.6 %collective-permute-done.3 = f32[4,4,4,128]{3,2,1,0:T(4,128)S(1)} collective-permute-done((f32[4,4,4,128]{3,2,1,0:T(4,128)S(1)}, f32[4,4,4,128]{3,2,1,0:T(4,128)S(1)}, u32[]{:S(2)}, u32[]{:S(2)}) %collective-permute-start.3) | collective-permute-done | bytes 32800 | tf_op jit(solution)/shard_map/ppermute | solution.py:800
  19.9 0.0 collective-permute-done.4
  20.0 8.9 %stress_deposit.1 = (f32[64,128]{1,0:T(8,128)S(1)}, f32[64,128]{1,0:T(8,128)S(1)}, f32[128,512]{1,0:T(8,128)S(1)}) custom-call(f32[4,128,128]{2,1,0:T(8,128)S(1)} %bitcast.51, f32[2,4,16,128]{3,2,1,0:T(8,128)S(1)} %pad_maximum_fusion.2.side_ref, f32[224,128]{1,0:T(8,128)S(1)} %bitcast.53, bf16[640,4096]{1,0:T(8,128)(2,1)S(1)} %plane.1.plane_ref, ...), custom_call_target="tpu_custom_call" | custom-call | tf_op jit(solution)/shard_map/stress_deposit/pallas_call | solution.py:758
  28.9 0.1 collective-permute-start.5
  28.9 2.6 %collective-permute-start.6 = (f32[64,128]{1,0:T(8,128)S(1)}, f32[64,128]{1,0:T(8,128)S(1)}, u32[]{:S(2)}, u32[]{:S(2)}) collective-permute-start(f32[64,128]{1,0:T(8,128)S(1)} %get-tuple-element.55), channel_id=1, source_target_pairs={{8,16},{16,8},{9,17},{17,9},{10,18},{18,10},{11,19},{19,11},{12,20... | collective-permute-start | bytes 98312 | tf_op jit(solution)/shard_map/ppermute | solution.py:800
  31.5 0.0 collective-permute-done.5.first_ref
  31.5 2.6 %collective-permute-done.6.second_ref = f32[64,128]{1,0:T(8,128)S(1)} collective-permute-done((f32[64,128]{1,0:T(8,128)S(1)}, f32[64,128]{1,0:T(8,128)S(1)}, u32[]{:S(2)}, u32[]{:S(2)}) %collective-permute-start.6) | collective-permute-done | bytes 32800 | tf_op jit(solution)/shard_map/ppermute | solution.py:800
  34.2 0.3 rim_x.1
  34.5 1.6 %collective-permute-start.7 = (f32[128,128]{1,0:T(8,128)S(1)}, f32[128,128]{1,0:T(8,128)S(1)}, u32[]{:S(2)}, u32[]{:S(2)}) collective-permute-start(f32[128,128]{1,0:T(8,128)S(1)} %get-tuple-element.57), channel_id=1, source_target_pairs={{0,2},{2,0},{4,6},{6,4},{1,3},{3,1},{5,7},{7,5},{8,10},{10,8},{12,... | collective-permute-start | bytes 196616 | tf_op jit(solution)/shard_map/ppermute | solution.py:800
  36.1 2.3 %collective-permute-start.8 = (f32[128,128]{1,0:T(8,128)S(1)}, f32[128,128]{1,0:T(8,128)S(1)}, u32[]{:S(2)}, u32[]{:S(2)}) collective-permute-start(f32[128,128]{1,0:T(8,128)S(1)} %get-tuple-element.58), channel_id=1, source_target_pairs={{2,4},{4,2},{3,5},{5,3},{10,12},{12,10},{11,13},{13,11},{18,20},{2... | collective-permute-start | bytes 196616 | tf_op jit(solution)/shard_map/ppermute | solution.py:800
  38.5 0.4 collective-permute-done.7.first_ref
  38.8 3.4 %collective-permute-done.8.second_ref = f32[128,128]{1,0:T(8,128)S(1)} collective-permute-done((f32[128,128]{1,0:T(8,128)S(1)}, f32[128,128]{1,0:T(8,128)S(1)}, u32[]{:S(2)}, u32[]{:S(2)}) %collective-permute-start.8) | collective-permute-done | bytes 65568 | tf_op jit(solution)/shard_map/ppermute | solution.py:800
  42.3 0.2 rim_y.1
  42.5 1.1 %collective-permute-start.9 = (f32[128,128]{1,0:T(8,128)S(1)}, f32[128,128]{1,0:T(8,128)S(1)}, u32[]{:S(2)}, u32[]{:S(2)}) collective-permute-start(f32[128,128]{1,0:T(8,128)S(1)} %get-tuple-element.60), channel_id=1, source_target_pairs={{0,1},{1,0},{2,3},{3,2},{4,5},{5,4},{6,7},{7,6},{8,9},{9,8},{10,11... | collective-permute-start | bytes 196616 | tf_op jit(solution)/shard_map/ppermute | solution.py:800
  43.6 3.3 %collective-permute-done.9.got_ref = f32[128,128]{1,0:T(8,128)S(1)} collective-permute-done((f32[128,128]{1,0:T(8,128)S(1)}, f32[128,128]{1,0:T(8,128)S(1)}, u32[]{:S(2)}, u32[]{:S(2)}) %collective-permute-start.9) | collective-permute-done | bytes 65568 | tf_op jit(solution)/shard_map/ppermute | solution.py:800
  46.9 0.7 %finish.1 = (f32[1,1,1,10,8,256]{5,4,3,2,1,0:T(8,128)}, f32[1,1,2,128]{3,2,1,0:T(2,128)}, f32[1,1,16,128]{3,2,1,0:T(8,128)}) custom-call(f32[128,256]{1,0:T(8,128)S(1)} %get-tuple-element.59.total_ref, f32[128,128]{1,0:T(8,128)S(1)} %collective-permute-done.9.got_ref), custom_call_target="tpu_custom_call" | custom-call | tf_op jit(solution)/shard_map/finish/pallas_call | solution.py:758
  (13 shorter events, 0.2 us)
Async XLA Ops:
  2.0 4.5 %collective-permute-start = (f32[4,2,8,128]{3,0,2,1:T(4,128)S(1)}, f32[4,2,8,128]{3,0,2,1:T(4,128)S(1)}, u32[]{:S(2)}, u32[]{:S(2)}) collective-permute-start(f32[4,2,8,128]{3,0,2,1:T(4,128)S(1)} %bitcast.73), channel_id=1, source_target_pairs={{0,1},{1,0},{2,3},{3,2},{4,5},{5,4},{6,7},{7,6},{8,9},{9,8},{10,11... | collective-permute-start | bytes 98312 | tf_op jit(solution)/shard_map/ppermute | solution.py:800
  6.6 7.4 %collective-permute-start.1 = (f32[4,4,8,128]{3,1,0,2:T(4,128)S(1)}, f32[4,4,8,128]{3,1,0,2:T(4,128)S(1)}, u32[]{:S(2)}, u32[]{:S(2)}) collective-permute-start(f32[4,4,8,128]{3,1,0,2:T(4,128)S(1)} %bitcast.72), channel_id=1, source_target_pairs={{2,4},{4,2},{3,5},{5,3},{10,12},{12,10},{11,13},{13,11},{18,20},{2... | collective-permute-start | bytes 196616 | tf_op jit(solution)/shard_map/ppermute | solution.py:800
  10.1 4.3 %collective-permute-start.2 = (f32[4,4,8,128]{3,1,0,2:T(4,128)S(1)}, f32[4,4,8,128]{3,1,0,2:T(4,128)S(1)}, u32[]{:S(2)}, u32[]{:S(2)}) collective-permute-start(f32[4,4,8,128]{3,1,0,2:T(4,128)S(1)} %bitcast.70), channel_id=1, source_target_pairs={{0,2},{2,0},{4,6},{6,4},{1,3},{3,1},{5,7},{7,5},{8,10},{10,8},{12,... | collective-permute-start | bytes 196616 | tf_op jit(solution)/shard_map/ppermute | solution.py:800
  14.7 5.2 %collective-permute-start.3 = (f32[4,4,4,128]{3,2,1,0:T(4,128)S(1)}, f32[4,4,4,128]{3,2,1,0:T(4,128)S(1)}, u32[]{:S(2)}, u32[]{:S(2)}) collective-permute-start(f32[4,4,4,128]{3,2,1,0:T(4,128)S(1)} %bitcast.77), channel_id=1, source_target_pairs={{8,16},{16,8},{9,17},{17,9},{10,18},{18,10},{11,19},{19,11},{12,20... | collective-permute-start | bytes 98312 | tf_op jit(solution)/shard_map/ppermute | solution.py:800
  16.6 3.3 %collective-permute-start.4 = (f32[4,4,4,128]{3,2,1,0:T(4,128)S(1)}, f32[4,4,4,128]{3,2,1,0:T(4,128)S(1)}, u32[]{:S(2)}, u32[]{:S(2)}) collective-permute-start(f32[4,4,4,128]{3,2,1,0:T(4,128)S(1)} %bitcast.75), channel_id=1, source_target_pairs={{0,8},{8,0},{16,24},{24,16},{1,9},{9,1},{17,25},{25,17},{2,10},{10... | collective-permute-start | bytes 98312 | tf_op jit(solution)/shard_map/ppermute | solution.py:800
  28.9 2.7 %collective-permute-start.5 = (f32[64,128]{1,0:T(8,128)S(1)}, f32[64,128]{1,0:T(8,128)S(1)}, u32[]{:S(2)}, u32[]{:S(2)}) collective-permute-start(f32[64,128]{1,0:T(8,128)S(1)} %get-tuple-element.54), channel_id=1, source_target_pairs={{0,8},{8,0},{16,24},{24,16},{1,9},{9,1},{17,25},{25,17},{2,10},{10... | collective-permute-start | bytes 98312 | tf_op jit(solution)/shard_map/ppermute | solution.py:800
  28.9 5.2 %collective-permute-start.6 = (f32[64,128]{1,0:T(8,128)S(1)}, f32[64,128]{1,0:T(8,128)S(1)}, u32[]{:S(2)}, u32[]{:S(2)}) collective-permute-start(f32[64,128]{1,0:T(8,128)S(1)} %get-tuple-element.55), channel_id=1, source_target_pairs={{8,16},{16,8},{9,17},{17,9},{10,18},{18,10},{11,19},{19,11},{12,20... | collective-permute-start | bytes 98312 | tf_op jit(solution)/shard_map/ppermute | solution.py:800
  34.5 4.3 %collective-permute-start.7 = (f32[128,128]{1,0:T(8,128)S(1)}, f32[128,128]{1,0:T(8,128)S(1)}, u32[]{:S(2)}, u32[]{:S(2)}) collective-permute-start(f32[128,128]{1,0:T(8,128)S(1)} %get-tuple-element.57), channel_id=1, source_target_pairs={{0,2},{2,0},{4,6},{6,4},{1,3},{3,1},{5,7},{7,5},{8,10},{10,8},{12,... | collective-permute-start | bytes 196616 | tf_op jit(solution)/shard_map/ppermute | solution.py:800
  36.1 6.1 %collective-permute-start.8 = (f32[128,128]{1,0:T(8,128)S(1)}, f32[128,128]{1,0:T(8,128)S(1)}, u32[]{:S(2)}, u32[]{:S(2)}) collective-permute-start(f32[128,128]{1,0:T(8,128)S(1)} %get-tuple-element.58), channel_id=1, source_target_pairs={{2,4},{4,2},{3,5},{5,3},{10,12},{12,10},{11,13},{13,11},{18,20},{2... | collective-permute-start | bytes 196616 | tf_op jit(solution)/shard_map/ppermute | solution.py:800
  42.5 4.3 %collective-permute-start.9 = (f32[128,128]{1,0:T(8,128)S(1)}, f32[128,128]{1,0:T(8,128)S(1)}, u32[]{:S(2)}, u32[]{:S(2)}) collective-permute-start(f32[128,128]{1,0:T(8,128)S(1)} %get-tuple-element.60), channel_id=1, source_target_pairs={{0,1},{1,0},{2,3},{3,2},{4,5},{5,4},{6,7},{7,6},{8,9},{9,8},{10,11... | collective-permute-start | bytes 196616 | tf_op jit(solution)/shard_map/ppermute | solution.py:800

commit v10 on v9

--- a/solution.py
+++ b/solution.py
@@ -594,12 +594,12 @@
 
         lax.fori_loop(0, NB, one_tile, 0)
 
-    def four_heights(q, carry):
-        for i in range(4):
-            put_height(4 * q + i)
+    def eight_heights(q, carry):
+        for i in range(8):
+            put_height(8 * q + i)
         return carry
 
-    lax.fori_loop(0, NB // 4, four_heights, 0)
+    lax.fori_loop(0, NB // 8, eight_heights, 0)
     wide_ref[...] = jnp.zeros(wide_ref.shape, F32)
     for pair in range(BOXES_DOWNSLOPE // 2):
         first, last = max(0, 8 * pair - 4), min(32, 8 * pair + 12)

time: 47.7 us -> 47.7 us (level)
  no operation moved by 1% of the time
where the time goes in v10:
time: 47.7 us; the launch traced here: 47.4 us
  Pallas kernels  19.2 us (40%)
  starting transfers between devices  14.8 us (31%)
  waiting for transfers between devices  11.7 us (25%)
  between operations  0.89 us (2%)
  local copies, waits for them, and re-layouts  0.51 us (1%)
    pallas_call x8, Pallas kernels, plain_call(): pl.pallas_call(kernel, out_shape=shapes, in_specs=[vmem] * len(args), out...  19.2 us
    ppermute x10, starting transfers between devices, swaps(): lax.ppermute(value, axis, links)  14.8 us
    ppermute x10, waiting for transfers between devices, swaps(): lax.ppermute(value, axis, links)  11.7 us
  transfers between devices with their start and end apart: 10, of which 6 were waited for; matrix products, arithmetic and copies ran while one was open for 1% of the time, Pallas kernels for 17%

profile of v10, /device:TPU:10, one launch (start us, length us, event | category | flops | bytes accessed | tf_op | source)
XLA Modules:
  0.0 47.4 jit_solution(545966974694081973)
XLA Ops:
  0.6 1.3 %box_sort.1 = (f32[7,32,128]{2,1,0:T(8,128)S(1)}, f32[4,32,128]{2,1,0:T(8,128)S(1)}) custom-call(f32[7,32,128]{2,1,0:T(8,128)} %bitcast.68, s32[27,1,32]{2,1,0:T(1,128)} %bitcast.78), custom_call_target="tpu_custom_call" | custom-call | tf_op jit(solution)/shard_map/box_sort/pallas_call | solution.py:758
  2.0 1.6 %collective-permute-start = (f32[4,2,8,128]{3,0,2,1:T(4,128)S(1)}, f32[4,2,8,128]{3,0,2,1:T(4,128)S(1)}, u32[]{:S(2)}, u32[]{:S(2)}) collective-permute-start(f32[4,2,8,128]{3,0,2,1:T(4,128)S(1)} %bitcast.73), channel_id=1, source_target_pairs={{0,1},{1,0},{2,3},{3,2},{4,5},{5,4},{6,7},{7,6},{8,9},{9,8},{10,11... | collective-permute-start | bytes 98312 | tf_op jit(solution)/shard_map/ppermute | solution.py:800
  3.6 2.9 %own.1 = (f32[1520,128]{1,0:T(8,128)S(1)}, f32[640,128]{1,0:T(8,128)S(1)}) custom-call(f32[7,32,128]{2,1,0:T(8,128)S(1)} %get-tuple-element.41.grains_ref.own_ref), custom_call_target="tpu_custom_call" | custom-call | tf_op jit(solution)/shard_map/own/pallas_call | solution.py:758
  6.5 0.0 collective-permute-done
  6.5 0.1 pad_maximum_fusion.1
  6.6 3.5 %collective-permute-start.1 = (f32[4,4,8,128]{3,1,0,2:T(4,128)S(1)}, f32[4,4,8,128]{3,1,0,2:T(4,128)S(1)}, u32[]{:S(2)}, u32[]{:S(2)}) collective-permute-start(f32[4,4,8,128]{3,1,0,2:T(4,128)S(1)} %bitcast.72), channel_id=1, source_target_pairs={{2,4},{4,2},{3,5},{5,3},{10,12},{12,10},{11,13},{13,11},{18,20},{2... | collective-permute-start | bytes 196616 | tf_op jit(solution)/shard_map/ppermute | solution.py:800
  10.1 0.1 collective-permute-start.2
  10.2 0.1 copy.11
  10.3 3.6 %plane.1.plane_ref = bf16[640,4096]{1,0:T(8,128)(2,1)S(1)} custom-call(f32[7,32,128]{2,1,0:T(8,128)S(1)} %get-tuple-element.41.grains_ref.own_ref), custom_call_target="tpu_custom_call" | custom-call | tf_op jit(solution)/shard_map/plane/pallas_call | solution.py:758
  14.0 0.5 collective-permute-done.2
  14.5 0.2 pad_maximum_fusion
  14.7 1.9 %collective-permute-start.3 = (f32[4,4,4,128]{3,2,1,0:T(4,128)S(1)}, f32[4,4,4,128]{3,2,1,0:T(4,128)S(1)}, u32[]{:S(2)}, u32[]{:S(2)}) collective-permute-start(f32[4,4,4,128]{3,2,1,0:T(4,128)S(1)} %bitcast.77), channel_id=1, source_target_pairs={{8,16},{16,8},{9,17},{17,9},{10,18},{18,10},{11,19},{19,11},{12,20... | collective-permute-start | bytes 98312 | tf_op jit(solution)/shard_map/ppermute | solution.py:800
  16.6 0.1 collective-permute-start.4
  16.7 0.2 copy.12
  16.9 0.2 copy.13
  17.0 1.3 %near.1 = (f32[8,32,128]{2,1,0:T(8,128)S(1)}, f32[1,128]{1,0:T(1,128)S(1)}, f32[1280,128]{1,0:T(8,128)S(1)}, f32[1280,128]{1,0:T(8,128)S(1)}) custom-call(f32[4,128,128]{2,1,0:T(8,128)S(1)} %bitcast.52), custom_call_target="tpu_custom_call" | custom-call | tf_op jit(solution)/shard_map/near/pallas_call | solution.py:758
  18.4 1.6 %collective-permute-done.3 = f32[4,4,4,128]{3,2,1,0:T(4,128)S(1)} collective-permute-done((f32[4,4,4,128]{3,2,1,0:T(4,128)S(1)}, f32[4,4,4,128]{3,2,1,0:T(4,128)S(1)}, u32[]{:S(2)}, u32[]{:S(2)}) %collective-permute-start.3) | collective-permute-done | bytes 32800 | tf_op jit(solution)/shard_map/ppermute | solution.py:800
  19.9 0.0 collective-permute-done.4
  20.0 8.8 %stress_deposit.1 = (f32[64,128]{1,0:T(8,128)S(1)}, f32[64,128]{1,0:T(8,128)S(1)}, f32[128,512]{1,0:T(8,128)S(1)}) custom-call(f32[4,128,128]{2,1,0:T(8,128)S(1)} %bitcast.51, f32[2,4,16,128]{3,2,1,0:T(8,128)S(1)} %pad_maximum_fusion.2.side_ref, f32[224,128]{1,0:T(8,128)S(1)} %bitcast.53, bf16[640,4096]{1,0:T(8,128)(2,1)S(1)} %plane.1.plane_ref, ...), custom_call_target="tpu_custom_call" | custom-call | tf_op jit(solution)/shard_map/stress_deposit/pallas_call | solution.py:758
  28.8 0.1 collective-permute-start.5
  28.9 2.6 %collective-permute-start.6 = (f32[64,128]{1,0:T(8,128)S(1)}, f32[64,128]{1,0:T(8,128)S(1)}, u32[]{:S(2)}, u32[]{:S(2)}) collective-permute-start(f32[64,128]{1,0:T(8,128)S(1)} %get-tuple-element.55), channel_id=1, source_target_pairs={{8,16},{16,8},{9,17},{17,9},{10,18},{18,10},{11,19},{19,11},{12,20... | collective-permute-start | bytes 98312 | tf_op jit(solution)/shard_map/ppermute | solution.py:800
  31.4 0.0 collective-permute-done.5.first_ref
  31.5 2.6 %collective-permute-done.6.second_ref = f32[64,128]{1,0:T(8,128)S(1)} collective-permute-done((f32[64,128]{1,0:T(8,128)S(1)}, f32[64,128]{1,0:T(8,128)S(1)}, u32[]{:S(2)}, u32[]{:S(2)}) %collective-permute-start.6) | collective-permute-done | bytes 32800 | tf_op jit(solution)/shard_map/ppermute | solution.py:800
  34.1 0.3 rim_x.1
  34.4 1.6 %collective-permute-start.7 = (f32[128,128]{1,0:T(8,128)S(1)}, f32[128,128]{1,0:T(8,128)S(1)}, u32[]{:S(2)}, u32[]{:S(2)}) collective-permute-start(f32[128,128]{1,0:T(8,128)S(1)} %get-tuple-element.57), channel_id=1, source_target_pairs={{0,2},{2,0},{4,6},{6,4},{1,3},{3,1},{5,7},{7,5},{8,10},{10,8},{12,... | collective-permute-start | bytes 196616 | tf_op jit(solution)/shard_map/ppermute | solution.py:800
  36.1 2.3 %collective-permute-start.8 = (f32[128,128]{1,0:T(8,128)S(1)}, f32[128,128]{1,0:T(8,128)S(1)}, u32[]{:S(2)}, u32[]{:S(2)}) collective-permute-start(f32[128,128]{1,0:T(8,128)S(1)} %get-tuple-element.58), channel_id=1, source_target_pairs={{2,4},{4,2},{3,5},{5,3},{10,12},{12,10},{11,13},{13,11},{18,20},{2... | collective-permute-start | bytes 196616 | tf_op jit(solution)/shard_map/ppermute | solution.py:800
  38.4 0.4 collective-permute-done.7.first_ref
  38.8 3.4 %collective-permute-done.8.second_ref = f32[128,128]{1,0:T(8,128)S(1)} collective-permute-done((f32[128,128]{1,0:T(8,128)S(1)}, f32[128,128]{1,0:T(8,128)S(1)}, u32[]{:S(2)}, u32[]{:S(2)}) %collective-permute-start.8) | collective-permute-done | bytes 65568 | tf_op jit(solution)/shard_map/ppermute | solution.py:800
  42.2 0.2 rim_y.1
  42.5 1.1 %collective-permute-start.9 = (f32[128,128]{1,0:T(8,128)S(1)}, f32[128,128]{1,0:T(8,128)S(1)}, u32[]{:S(2)}, u32[]{:S(2)}) collective-permute-start(f32[128,128]{1,0:T(8,128)S(1)} %get-tuple-element.60), channel_id=1, source_target_pairs={{0,1},{1,0},{2,3},{3,2},{4,5},{5,4},{6,7},{7,6},{8,9},{9,8},{10,11... | collective-permute-start | bytes 196616 | tf_op jit(solution)/shard_map/ppermute | solution.py:800
  43.5 3.3 %collective-permute-done.9.got_ref = f32[128,128]{1,0:T(8,128)S(1)} collective-permute-done((f32[128,128]{1,0:T(8,128)S(1)}, f32[128,128]{1,0:T(8,128)S(1)}, u32[]{:S(2)}, u32[]{:S(2)}) %collective-permute-start.9) | collective-permute-done | bytes 65568 | tf_op jit(solution)/shard_map/ppermute | solution.py:800
  46.8 0.7 %finish.1 = (f32[1,1,1,10,8,256]{5,4,3,2,1,0:T(8,128)}, f32[1,1,2,128]{3,2,1,0:T(2,128)}, f32[1,1,16,128]{3,2,1,0:T(8,128)}) custom-call(f32[128,256]{1,0:T(8,128)S(1)} %get-tuple-element.59.total_ref, f32[128,128]{1,0:T(8,128)S(1)} %collective-permute-done.9.got_ref), custom_call_target="tpu_custom_call" | custom-call | tf_op jit(solution)/shard_map/finish/pallas_call | solution.py:758
  (13 shorter events, 0.2 us)
Async XLA Ops:
  2.0 4.5 %collective-permute-start = (f32[4,2,8,128]{3,0,2,1:T(4,128)S(1)}, f32[4,2,8,128]{3,0,2,1:T(4,128)S(1)}, u32[]{:S(2)}, u32[]{:S(2)}) collective-permute-start(f32[4,2,8,128]{3,0,2,1:T(4,128)S(1)} %bitcast.73), channel_id=1, source_target_pairs={{0,1},{1,0},{2,3},{3,2},{4,5},{5,4},{6,7},{7,6},{8,9},{9,8},{10,11... | collective-permute-start | bytes 98312 | tf_op jit(solution)/shard_map/ppermute | solution.py:800
  6.6 7.4 %collective-permute-start.1 = (f32[4,4,8,128]{3,1,0,2:T(4,128)S(1)}, f32[4,4,8,128]{3,1,0,2:T(4,128)S(1)}, u32[]{:S(2)}, u32[]{:S(2)}) collective-permute-start(f32[4,4,8,128]{3,1,0,2:T(4,128)S(1)} %bitcast.72), channel_id=1, source_target_pairs={{2,4},{4,2},{3,5},{5,3},{10,12},{12,10},{11,13},{13,11},{18,20},{2... | collective-permute-start | bytes 196616 | tf_op jit(solution)/shard_map/ppermute | solution.py:800
  10.1 4.3 %collective-permute-start.2 = (f32[4,4,8,128]{3,1,0,2:T(4,128)S(1)}, f32[4,4,8,128]{3,1,0,2:T(4,128)S(1)}, u32[]{:S(2)}, u32[]{:S(2)}) collective-permute-start(f32[4,4,8,128]{3,1,0,2:T(4,128)S(1)} %bitcast.70), channel_id=1, source_target_pairs={{0,2},{2,0},{4,6},{6,4},{1,3},{3,1},{5,7},{7,5},{8,10},{10,8},{12,... | collective-permute-start | bytes 196616 | tf_op jit(solution)/shard_map/ppermute | solution.py:800
  14.7 5.2 %collective-permute-start.3 = (f32[4,4,4,128]{3,2,1,0:T(4,128)S(1)}, f32[4,4,4,128]{3,2,1,0:T(4,128)S(1)}, u32[]{:S(2)}, u32[]{:S(2)}) collective-permute-start(f32[4,4,4,128]{3,2,1,0:T(4,128)S(1)} %bitcast.77), channel_id=1, source_target_pairs={{8,16},{16,8},{9,17},{17,9},{10,18},{18,10},{11,19},{19,11},{12,20... | collective-permute-start | bytes 98312 | tf_op jit(solution)/shard_map/ppermute | solution.py:800
  16.6 3.3 %collective-permute-start.4 = (f32[4,4,4,128]{3,2,1,0:T(4,128)S(1)}, f32[4,4,4,128]{3,2,1,0:T(4,128)S(1)}, u32[]{:S(2)}, u32[]{:S(2)}) collective-permute-start(f32[4,4,4,128]{3,2,1,0:T(4,128)S(1)} %bitcast.75), channel_id=1, source_target_pairs={{0,8},{8,0},{16,24},{24,16},{1,9},{9,1},{17,25},{25,17},{2,10},{10... | collective-permute-start | bytes 98312 | tf_op jit(solution)/shard_map/ppermute | solution.py:800
  28.8 2.7 %collective-permute-start.5 = (f32[64,128]{1,0:T(8,128)S(1)}, f32[64,128]{1,0:T(8,128)S(1)}, u32[]{:S(2)}, u32[]{:S(2)}) collective-permute-start(f32[64,128]{1,0:T(8,128)S(1)} %get-tuple-element.54), channel_id=1, source_target_pairs={{0,8},{8,0},{16,24},{24,16},{1,9},{9,1},{17,25},{25,17},{2,10},{10... | collective-permute-start | bytes 98312 | tf_op jit(solution)/shard_map/ppermute | solution.py:800
  28.9 5.2 %collective-permute-start.6 = (f32[64,128]{1,0:T(8,128)S(1)}, f32[64,128]{1,0:T(8,128)S(1)}, u32[]{:S(2)}, u32[]{:S(2)}) collective-permute-start(f32[64,128]{1,0:T(8,128)S(1)} %get-tuple-element.55), channel_id=1, source_target_pairs={{8,16},{16,8},{9,17},{17,9},{10,18},{18,10},{11,19},{19,11},{12,20... | collective-permute-start | bytes 98312 | tf_op jit(solution)/shard_map/ppermute | solution.py:800
  34.4 4.3 %collective-permute-start.7 = (f32[128,128]{1,0:T(8,128)S(1)}, f32[128,128]{1,0:T(8,128)S(1)}, u32[]{:S(2)}, u32[]{:S(2)}) collective-permute-start(f32[128,128]{1,0:T(8,128)S(1)} %get-tuple-element.57), channel_id=1, source_target_pairs={{0,2},{2,0},{4,6},{6,4},{1,3},{3,1},{5,7},{7,5},{8,10},{10,8},{12,... | collective-permute-start | bytes 196616 | tf_op jit(solution)/shard_map/ppermute | solution.py:800
  36.1 6.1 %collective-permute-start.8 = (f32[128,128]{1,0:T(8,128)S(1)}, f32[128,128]{1,0:T(8,128)S(1)}, u32[]{:S(2)}, u32[]{:S(2)}) collective-permute-start(f32[128,128]{1,0:T(8,128)S(1)} %get-tuple-element.58), channel_id=1, source_target_pairs={{2,4},{4,2},{3,5},{5,3},{10,12},{12,10},{11,13},{13,11},{18,20},{2... | collective-permute-start | bytes 196616 | tf_op jit(solution)/shard_map/ppermute | solution.py:800
  42.5 4.3 %collective-permute-start.9 = (f32[128,128]{1,0:T(8,128)S(1)}, f32[128,128]{1,0:T(8,128)S(1)}, u32[]{:S(2)}, u32[]{:S(2)}) collective-permute-start(f32[128,128]{1,0:T(8,128)S(1)} %get-tuple-element.60), channel_id=1, source_target_pairs={{0,1},{1,0},{2,3},{3,2},{4,5},{5,4},{6,7},{7,6},{8,9},{9,8},{10,11... | collective-permute-start | bytes 196616 | tf_op jit(solution)/shard_map/ppermute | solution.py:800
